TPU v7x, 256 devices: a whole 4x4x8 slice. The times are simulated.
256 devices in a mesh: pipe: 4 (over z_hi, core), expert: 64 (over x, z_lo, y).
Axes of the slice: x: 4, y: 4, z: 8 (z_hi: 2, z_lo: 4; z = z_hi * 4 + z_lo), core: 2. Of those that a mesh axis runs over, the one named last changes fastest.
Arguments:
- tokens: bfloat16 [4, 8192, 3584], P('pipe', 'expert'), may hold values from -6 to 6
- expert_ids: int32 [4, 8192, 4], P('pipe', 'expert'), may hold values from 0 to 63, all different within a row; in each aligned block of 128 rows (0 to 127, 128 to 255, ..., all dimensions but the last counted through in order) at most 14 rows name the same one
- up_weight: bfloat16 [4, 64, 3584, 512], P('pipe', 'expert'), may hold values from -0.1875 to 0.1875
- up_grad: bfloat16 [4, 64, 64, 14, 1024], P('pipe', 'expert'), may hold values from -1.1953125 to 1.1953125
Outputs:
- token_grad: bfloat16 [4, 8192, 3584], P('pipe', 'expert')
- weight_grad: bfloat16 [4, 64, 3584, 512], P('pipe', 'expert')
Inputs may be any that keep to these rules, and one draw needn't show every extreme that they name: `expert_ids`: A token's 4 experts are distinct. Among the 128 tokens of one device no expert is named by more than 14 tokens, and on some device one expert is named by exactly 14.
All inputs are finite; a program needn't handle non-finite values.
Results may differ from a plain program's by a relative error of at most 0.0051.
Values may be sent and summed in bfloat16 or wider, within the bound.
No kernel may reach another device: no remote copies, remote signals or barrier semaphores. Data moves between devices by JAX's collectives and lax.ppermute only.
A program may use at most 128 MiB of HBM per device.

v0:
```python
import jax
import jax.numpy as jnp
from jax import lax
from jax.sharding import PartitionSpec as P


def from_partner(value, axis, stride):
    mask = 2**stride
    pairs = [(source, source ^ mask) for source in range(lax.axis_size(axis))]
    return lax.ppermute(value, axis, pairs)


def on_device(tokens, expert_ids, up_weight, up_grad):
    section_count = lax.axis_size("pipe")
    section_bits = section_count.bit_length() - 1
    token_rows = tokens[0]
    token_ids = expert_ids[0]
    owner_count = up_grad.shape[2]
    capacity = up_grad.shape[3]
    expert_lane = jnp.arange(owner_count, dtype=jnp.int32)
    named_count = jnp.sum(
        (token_ids[:, :, None] == expert_lane[None, None, :]).astype(jnp.int32), axis=1
    )
    slot_before = jnp.cumsum(named_count, axis=0) - named_count
    slot_index = jnp.arange(capacity, dtype=jnp.int32)
    selector = (
        (named_count.T[:, None, :] == 1) & (slot_before.T[:, None, :] == slot_index[None, :, None])
    ).astype(jnp.bfloat16)
    outgoing = jnp.einsum(
        "ejt,td->ejd", selector, token_rows, preferred_element_type=jnp.float32
    ).astype(jnp.bfloat16)
    own_half = up_weight[0, 0]
    partner_half = own_half
    for bit_number in range(section_bits):
        partner_half = from_partner(partner_half, "pipe", bit_number)
    lower_side = lax.axis_index("pipe") < section_count // 2
    full_weight = jnp.concatenate(
        [
            jnp.where(lower_side, own_half, partner_half),
            jnp.where(lower_side, partner_half, own_half),
        ],
        axis=1,
    )
    grad_rows = up_grad[0, 0]
    row_grad = jnp.einsum(
        "sjf,df->sjd", grad_rows, full_weight, preferred_element_type=jnp.float32
    ).astype(jnp.bfloat16)
    returned = lax.all_to_all(row_grad, "expert", split_axis=0, concat_axis=0, tiled=True)
    token_grad = jnp.einsum(
        "ejt,ejd->td", selector, returned, preferred_element_type=jnp.float32
    ).astype(jnp.bfloat16)
    arrived = lax.all_to_all(outgoing, "expert", split_axis=0, concat_axis=0, tiled=True)
    partial_value = jnp.einsum(
        "sjd,sjf->df", arrived, grad_rows, preferred_element_type=jnp.float32
    ).astype(jnp.bfloat16)
    width_half = own_half.shape[1]
    local_part = jnp.where(lower_side, partial_value[:, :width_half], partial_value[:, width_half:])
    whole_part = partial_value
    for bit_number in range(section_bits):
        whole_part = from_partner(whole_part, "pipe", bit_number)
    remote_part = jnp.where(lower_side, whole_part[:, :width_half], whole_part[:, width_half:])
    weight_grad = (local_part.astype(jnp.float32) + remote_part.astype(jnp.float32)).astype(
        jnp.bfloat16
    )
    return (token_grad[None], weight_grad[None, None])


def solution(mesh):
    placed = (
        P("pipe", "expert", None),
        P("pipe", "expert", None),
        P("pipe", "expert", None, None),
        P("pipe", "expert", None, None, None),
    )
    return jax.shard_map(
        on_device,
        mesh=mesh,
        in_specs=placed,
        out_specs=(P("pipe", "expert", None), P("pipe", "expert", None, None)),
        check_vma=False,
    )
```

profile of v0, /device:TPU:32, one launch (start us, length us, event | category | flops | bytes accessed | tf_op | source)
XLA Modules:
  0.0 882.9 jit_solution(1534867082329096721)
XLA Ops:
  0.6 0.0 copy-start
  0.6 0.8 convert_reduce_fusion
  1.5 0.1 copy.14
  1.6 0.2 reduce_window_sum.11
  1.8 0.1 copy.16
  1.8 3.0 convolution_convert_fusion
  4.9 6.5 copy.19
  11.3 11.8 %all-to-all-start.1 = ((bf16[64,14,3584]{2,1,0:T(8,128)(2,1)}), bf16[64,14,3584]{2,1,0:T(8,128)(2,1)}, u32[]{:S(2)}, u32[]{:S(2)}) async-start(bf16[64,14,3584]{2,1,0:T(8,128)(2,1)} %copy.19), calls=%async_computation.1 | async-start | bytes 14680064 | tf_op jit(solution)/shard_map/all_to_all | solution.py:52
  23.2 0.1 collective-permute-start
  23.3 6.7 collective-permute-done
  30.0 4.5 collective-permute-start.1
  34.5 162.8 %collective-permute-done.1 = bf16[3584,512]{1,0:T(8,128)(2,1)} collective-permute-done((bf16[3584,512]{1,0:T(8,128)(2,1)}, bf16[3584,512]{1,0:T(8,128)(2,1)}, u32[]{:S(2)}, u32[]{:S(2)}) %collective-permute-start.1) | collective-permute-done | bytes 3670048 | tf_op jit(solution)/shard_map/ppermute | solution.py:10
  197.3 6.6 broadcast_select_fusion.1
  203.9 137.8 %all-to-all-done.1 = bf16[64,14,3584]{2,1,0:T(8,128)(2,1)} async-done(((bf16[64,14,3584]{2,1,0:T(8,128)(2,1)}), bf16[64,14,3584]{2,1,0:T(8,128)(2,1)}, u32[]{:S(2)}, u32[]{:S(2)}) %all-to-all-start.1) | async-done | bytes 6422560 | tf_op jit(solution)/shard_map/all_to_all | solution.py:52
  341.7 0.0 copy-done
  341.7 0.0 copy-start.1
  341.7 0.0 copy-start.2
  341.7 17.5 %bitcast_convert_fusion = bf16[3584,1024]{1,0:T(8,128)(2,1)} fusion(bf16[64,14,3584]{2,1,0:T(8,128)(2,1)} %all-to-all-done.1, bf16[1,1,64,14,1024]{4,2,3,1,0:T(8,128)(2,1)S(1)} %copy-done), kind=kOutput, calls=%fused_computation | convolution fusion | flops 6580338688 | bytes 15597568 | tf_op jit(solution)/shard_map/sjd,sjf->df/dot_general | solution.py:53
  359.2 0.0 collective-permute-start.2
  359.2 0.0 copy-done.1
  359.2 0.0 copy-done.2
  359.2 7.1 fusion.7
  366.3 6.5 copy.17
  372.8 13.1 %all-to-all-start = ((bf16[64,14,3584]{2,1,0:T(8,128)(2,1)}), bf16[64,14,3584]{2,1,0:T(8,128)(2,1)}, u32[]{:S(2)}, u32[]{:S(2)}) async-start(bf16[64,14,3584]{2,1,0:T(8,128)(2,1)} %copy.17), calls=%async_computation | async-start | bytes 14680064 | tf_op jit(solution)/shard_map/all_to_all | solution.py:48
  386.0 0.0 collective-permute-done.2
  386.0 5.4 collective-permute-start.3
  391.4 472.6 %all-to-all-done = bf16[64,14,3584]{2,1,0:T(8,128)(2,1)} async-done(((bf16[64,14,3584]{2,1,0:T(8,128)(2,1)}), bf16[64,14,3584]{2,1,0:T(8,128)(2,1)}, u32[]{:S(2)}, u32[]{:S(2)}) %all-to-all-start) | async-done | bytes 6422560 | tf_op jit(solution)/shard_map/all_to_all | solution.py:48
  864.0 11.3 %fusion.14 = bf16[1,128,3584]{2,1,0:T(8,128)(2,1)} fusion(bf16[64,14,3584]{2,1,0:T(8,128)(2,1)} %all-to-all-done, s32[64,128]{1,0:T(8,128)S(1)} %copy.16, pred[64,128]{1,0:T(8,128)(4,1)S(1)} %compare_bitcast_fusion), kind=kOutput, calls=%fused_computation.14 | convolution fusion | flops 822771712 | bytes 7380992 | tf_op jit(solution)/shard_map/ejt,ejd->td/dot_general | solution.py:49
  875.3 0.0 collective-permute-done.3
  875.3 7.6 fusion.17
  (2 shorter events, 0.0 us)
Async XLA Ops:
  0.6 341.1 %copy-start = (bf16[1,1,64,14,1024]{4,2,3,1,0:T(8,128)(2,1)S(1)}, bf16[1,1,64,14,1024]{4,2,3,1,0:T(8,128)(2,1)}, u32[]{:S(2)}) copy-start(bf16[1,1,64,14,1024]{4,2,3,1,0:T(8,128)(2,1)} %param.7) | copy-start | bytes 5505028
  11.3 330.4 %all-to-all-start.1 = ((bf16[64,14,3584]{2,1,0:T(8,128)(2,1)}), bf16[64,14,3584]{2,1,0:T(8,128)(2,1)}, u32[]{:S(2)}, u32[]{:S(2)}) async-start(bf16[64,14,3584]{2,1,0:T(8,128)(2,1)} %copy.19), calls=%async_computation.1 | async-start | bytes 14680064 | tf_op jit(solution)/shard_map/all_to_all | solution.py:52
  23.2 6.8 collective-permute-start
  30.0 167.3 %collective-permute-start.1 = (bf16[3584,512]{1,0:T(8,128)(2,1)}, bf16[3584,512]{1,0:T(8,128)(2,1)}, u32[]{:S(2)}, u32[]{:S(2)}) collective-permute-start(bf16[3584,512]{1,0:T(8,128)(2,1)} %collective-permute-done), channel_id=1, source_target_pairs={{0,128},{64,192},{128,0},{192,64},{1,129},{65,193},{129,1},{193,65... | collective-permute-start | bytes 11010056 | tf_op jit(solution)/shard_map/ppermute | solution.py:10
  341.7 17.5 %copy-start.1 = (bf16[3584,512]{1,0:T(8,128)(2,1)S(1)}, bf16[3584,512]{1,0:T(8,128)(2,1)}, u32[]{:S(2)}) copy-start(bf16[3584,512]{1,0:T(8,128)(2,1)} %get-tuple-element.2) | copy-start | bytes 11010052
  341.7 17.5 %copy-start.2 = (bf16[3584,512]{1,0:T(8,128)(2,1)S(1)}, bf16[3584,512]{1,0:T(8,128)(2,1)}, u32[]{:S(2)}) copy-start(bf16[3584,512]{1,0:T(8,128)(2,1)} %get-tuple-element.3) | copy-start | bytes 11010052
  359.2 26.7 %collective-permute-start.2 = (bf16[3584,1024]{1,0:T(8,128)(2,1)}, bf16[3584,1024]{1,0:T(8,128)(2,1)}, u32[]{:S(2)}, u32[]{:S(2)}) collective-permute-start(bf16[3584,1024]{1,0:T(8,128)(2,1)} %bitcast_convert_fusion), channel_id=1, source_target_pairs={{0,64},{64,0},{128,192},{192,128},{1,65},{65,1},{129,193},{193,129... | collective-permute-start | bytes 22020104 | tf_op jit(solution)/shard_map/ppermute | solution.py:10
  372.8 491.2 %all-to-all-start = ((bf16[64,14,3584]{2,1,0:T(8,128)(2,1)}), bf16[64,14,3584]{2,1,0:T(8,128)(2,1)}, u32[]{:S(2)}, u32[]{:S(2)}) async-start(bf16[64,14,3584]{2,1,0:T(8,128)(2,1)} %copy.17), calls=%async_computation | async-start | bytes 14680064 | tf_op jit(solution)/shard_map/all_to_all | solution.py:48
  386.0 489.4 %collective-permute-start.3 = (bf16[3584,1024]{1,0:T(8,128)(2,1)}, bf16[3584,1024]{1,0:T(8,128)(2,1)}, u32[]{:S(2)}, u32[]{:S(2)}) collective-permute-start(bf16[3584,1024]{1,0:T(8,128)(2,1)} %collective-permute-done.2), channel_id=1, source_target_pairs={{0,128},{64,192},{128,0},{192,64},{1,129},{65,193},{129,1},{193,65... | collective-permute-start | bytes 22020104 | tf_op jit(solution)/shard_map/ppermute | solution.py:10
where the time goes:
time: 889 us; the launch traced here: 883 us
  waiting for transfers between devices  780 us (88%)
  matrix products  38.9 us (4%)
  starting transfers between devices  35 us (4%)
  other arithmetic  15.2 us (2%)
  local copies, waits for them, and re-layouts  13.2 us (1%)
    all_to_all x1, waiting for transfers between devices, on_device(): lax.all_to_all(row_grad, 'expert', split_axis=0, concat_axis=0, tiled=True)  473 us
    ppermute x4, waiting for transfers between devices, from_partner(): return lax.ppermute(value, axis, pairs)  170 us
    all_to_all x1, waiting for transfers between devices, on_device(): lax.all_to_all(outgoing, 'expert', split_axis=0, concat_axis=0, tiled=True)  138 us
  transfers between devices with their start and end apart: 6, of which 4 were waited for; matrix products, arithmetic and copies ran while one was open for 4% of the time, Pallas kernels for 0%

commit v1 on v0

v1 whole, which is shorter than its diff:
```python
import jax
import jax.numpy as jnp
from jax import lax
from jax.sharding import Mesh, PartitionSpec as P

HI, CORE, X, LO, Y = "hi", "core", "x", "lo", "y"
AXES = (HI, CORE, X, LO, Y)


def mirror_pairs(sizes):
    n_hi, n_core, n_x, n_lo, n_y = sizes
    block = n_x * n_lo * n_y
    pairs = []
    for section in range(n_hi * n_core):
        for place in range(block):
            pairs.append((section * block + place, (n_hi * n_core - 1 - section) * block + place))
    return pairs


def mirror_rings(sizes):
    n_hi, n_core, n_x, n_lo, n_y = sizes
    return [
        [(hi * n_core + (core ^ hi)) * n_lo + lo for hi in range(n_hi) for lo in range(n_lo)]
        for core in range(n_core)
    ]


def dot(a, b, dims):
    return lax.dot_general(a, b, (dims, ((), ())), preferred_element_type=jnp.float32)


def on_device(sizes, tokens, expert_ids, up_weight, up_grad):
    n_hi, n_core, n_x, n_lo, n_y = sizes
    token_rows = tokens[0]
    width = token_rows.shape[1]
    count = token_rows.shape[0]
    weight = up_weight[0, 0]
    half = weight.shape[1]
    sources, most = up_grad.shape[2], up_grad.shape[3]
    rows = sources * most
    plane = n_x * n_y
    slots = n_lo * most
    low = lax.axis_index(HI) == 0
    rings = mirror_rings(sizes)
    ring_axes = (HI, CORE, LO)

    grad = jnp.transpose(up_grad[0, 0], (1, 0, 2)).reshape(rows, 2 * half)
    grad_own = jnp.where(low, grad[:, :half], grad[:, half:])
    grad_send = jnp.where(low, grad[:, half:], grad[:, :half])
    grad_mirror = lax.ppermute(grad_send, AXES, mirror_pairs(sizes))

    place = jnp.arange(rows, dtype=jnp.int32)
    at_x, at_y = place // (n_y * slots), (place // slots) % n_y
    at_lo, at_slot = (place // most) % n_lo, place % most
    taken = at_slot * sources + (at_x * n_lo + at_lo) * n_y + at_y
    order = (taken[:, None] == place[None, :]).astype(jnp.bfloat16)
    own_rows = dot(order, grad_own, ((1,), (0,))).astype(jnp.bfloat16)
    mirror_rows = dot(order, grad_mirror, ((1,), (0,))).astype(jnp.bfloat16)

    def exchange(value):
        value = value.reshape(plane, slots, width)
        return lax.all_to_all(value, (X, Y), 0, 0, tiled=True).reshape(rows, width)

    own_out = dot(own_rows, weight, ((1,), (1,))).astype(jnp.bfloat16)
    own_back = exchange(own_out)
    mirror_out = dot(mirror_rows, weight, ((1,), (1,))).astype(jnp.bfloat16)
    mirror_back = exchange(mirror_out)

    ids = lax.all_gather(expert_ids[0].T, ring_axes, axis=0, axis_index_groups=rings)
    gathered = lax.all_gather(token_rows, ring_axes, axis=0, axis_index_groups=rings, tiled=True)
    ids = ids.reshape(n_hi, n_lo, expert_ids.shape[2], count)
    member = jnp.arange(plane, dtype=jnp.int32)
    expert = ((member // n_y) * n_lo + lax.axis_index(LO)) * n_y + member % n_y
    named = jnp.any(ids[:, :, None] == expert[None, None, :, None, None], axis=3)
    earlier = jnp.arange(count)[:, None] < jnp.arange(count)[None, :]
    before = dot(named.astype(jnp.bfloat16), earlier.astype(jnp.bfloat16), ((3,), (0,)))
    source = jnp.arange(n_lo, dtype=jnp.int32)[None, :, None, None]
    key = jnp.where(named, source * most + before.astype(jnp.int32), -1)
    key = jnp.where(named & (before < most), key, -1)
    key = jnp.transpose(key, (0, 2, 1, 3)).reshape(n_hi, plane, n_lo * count)

    def selector(some):
        slot = jnp.arange(slots, dtype=jnp.int32)[None, :, None]
        return (some[:, None, :] == slot).astype(jnp.bfloat16).reshape(rows, n_lo * count)

    key_own = jnp.where(low, key[0], key[1])
    key_mirror = jnp.where(low, key[1], key[0])
    sums_own = dot(selector(key_own), own_back, ((0,), (0,))).astype(jnp.bfloat16)
    sums_mirror = dot(selector(key_mirror), mirror_back, ((0,), (0,))).astype(jnp.bfloat16)
    sums = jnp.concatenate(
        [jnp.where(low, sums_own, sums_mirror), jnp.where(low, sums_mirror, sums_own)]
    )
    token_grad = lax.psum_scatter(
        sums, ring_axes, scatter_dimension=0, axis_index_groups=rings, tiled=True
    )

    per_section = n_lo * count
    sent_first = dot(selector(key[0]), gathered[:per_section], ((1,), (0,))).astype(jnp.bfloat16)
    sent_second = dot(selector(key[1]), gathered[per_section:], ((1,), (0,))).astype(jnp.bfloat16)
    arrived_first = exchange(sent_first)
    arrived_second = exchange(sent_second)
    rows_first = jnp.where(low, own_rows, mirror_rows)
    rows_second = jnp.where(low, mirror_rows, own_rows)
    total = dot(arrived_first, rows_first, ((0,), (0,)))
    total = total + dot(arrived_second, rows_second, ((0,), (0,)))
    return (token_grad[None], total.astype(jnp.bfloat16)[None, None])


def solution(mesh):
    sizes = (2, 2, 4, 4, 4)
    fine = Mesh(mesh.devices.reshape(sizes), AXES)
    pipe, expert = (HI, CORE), (X, LO, Y)

    def device_body(*args):
        return on_device(sizes, *args)

    return jax.shard_map(
        device_body,
        mesh=fine,
        in_specs=(
            P(pipe, expert, None),
            P(pipe, expert, None),
            P(pipe, expert, None, None),
            P(pipe, expert, None, None, None),
        ),
        out_specs=(P(pipe, expert, None), P(pipe, expert, None, None)),
        check_vma=False,
    )
```

time: 889 us -> 502 us (0.56)
  waiting for transfers between devices: 780 us -> 354 us
  matrix products: 38.9 us -> 64 us
  blocking collectives: 0 us -> 19.3 us
  between operations: 0.71 us -> 14.2 us
  local copies, waits for them, and re-layouts: 13.2 us -> 1.08 us
    all_to_all x2 -> x4, waiting for transfers between devices: 610 us -> 313 us  [exchange(): return lax.all_to_all(value, (X, Y), 0, 0, tiled=True).reshape(rows, width)]
    ppermute x4 -> x1, waiting for transfers between devices: 170 us -> 40.4 us  [on_device(): grad_mirror = lax.ppermute(grad_send, AXES, mirror_pairs(sizes))]
    dot_general x4 -> x11, matrix products: 38.9 us -> 64 us  [dot(): lax.dot_general(a, b, (dims, ((), ())), preferred_element_type=jnp.float32)]
    all_gather x0 -> x1, blocking collectives: none -> 19.3 us  [on_device(): lax.all_gather(expert_ids[0].T, ring_axes, axis=0, axis_index_groups=rings)]
    convert_element_type x2 -> x0, local copies, waits for them, and re-layouts: 13 us -> none  [the longest x1 6.51 us: on_device(): row_grad = jnp.einsum('sjf,df->sjd', grad_rows, full_weight, preferred_el...]
    all_to_all x2 -> x4, starting transfers between devices: 25 us -> 34.8 us  [exchange(): return lax.all_to_all(value, (X, Y), 0, 0, tiled=True).reshape(rows, width)]
  transfers between devices with their start and end apart: 6 -> 7, of which waited for: 4 -> 5; matrix products, arithmetic and copies ran while one was open for 4% -> 13% of each run, Pallas kernels for 0% -> 0%
where the time goes in v1:
time: 502 us
  waiting for transfers between devices  354 us (71%)
  matrix products  64 us (13%)
  starting transfers between devices  40.7 us (8%)
  blocking collectives  19.3 us (4%)
  between operations  14.2 us (3%)
  other arithmetic  7.9 us (2%)
    all_to_all x4, waiting for transfers between devices, exchange(): return lax.all_to_all(value, (X, Y), 0, 0, tiled=True).reshape(rows, width)  313 us
    dot_general x11, matrix products, dot(): lax.dot_general(a, b, (dims, ((), ())), preferred_element_type=jnp.float32)  64 us
    ppermute x1, waiting for transfers between devices, on_device(): grad_mirror = lax.ppermute(grad_send, AXES, mirror_pairs(sizes))  40.4 us
    all_to_all x4, starting transfers between devices, exchange(): return lax.all_to_all(value, (X, Y), 0, 0, tiled=True).reshape(rows, width)  34.8 us
    all_gather x1, blocking collectives, on_device(): lax.all_gather(expert_ids[0].T, ring_axes, axis=0, axis_index_groups=rings)  19.3 us
  transfers between devices with their start and end apart: 7, of which 5 were waited for; matrix products, arithmetic and copies ran while one was open for 13% of the time, Pallas kernels for 0%

profile of v1, /device:TPU:32, one launch (start us, length us, event | category | flops | bytes accessed | tf_op | source)
XLA Modules:
  0.0 501.7 jit_solution(14514019978678432248)
XLA Ops:
  7.2 1.7 broadcast_select_fusion.2
  8.9 5.8 %collective-permute-start = (bf16[896,512]{1,0:T(8,128)(2,1)S(1)}, bf16[896,512]{1,0:T(8,128)(2,1)S(1)}, u32[]{:S(2)}, u32[]{:S(2)}) collective-permute-start(bf16[896,512]{1,0:T(8,128)(2,1)S(1)} %broadcast_select_fusion.2), channel_id=1, source_target_pairs={{0,192},{1,193},{2,194},{3,195},{4,196},{5,197},{6,198},{7,199},{8... | collective-permute-start | bytes 2752520 | tf_op jit(solution)/shard_map/ppermute | solution.py:50
  14.7 40.4 %collective-permute-done = bf16[896,512]{1,0:T(8,128)(2,1)S(1)} collective-permute-done((bf16[896,512]{1,0:T(8,128)(2,1)S(1)}, bf16[896,512]{1,0:T(8,128)(2,1)S(1)}, u32[]{:S(2)}, u32[]{:S(2)}) %collective-permute-start) | collective-permute-done | bytes 917536 | tf_op jit(solution)/shard_map/ppermute | solution.py:50
  55.1 1.2 fusion.8
  56.3 5.6 %convolution_convert_fusion.2 = bf16[896,3584]{1,0:T(8,128)(2,1)} fusion(bf16[896,512]{1,0:T(8,128)(2,1)S(1)} %fusion.8, bf16[1,1,3584,512]{3,2,1,0:T(8,128)(2,1)S(1)} %copy-done.2), kind=kOutput, calls=%fused_computation.6 | convolution fusion | flops 3291545600 | bytes 11010048 | tf_op jit(solution)/shard_map/dot_general | solution.py:29
  61.8 7.2 %all-to-all-start.1 = ((bf16[16,56,3584]{2,1,0:T(8,128)(2,1)}), bf16[16,56,3584]{2,1,0:T(8,128)(2,1)}, u32[]{:S(2)}, u32[]{:S(2)}) async-start(bf16[16,56,3584]{2,1,0:T(8,128)(2,1)} %bitcast.75), calls=%async_computation.1 | async-start | bytes 12845056 | tf_op jit(solution)/shard_map/all_to_all | solution.py:62
  69.1 0.0 all-gather.5.cloned.1.call-start
  69.1 0.7 all-gather.5.cloned.1.call-update
  69.8 1.2 fusion.7
  71.0 0.9 copy-done.4
  71.9 5.5 %convolution_convert_fusion.3 = bf16[896,3584]{1,0:T(8,128)(2,1)} fusion(bf16[896,512]{1,0:T(8,128)(2,1)S(1)} %fusion.7, bf16[1,1,3584,512]{3,2,1,0:T(8,128)(2,1)S(1)} %copy-done.3), kind=kOutput, calls=%fused_computation.7 | convolution fusion | flops 3291545600 | bytes 11010048 | tf_op jit(solution)/shard_map/dot_general | solution.py:29
  77.4 100.3 %all-to-all-done.1 = bf16[16,56,3584]{2,1,0:T(8,128)(2,1)} async-done(((bf16[16,56,3584]{2,1,0:T(8,128)(2,1)}), bf16[16,56,3584]{2,1,0:T(8,128)(2,1)}, u32[]{:S(2)}, u32[]{:S(2)}) %all-to-all-start.1) | async-done | bytes 6422560 | tf_op jit(solution)/shard_map/all_to_all | solution.py:62
  177.7 12.3 %all-to-all-start = ((bf16[16,56,3584]{2,1,0:T(8,128)(2,1)}), bf16[16,56,3584]{2,1,0:T(8,128)(2,1)}, u32[]{:S(2)}, u32[]{:S(2)}) async-start(bf16[16,56,3584]{2,1,0:T(8,128)(2,1)} %bitcast.74), calls=%async_computation | async-start | bytes 12845056 | tf_op jit(solution)/shard_map/all_to_all | solution.py:62
  190.0 0.0 reduce-scatter.2.cloned.1.call-start
  190.0 19.3 %all-gather.2 = s32[8,4,128]{2,1,0:T(4,128)S(1)} all-gather(s32[1,4,128]{2,1,0:T(4,128)S(1)} %bitcast.85), channel_id=2, replica_groups={{0,4,8,12,192,196,200,204},{64,68,72,76,128,132,136,140},{1,5,9,13,193,..., dimensions={0}, use_global_device_ids=true | all-gather | bytes 18432 | tf_op jit(solution)/shard_map/all_gather | solution.py:69
  209.4 0.1 compare_reduce_fusion
  209.5 0.2 select_bitcast_fusion
  209.7 8.3 %bitcast_convert_fusion = bf16[512,3584]{1,0:T(8,128)(2,1)} fusion(bf16[16,56,3584]{2,1,0:T(8,128)(2,1)} %all-to-all-done.1, s32[16,512]{1,0:T(8,128)S(1)} %get-tuple-element.5), kind=kOutput, calls=%fused_computation.1 | convolution fusion | flops 3290628096 | bytes 10125312 | tf_op jit(solution)/shard_map/dot_general | solution.py:29
  218.0 73.3 %all-to-all-done = bf16[16,56,3584]{2,1,0:T(8,128)(2,1)} async-done(((bf16[16,56,3584]{2,1,0:T(8,128)(2,1)}), bf16[16,56,3584]{2,1,0:T(8,128)(2,1)}, u32[]{:S(2)}, u32[]{:S(2)}) %all-to-all-start) | async-done | bytes 6422560 | tf_op jit(solution)/shard_map/all_to_all | solution.py:62
  291.4 8.9 %broadcast_select_fusion.1 = (bf16[512,3584]{1,0:T(8,128)(2,1)S(1)}, bf16[512,3584]{1,0:T(8,128)(2,1)}) fusion(bf16[512,3584]{1,0:T(8,128)(2,1)} %bitcast_convert_fusion, pred[]{:T(512)S(6)} %eq.109, bf16[16,56,3584]{2,1,0:T(8,128)(2,1)} %all-to-all-done, s32[16,512]{1,0:T(8,128)S(1)} %get-tuple-element.4), kind=kOutput, calls=%fused_computation.14 | convolution fusion | flops 3294298112 | bytes 17465344 | tf_op jit(solution)/shard_map/dot_general | solution.py:29
  300.2 5.5 %pad_maximum_fusion = bf16[1024,3584]{1,0:T(8,128)(2,1)} fusion(bf16[512,3584]{1,0:T(8,128)(2,1)} %get-tuple-element.3, bf16[512,3584]{1,0:T(8,128)(2,1)S(1)} %get-tuple-element.2), kind=kLoop, calls=%fused_computation | loop fusion | flops 14680064 | bytes 14680064 | tf_op jit(solution)/shard_map/concatenate | solution.py:90
  305.7 0.1 eq.126
  305.8 0.6 bitcast_compare_fusion
  306.4 0.0 all-gather.5.cloned.1.call-done
  306.5 7.4 %convolution_convert_fusion.1 = bf16[896,3584]{1,0:T(8,128)(2,1)} fusion(pred[896,512]{1,0:T(32,128)(4,1)S(1)} %get-tuple-element.9, bf16[1,1024,3584]{2,1,0:T(8,128)(2,1)} %all-gather.5.cloned.1.call-done), kind=kOutput, calls=%fused_computation.5 | convolution fusion | flops 3291545600 | bytes 10551296 | tf_op jit(solution)/shard_map/dot_general | solution.py:29
  313.8 8.3 %all-to-all-start.2 = ((bf16[16,56,3584]{2,1,0:T(8,128)(2,1)}), bf16[16,56,3584]{2,1,0:T(8,128)(2,1)}, u32[]{:S(2)}, u32[]{:S(2)}) async-start(bf16[16,56,3584]{2,1,0:T(8,128)(2,1)} %bitcast.77), calls=%async_computation.3 | async-start | bytes 12845056 | tf_op jit(solution)/shard_map/all_to_all | solution.py:62
  322.2 7.5 %convolution_convert_fusion = bf16[896,3584]{1,0:T(8,128)(2,1)} fusion(pred[896,512]{1,0:T(32,128)(4,1)S(1)} %get-tuple-element.8, bf16[1,1024,3584]{2,1,0:T(8,128)(2,1)} %all-gather.5.cloned.1.call-done), kind=kOutput, calls=%fused_computation.4 | convolution fusion | flops 3291545600 | bytes 10551296 | tf_op jit(solution)/shard_map/dot_general | solution.py:29
  329.7 72.4 %all-to-all-done.2 = bf16[16,56,3584]{2,1,0:T(8,128)(2,1)} async-done(((bf16[16,56,3584]{2,1,0:T(8,128)(2,1)}), bf16[16,56,3584]{2,1,0:T(8,128)(2,1)}, u32[]{:S(2)}, u32[]{:S(2)}) %all-to-all-start.2) | async-done | bytes 6422560 | tf_op jit(solution)/shard_map/all_to_all | solution.py:62
  402.1 7.0 %all-to-all-start.3 = ((bf16[16,56,3584]{2,1,0:T(8,128)(2,1)}), bf16[16,56,3584]{2,1,0:T(8,128)(2,1)}, u32[]{:S(2)}, u32[]{:S(2)}) async-start(bf16[16,56,3584]{2,1,0:T(8,128)(2,1)} %bitcast.76), calls=%async_computation.4 | async-start | bytes 12845056 | tf_op jit(solution)/shard_map/all_to_all | solution.py:62
  409.0 9.0 %fusion.10 = f32[3584,512]{1,0:T(8,128)} fusion(bf16[896,3584]{1,0:T(8,128)(2,1)} %bitcast.21, bf16[896,512]{1,0:T(8,128)(2,1)S(1)} %copy-done.5, bf16[896,512]{1,0:T(8,128)(2,1)S(1)} %fusion.8, pred[]{:T(512)S(6)} %eq.109), kind=kOutput, calls=%fused_computation.27 | convolution fusion | flops 3288793088 | bytes 15597569 | tf_op jit(solution)/shard_map/dot_general | solution.py:29
  418.0 67.4 %all-to-all-done.3 = bf16[16,56,3584]{2,1,0:T(8,128)(2,1)} async-done(((bf16[16,56,3584]{2,1,0:T(8,128)(2,1)}), bf16[16,56,3584]{2,1,0:T(8,128)(2,1)}, u32[]{:S(2)}, u32[]{:S(2)}) %all-to-all-start.3) | async-done | bytes 6422560 | tf_op jit(solution)/shard_map/all_to_all | solution.py:62
  485.4 9.5 %fusion = bf16[1,1,3584,512]{3,2,1,0:T(8,128)(2,1)} fusion(f32[3584,512]{1,0:T(8,128)} %fusion.10, bf16[896,3584]{1,0:T(8,128)(2,1)} %bitcast.25, bf16[896,512]{1,0:T(8,128)(2,1)S(1)} %fusion.8, bf16[896,512]{1,0:T(8,128)(2,1)S(1)} %copy-done.5, pred[]{:T(512)S(6)} %eq.109), kind=kOutput, calls=%fused_computation.8 | convolution fusion | flops 3292463104 | bytes 19267584 | tf_op jit(solution)/shard_map/dot_general | solution.py:29
  (22 shorter events, 0.1 us)
Async XLA Ops:
  7.2 49.1 %copy-start.2 = (bf16[1,1,3584,512]{3,2,1,0:T(8,128)(2,1)S(1)}, bf16[1,1,3584,512]{3,2,1,0:T(8,128)(2,1)}, u32[]{:S(2)}) copy-start(bf16[1,1,3584,512]{3,2,1,0:T(8,128)(2,1)} %param.6) | copy-start | bytes 11010052
  8.9 46.2 %collective-permute-start = (bf16[896,512]{1,0:T(8,128)(2,1)S(1)}, bf16[896,512]{1,0:T(8,128)(2,1)S(1)}, u32[]{:S(2)}, u32[]{:S(2)}) collective-permute-start(bf16[896,512]{1,0:T(8,128)(2,1)S(1)} %broadcast_select_fusion.2), channel_id=1, source_target_pairs={{0,192},{1,193},{2,194},{3,195},{4,196},{5,197},{6,198},{7,199},{8... | collective-permute-start | bytes 2752520 | tf_op jit(solution)/shard_map/ppermute | solution.py:50
  61.8 8.0 %copy-start = (bf16[1,1,64,14,1024]{4,2,3,1,0:T(8,128)(2,1)S(1)}, bf16[1,1,64,14,1024]{4,2,3,1,0:T(8,128)(2,1)}, u32[]{:S(2)}) copy-start(bf16[1,1,64,14,1024]{4,2,3,1,0:T(8,128)(2,1)} %param.7) | copy-start | bytes 5505028
  61.8 115.8 %all-to-all-start.1 = ((bf16[16,56,3584]{2,1,0:T(8,128)(2,1)}), bf16[16,56,3584]{2,1,0:T(8,128)(2,1)}, u32[]{:S(2)}, u32[]{:S(2)}) async-start(bf16[16,56,3584]{2,1,0:T(8,128)(2,1)} %bitcast.75), calls=%async_computation.1 | async-start | bytes 12845056 | tf_op jit(solution)/shard_map/all_to_all | solution.py:62
  69.1 237.4 %all-gather.5.cloned.1.call-start = ((), (), s32[]{:S(2)}) async-start(), calls=%async_computation.6 | async-start | bytes 8257536 | tf_op jit(solution)/shard_map/all_gather | solution.py:70
  69.8 2.1 copy-start.3
  71.0 0.9 copy-start.4
  177.7 12.4 %copy-start.1 = (s32[1,128,4]{1,2,0:T(4,128)S(1)}, s32[1,128,4]{1,2,0:T(4,128)}, u32[]{:S(2)}) copy-start(s32[1,128,4]{1,2,0:T(4,128)} %param.5) | copy-start | bytes 6148
  177.7 113.7 %all-to-all-start = ((bf16[16,56,3584]{2,1,0:T(8,128)(2,1)}), bf16[16,56,3584]{2,1,0:T(8,128)(2,1)}, u32[]{:S(2)}, u32[]{:S(2)}) async-start(bf16[16,56,3584]{2,1,0:T(8,128)(2,1)} %bitcast.74), calls=%async_computation | async-start | bytes 12845056 | tf_op jit(solution)/shard_map/all_to_all | solution.py:62
  190.0 304.9 %reduce-scatter.2.cloned.1.call-start = ((), (), s32[]{:S(2)}) async-start(), calls=%async_computation.5 | async-start | bytes 8257536 | tf_op jit(solution)/shard_map/reduce_scatter | solution.py:93
  313.8 88.2 %all-to-all-start.2 = ((bf16[16,56,3584]{2,1,0:T(8,128)(2,1)}), bf16[16,56,3584]{2,1,0:T(8,128)(2,1)}, u32[]{:S(2)}, u32[]{:S(2)}) async-start(bf16[16,56,3584]{2,1,0:T(8,128)(2,1)} %bitcast.77), calls=%async_computation.3 | async-start | bytes 12845056 | tf_op jit(solution)/shard_map/all_to_all | solution.py:62
  402.1 7.0 %copy-start.5 = (bf16[896,512]{1,0:T(8,128)(2,1)S(1)}, bf16[896,512]{1,0:T(8,128)(2,1)}, u32[]{:S(2)}) copy-start(bf16[896,512]{1,0:T(8,128)(2,1)} %copy-done.4) | copy-start | bytes 2752516
  402.1 83.3 %all-to-all-start.3 = ((bf16[16,56,3584]{2,1,0:T(8,128)(2,1)}), bf16[16,56,3584]{2,1,0:T(8,128)(2,1)}, u32[]{:S(2)}, u32[]{:S(2)}) async-start(bf16[16,56,3584]{2,1,0:T(8,128)(2,1)} %bitcast.76), calls=%async_computation.4 | async-start | bytes 12845056 | tf_op jit(solution)/shard_map/all_to_all | solution.py:62
Sparse Core Ops, SparseCore 0:
  71.7 85.2 all-gather.4
  305.9 84.8 reduce-scatter.1

commit v2 on v1

v2 whole, which is shorter than its diff:
```python
import functools

import jax
import jax.numpy as jnp
from jax import lax
from jax.experimental import pallas as pl
from jax.experimental.pallas import tpu as pltpu
from jax.sharding import Mesh, PartitionSpec as P


HI, CORE, X, LO, Y = "hi", "core", "x", "lo", "y"
AXES = (HI, CORE, X, LO, Y)


def mirror_pairs(sizes):
    n_hi, n_core, n_x, n_lo, n_y = sizes
    block = n_x * n_lo * n_y
    pairs = []
    for section in range(n_hi * n_core):
        for place in range(block):
            pairs.append((section * block + place, (n_hi * n_core - 1 - section) * block + place))
    return pairs


def mirror_rings(sizes):
    n_hi, n_core, _, n_lo, _ = sizes
    return [
        [(hi * n_core + (core ^ hi)) * n_lo + lo for hi in range(n_hi) for lo in range(n_lo)]
        for core in range(n_core)
    ]


def shifted(value, axis, size, by):
    if by == 0:
        return value
    return lax.ppermute(value, axis, [(i, (i + by) % size) for i in range(size)])


def dot(a, b, dims):
    return lax.dot_general(a, b, (dims, ((), ())), preferred_element_type=jnp.float32)


def hidden_sum_kernel(*refs):
    grads, out = refs[0], refs[-1]
    total = None
    for i, piece in enumerate(refs[1:-1]):
        part = jnp.dot(grads[i], piece[...], preferred_element_type=jnp.float32)
        total = part if total is None else total + part
    out[...] = total.T.astype(out.dtype)


def hidden_sum(grads, pieces):
    count, half, depth = grads.shape
    width = pieces[0].shape[1]
    tile = 512 if width % 512 == 0 else width
    return pl.pallas_call(
        hidden_sum_kernel,
        out_shape=jax.ShapeDtypeStruct((width, half), jnp.bfloat16),
        grid=(width // tile,),
        in_specs=[pl.BlockSpec((count, half, depth), lambda i: (0, 0, 0))]
        + [pl.BlockSpec((depth, tile), lambda i: (0, i))] * count,
        out_specs=pl.BlockSpec((tile, half), lambda i: (i, 0)),
        name="hidden_sum",
    )(grads, *pieces)


def merge_kernel(*refs):
    out = refs[-1]
    size = refs[0].shape[0]
    for i, piece in enumerate(refs[:-1]):
        out[i * size : (i + 1) * size, :] = piece[...]


def merged(parts, step, size):
    width = parts[0].shape[1]
    tile = 896 if width % 896 == 0 else width
    return pl.pallas_call(
        merge_kernel,
        out_shape=jax.ShapeDtypeStruct((len(parts) * size, width), parts[0].dtype),
        grid=(width // tile,),
        in_specs=[pl.BlockSpec((size, tile), lambda i: (step, i))] * len(parts),
        out_specs=pl.BlockSpec((len(parts) * size, tile), lambda i: (0, i)),
        name="merged",
    )(*parts)


def key_kernel(sizes, most, top, place, ids, out, named_all):
    _, _, n_x, n_lo, n_y = sizes
    plane, count = n_x * n_y, ids.shape[2]
    my_x, my_lo, my_y = place[0], place[1], place[2]
    member = lax.broadcasted_iota(jnp.int32, (plane, count), 0)
    major, minor = member // n_y, member % n_y
    orders = (
        (0, (my_x + major) % n_x, (my_y + minor) % n_y),
        (1, (my_x + minor) % n_x, (my_y + major) % n_y),
        (0, major, minor),
        (1, major, minor),
    )
    for i, (hi, at_x, at_y) in enumerate(orders):
        expert = ((at_x * n_lo + my_lo) * n_y + at_y).astype(jnp.float32)
        for lo in range(n_lo):
            some = ids[hi * n_lo + lo].astype(jnp.float32)
            named = expert == some[0:1]
            for k in range(1, top):
                named = named | (expert == some[k : k + 1])
            row = (i * n_lo + lo) * plane
            named_all[row : row + plane, :] = jnp.where(named, 1.0, 0.0)
    token = lax.broadcasted_iota(jnp.int32, (count, count), 0)
    later = lax.broadcasted_iota(jnp.int32, (count, count), 1)
    earlier = jnp.where(token < later, 1.0, 0.0).astype(jnp.bfloat16)
    before = jnp.dot(
        named_all[...].astype(jnp.bfloat16), earlier, preferred_element_type=jnp.float32
    )
    for i in range(len(orders)):
        for lo in range(n_lo):
            row = (i * n_lo + lo) * plane
            slot = before[row : row + plane].astype(jnp.int32) + lo * most
            key = jnp.where(named_all[row : row + plane, :] > 0.5, slot, -1)
            out[i, :, lo * count : (lo + 1) * count] = key


def key_table(sizes, most, top, count, place, gathered):
    _, _, n_x, n_lo, n_y = sizes
    rings, per_source, _ = gathered.shape
    spare = per_source - count
    shape = (4, n_x * n_y, n_lo * count)
    return pl.pallas_call(
        functools.partial(key_kernel, sizes, most, top),
        out_shape=jax.ShapeDtypeStruct(shape, jnp.int32),
        grid=(1,),
        in_specs=[
            pl.BlockSpec(memory_space=pltpu.SMEM),
            pl.BlockSpec((rings, spare, count), lambda i: (0, count // spare, 0)),
        ],
        out_specs=pl.BlockSpec(shape, lambda i: (0, 0, 0)),
        scratch_shapes=[pltpu.VMEM((4 * n_lo * n_x * n_y, count), jnp.float32)],
        name="key_table",
    )(place, gathered)


def on_device(sizes, tokens, expert_ids, up_weight, up_grad):
    n_hi, _, n_x, n_lo, n_y = sizes
    token_rows = tokens[0]
    count, width = token_rows.shape
    weight = up_weight[0, 0]
    half = weight.shape[1]
    sources, most = up_grad.shape[2], up_grad.shape[3]
    top = expert_ids.shape[2]
    rows = sources * most
    plane = n_x * n_y
    slots = n_lo * most
    low = lax.axis_index(HI) == 0
    rings = mirror_rings(sizes)
    ring_axes = (HI, CORE, LO)
    bf16 = jnp.bfloat16
    spare = 8

    grad = jnp.transpose(up_grad[0, 0], (1, 0, 2)).reshape(rows, 2 * half)
    grad_own = jnp.where(low, grad[:, :half], grad[:, half:])
    grad_send = jnp.where(low, grad[:, half:], grad[:, :half])
    grad_mirror = lax.ppermute(grad_send, AXES, mirror_pairs(sizes))

    id_rows = jnp.pad(expert_ids[0].T.astype(bf16), ((0, spare - top), (0, width - count)))
    outgoing = jnp.concatenate([token_rows, id_rows])
    gathered = lax.all_gather(outgoing, ring_axes, axis=0, axis_index_groups=rings, tiled=True)

    def order(place, at_x, at_y):
        at_lo, at_slot = (place // most) % n_lo, place % most
        taken = at_slot * sources + (at_x * n_lo + at_lo) * n_y + at_y
        return (taken[:, None] == place[None, :]).astype(bf16)

    place = jnp.arange(rows, dtype=jnp.int32)
    by_place = order(place, place // (n_y * slots), (place // slots) % n_y)

    def row_grad(grads):
        sorted_rows = dot(by_place, grads, ((1,), (0,))).astype(bf16)
        return dot(sorted_rows, weight, ((1,), (1,))).astype(bf16)

    def exchange(value):
        value = value.reshape(plane, slots, width)
        return lax.all_to_all(value, (X, Y), 0, 0, tiled=True).reshape(rows, width)

    own_out = row_grad(grad_own)
    own_back = exchange(own_out)
    own_back, grad_mirror = lax.optimization_barrier((own_back, grad_mirror))
    mirror_out = row_grad(grad_mirror)
    mirror_back = exchange(mirror_out)
    my_x, my_lo, my_y = lax.axis_index(X), lax.axis_index(LO), lax.axis_index(Y)
    own_back, mirror_back, grad_own, grad_mirror, gathered, my_x, my_lo, my_y, nil = (
        lax.optimization_barrier(
            (own_back, mirror_back, grad_own, grad_mirror, gathered, my_x, my_lo, my_y, jnp.int32(0))
        )
    )

    per_source = count + spare
    keys = key_table(
        sizes,
        most,
        top,
        count,
        jnp.stack([my_x, my_lo, my_y]).astype(jnp.int32),
        gathered.reshape(n_hi * n_lo, per_source, width),
    )
    spaced = jnp.pad(
        keys[:2].reshape(2, plane, n_lo, count),
        ((0, 0), (0, 0), (0, 0), (0, spare)),
        constant_values=-1,
    ).reshape(2, plane, n_lo * per_source)

    def selector(some):
        slot = (jnp.arange(slots, dtype=jnp.int32) + nil)[None, :, None]
        return (some[:, None, :] == slot).astype(bf16).reshape(-1, some.shape[1])

    per_section = n_lo * per_source
    near_first, near_second = [None] * n_x, [None] * n_y
    for step in (1, 3, 2, 0):
        for key, which, near, axis, size in (
            (spaced[0], 0, near_first, X, n_x),
            (spaced[1], 1, near_second, Y, n_y),
        ):
            some = selector(key[step * (plane // size) : (step + 1) * (plane // size)])
            section = gathered[which * per_section : (which + 1) * per_section]
            sent = dot(some, section, ((1,), (0,))).astype(bf16)
            near[step] = shifted(sent, axis, size, step)

    key_own = jnp.where(low, keys[2], keys[3])
    key_mirror = jnp.where(low, keys[3], keys[2])
    sums_own = dot(selector(key_own), own_back, ((0,), (0,))).astype(bf16)
    sums_mirror = dot(selector(key_mirror), mirror_back, ((0,), (0,))).astype(bf16)
    sums = jnp.concatenate(
        [jnp.where(low, sums_own, sums_mirror), jnp.where(low, sums_mirror, sums_own)]
    )
    token_grad = lax.psum_scatter(
        sums, ring_axes, scatter_dimension=0, axis_index_groups=rings, tiled=True
    )

    grad_first = jnp.where(low, grad_own, grad_mirror)
    grad_second = jnp.where(low, grad_mirror, grad_own)
    late = place + nil
    outer, inner = late // (n_y * slots), (late // slots) % n_y
    order_first = order(late, (my_x - inner) % n_x, (my_y - outer) % n_y).reshape(n_y, -1, rows)
    order_second = order(late, (my_x - outer) % n_x, (my_y - inner) % n_y).reshape(n_x, -1, rows)
    turned_grad = jnp.concatenate(
        [
            jnp.einsum("rf,kcr->kfc", some, by, preferred_element_type=jnp.float32)
            for some, by in ((grad_first, order_first), (grad_second, order_second))
        ]
    ).astype(bf16)

    far_first, far_second = [None] * n_y, [None] * n_x
    for step in (1, 3, 2, 0):
        far_first[step] = shifted(merged(near_first, step, slots), Y, n_y, step)
        far_second[step] = shifted(merged(near_second, step, slots), X, n_x, step)
    weight_grad = hidden_sum(turned_grad, far_first + far_second)
    return (token_grad[None], weight_grad[None, None])


def solution(mesh):
    sizes = (2, 2, 4, 4, 4)
    fine = Mesh(mesh.devices.reshape(sizes), AXES)
    pipe, expert = (HI, CORE), (X, LO, Y)

    def device_body(*args):
        return on_device(sizes, *args)

    return jax.shard_map(
        device_body,
        mesh=fine,
        in_specs=(
            P(pipe, expert, None),
            P(pipe, expert, None),
            P(pipe, expert, None, None),
            P(pipe, expert, None, None, None),
        ),
        out_specs=(P(pipe, expert, None), P(pipe, expert, None, None)),
        check_vma=False,
    )
```

time: 502 us -> 521 us (1.038)
  Pallas kernels: 0 us -> 45.6 us
  waiting for transfers between devices: 354 us -> 327 us
  blocking collectives: 19.3 us -> 0 us
  starting transfers between devices: 40.7 us -> 51.8 us
  other arithmetic: 7.9 us -> 13.9 us
    all_to_all x4 -> x2, waiting for transfers between devices: 313 us -> 136 us  [exchange(): return lax.all_to_all(value, (X, Y), 0, 0, tiled=True).reshape(rows, width)]
    ppermute x0 -> x12, waiting for transfers between devices: none -> 131 us  [shifted(): lax.ppermute(value, axis, [(i, (i + by) % size) for i in range(size)])]
    pallas_call x0 -> x10, Pallas kernels: none -> 45.6 us  [the longest x8 30.1 us: merged(): pl.pallas_call(merge_kernel, out_shape=jax.ShapeDtypeStruct((len(parts) *...]
    ppermute x0 -> x12, starting transfers between devices: none -> 26.2 us  [shifted(): lax.ppermute(value, axis, [(i, (i + by) % size) for i in range(size)])]
    all_gather x1 -> x0, blocking collectives: 19.3 us -> none  [on_device(): lax.all_gather(expert_ids[0].T, ring_axes, axis=0, axis_index_groups=rings)]
    ppermute x1, waiting for transfers between devices: 40.4 us -> 59.5 us  [on_device(): grad_mirror = lax.ppermute(grad_send, AXES, mirror_pairs(sizes))]
    all_to_all x4 -> x2, starting transfers between devices: 34.8 us -> 19.8 us  [exchange(): return lax.all_to_all(value, (X, Y), 0, 0, tiled=True).reshape(rows, width)]
    dot_general x11 -> x12, matrix products: 64 us -> 56.9 us  [dot(): lax.dot_general(a, b, (dims, ((), ())), preferred_element_type=jnp.float32)]
  transfers between devices with their start and end apart: 7 -> 17, of which waited for: 5 -> 9; matrix products, arithmetic and copies ran while one was open for 13% -> 10% of each run, Pallas kernels for 0% -> 9%
where the time goes in v2:
time: 521 us; the launch traced here: 517 us
  waiting for transfers between devices  327 us (63%)
  matrix products  61.6 us (12%)
  starting transfers between devices  51.8 us (10%)
  Pallas kernels  45.6 us (9%)
  between operations  14.3 us (3%)
  other arithmetic  13.9 us (3%)
    all_to_all x2, waiting for transfers between devices, exchange(): return lax.all_to_all(value, (X, Y), 0, 0, tiled=True).reshape(rows, width)  136 us
    ppermute x12, waiting for transfers between devices, shifted(): lax.ppermute(value, axis, [(i, (i + by) % size) for i in range(size)])  131 us
    ppermute x1, waiting for transfers between devices, on_device(): grad_mirror = lax.ppermute(grad_send, AXES, mirror_pairs(sizes))  59.5 us
    dot_general x12, matrix products, dot(): lax.dot_general(a, b, (dims, ((), ())), preferred_element_type=jnp.float32)  56.9 us
    pallas_call x8, Pallas kernels, merged(): pl.pallas_call(merge_kernel, out_shape=jax.ShapeDtypeStruct((len(parts) *...  30.1 us
    ppermute x12, starting transfers between devices, shifted(): lax.ppermute(value, axis, [(i, (i + by) % size) for i in range(size)])  26.2 us
    all_to_all x2, starting transfers between devices, exchange(): return lax.all_to_all(value, (X, Y), 0, 0, tiled=True).reshape(rows, width)  19.8 us
    pallas_call x1, Pallas kernels, hidden_sum(): pl.pallas_call(hidden_sum_kernel, out_shape=jax.ShapeDtypeStruct((width,...  14 us
  transfers between devices with their start and end apart: 17, of which 9 were waited for; matrix products, arithmetic and copies ran while one was open for 10% of the time, Pallas kernels for 9%

profile of v2, /device:TPU:32, one launch (start us, length us, event | category | flops | bytes accessed | tf_op | source)
XLA Modules:
  0.0 517.0 jit_solution(11772132256965699446)
XLA Ops:
  11.3 8.9 %convolution_convert_fusion.1 = bf16[896,3584]{1,0:T(8,128)(2,1)} fusion(bf16[1,1,3584,512]{3,2,1,0:T(8,128)(2,1)} %param.6, bf16[896,512]{1,0:T(8,128)(2,1)S(1)} %get-tuple-element.22, s32[896]{0:T(1024)S(1)} %fusion.48), kind=kOutput, calls=%fused_computation.2 | convolution fusion | flops 4114890752 | bytes 11013632 | tf_op jit(solution)/shard_map/dot_general | solution.py:40
  20.2 7.2 %all-to-all-start = ((bf16[16,56,3584]{2,1,0:T(8,128)(2,1)}), bf16[16,56,3584]{2,1,0:T(8,128)(2,1)}, u32[]{:S(2)}, u32[]{:S(2)}) async-start(bf16[16,56,3584]{2,1,0:T(8,128)(2,1)} %bitcast.75), calls=%async_computation | async-start | bytes 12845056 | tf_op jit(solution)/shard_map/all_to_all | solution.py:181
  27.4 5.5 %collective-permute-start = (bf16[896,512]{1,0:T(8,128)(2,1)S(1)}, bf16[896,512]{1,0:T(8,128)(2,1)S(1)}, u32[]{:S(2)}, u32[]{:S(2)}) collective-permute-start(bf16[896,512]{1,0:T(8,128)(2,1)S(1)} %copy-done.5), channel_id=1, source_target_pairs={{0,192},{1,193},{2,194},{3,195},{4,196},{5,197},{6,198},{7,199},{8... | collective-permute-start | bytes 2752520 | tf_op jit(solution)/shard_map/ppermute | solution.py:161
  33.0 59.5 %collective-permute-done = bf16[896,512]{1,0:T(8,128)(2,1)S(1)} collective-permute-done((bf16[896,512]{1,0:T(8,128)(2,1)S(1)}, bf16[896,512]{1,0:T(8,128)(2,1)S(1)}, u32[]{:S(2)}, u32[]{:S(2)}) %collective-permute-start) | collective-permute-done | bytes 917536 | tf_op jit(solution)/shard_map/ppermute | solution.py:161
  92.5 38.6 %all-to-all-done = bf16[16,56,3584]{2,1,0:T(8,128)(2,1)} async-done(((bf16[16,56,3584]{2,1,0:T(8,128)(2,1)}), bf16[16,56,3584]{2,1,0:T(8,128)(2,1)}, u32[]{:S(2)}, u32[]{:S(2)}) %all-to-all-start) | async-done | bytes 6422560 | tf_op jit(solution)/shard_map/all_to_all | solution.py:181
  131.1 8.6 %convolution_convert_fusion = bf16[896,3584]{1,0:T(8,128)(2,1)} fusion(bf16[1,1,3584,512]{3,2,1,0:T(8,128)(2,1)} %param.6, bf16[896,512]{1,0:T(8,128)(2,1)S(1)} %collective-permute-done, s32[896]{0:T(1024)S(1)} %fusion.48), kind=kOutput, calls=%fused_computation.1 | convolution fusion | flops 4114890752 | bytes 11013632 | tf_op jit(solution)/shard_map/dot_general | solution.py:40
  139.7 12.6 %all-to-all-start.1 = ((bf16[16,56,3584]{2,1,0:T(8,128)(2,1)}), bf16[16,56,3584]{2,1,0:T(8,128)(2,1)}, u32[]{:S(2)}, u32[]{:S(2)}) async-start(bf16[16,56,3584]{2,1,0:T(8,128)(2,1)} %bitcast.74), calls=%async_computation.1 | async-start | bytes 12845056 | tf_op jit(solution)/shard_map/all_to_all | solution.py:181
  152.5 97.6 %all-to-all-done.1 = bf16[16,56,3584]{2,1,0:T(8,128)(2,1)} async-done(((bf16[16,56,3584]{2,1,0:T(8,128)(2,1)}), bf16[16,56,3584]{2,1,0:T(8,128)(2,1)}, u32[]{:S(2)}, u32[]{:S(2)}) %all-to-all-start.1) | async-done | bytes 6422560 | tf_op jit(solution)/shard_map/all_to_all | solution.py:181
  253.7 7.1 %convolution_convert_fusion.2 = bf16[512,3584]{1,0:T(8,128)(2,1)S(1)} fusion(pred[896,512]{1,0:T(32,128)(4,1)S(1)} %get-tuple-element.39, bf16[896,3584]{1,0:T(8,128)(2,1)} %bitcast.9), kind=kOutput, calls=%fused_computation.3 | convolution fusion | flops 3290169344 | bytes 10551296 | tf_op jit(solution)/shard_map/dot_general | solution.py:40
  260.8 8.3 %broadcast_select_fusion.1 = (bf16[512,3584]{1,0:T(8,128)(2,1)S(1)}, bf16[512,3584]{1,0:T(8,128)(2,1)}) fusion(bf16[512,3584]{1,0:T(8,128)(2,1)S(1)} %convolution_convert_fusion.2, pred[]{:T(512)S(6)} %eq.229, pred[896,512]{1,0:T(32,128)(4,1)S(1)} %get-tuple-element.38, bf16[896,3584]{1,0:T(8,128)(2,1)} %bitcast.7), kind=kOutput, calls=%fused_computation.16 | convolution fusion | flops 3293839360 | bytes 17891328 | tf_op jit(solution)/shard_map/dot_general | solution.py:40
  269.1 5.5 %pad_maximum_fusion = bf16[1024,3584]{1,0:T(8,128)(2,1)} fusion(bf16[512,3584]{1,0:T(8,128)(2,1)} %get-tuple-element.25, bf16[512,3584]{1,0:T(8,128)(2,1)S(1)} %get-tuple-element.24), kind=kLoop, calls=%fused_computation | loop fusion | flops 14680064 | bytes 14680064 | tf_op jit(solution)/shard_map/concatenate | solution.py:230
  277.0 3.7 convolution_convert_fusion.10
  280.8 3.7 convolution_convert_fusion.9
  286.1 3.5 collective-permute-start.3
  296.1 6.3 %collective-permute-start.8 = (bf16[224,3584]{1,0:T(8,128)(2,1)}, bf16[224,3584]{1,0:T(8,128)(2,1)}, u32[]{:S(2)}, u32[]{:S(2)}) collective-permute-start(bf16[224,3584]{1,0:T(8,128)(2,1)} %convolution_convert_fusion.5), channel_id=1, source_target_pairs={{0,2},{1,3},{2,0},{3,1},{4,6},{5,7},{6,4},{7,5},{8,10},{9,11},{10,... | collective-permute-start | bytes 4816904 | tf_op jit(solution)/shard_map/ppermute | solution.py:36
  305.0 46.3 %collective-permute-done.1.refs_1_ = bf16[224,3584]{1,0:T(8,128)(2,1)S(1)} collective-permute-done((bf16[224,3584]{1,0:T(8,128)(2,1)S(1)}, bf16[224,3584]{1,0:T(8,128)(2,1)S(1)}, u32[]{:S(2)}, u32[]{:S(2)}) %collective-permute-start.1) | collective-permute-done | bytes 1605664 | tf_op jit(solution)/shard_map/ppermute | solution.py:36
  355.7 3.8 merged.9
  361.0 4.8 convolution_convert_fusion.7.refs_0_
  365.8 3.8 merged.10
  372.4 3.8 merged.11
  376.5 43.0 %collective-permute-done.9.refs_3_ = bf16[224,3584]{1,0:T(8,128)(2,1)} collective-permute-done((bf16[224,3584]{1,0:T(8,128)(2,1)}, bf16[224,3584]{1,0:T(8,128)(2,1)}, u32[]{:S(2)}, u32[]{:S(2)}) %collective-permute-start.9) | collective-permute-done | bytes 1605664 | tf_op jit(solution)/shard_map/ppermute | solution.py:36
  419.5 3.8 merged.13
  423.2 4.9 collective-permute-start.10
  428.1 3.8 merged.14
  434.4 3.7 merged.15
  438.2 3.0 collective-permute-start.12
  448.6 3.8 merged.8.refs_1_
  452.4 3.7 merged.12.refs_5_
  456.1 7.8 %collective-permute-done.10.refs_6_ = bf16[224,3584]{1,0:T(8,128)(2,1)} collective-permute-done((bf16[224,3584]{1,0:T(8,128)(2,1)}, bf16[224,3584]{1,0:T(8,128)(2,1)}, u32[]{:S(2)}, u32[]{:S(2)}) %collective-permute-start.10) | collective-permute-done | bytes 1605664 | tf_op jit(solution)/shard_map/ppermute | solution.py:36
  463.9 28.8 %collective-permute-done.11.refs_7_ = bf16[224,3584]{1,0:T(8,128)(2,1)} collective-permute-done((bf16[224,3584]{1,0:T(8,128)(2,1)}, bf16[224,3584]{1,0:T(8,128)(2,1)}, u32[]{:S(2)}, u32[]{:S(2)}) %collective-permute-start.11) | collective-permute-done | bytes 1605664 | tf_op jit(solution)/shard_map/ppermute | solution.py:36
  492.8 3.5 collective-permute-done.12.refs_8_
  496.2 14.0 %hidden_sum.1 = bf16[3584,512]{1,0:T(8,128)(2,1)} custom-call(bf16[8,512,224]{2,1,0:T(8,128)(2,1)} %pad_maximum_fusion.1.refs_0_, bf16[224,3584]{1,0:T(8,128)(2,1)} %merged.8.refs_1_, bf16[224,3584]{1,0:T(8,128)(2,1)} %copy-done.3, bf16[224,3584]{1,0:T(8,128)(2,1)} %collective-permute-done.5.refs_3_, bf16[224,3584]{1,0:T(8,128)(2,1)} %collective-permute-done.6.refs_4_, ...), custom_call_target="tpu_custom_call" | custom-call | tf_op jit(solution)/shard_map/hidden_sum/pallas_call | solution.py:56
  (78 shorter events, 40.1 us)
Async XLA Ops:
  7.2 3.1 copy-start.2
  7.2 242.9 %all-gather.2.cloned.1.call-start = ((), (), s32[]{:S(2)}) async-start(), calls=%async_computation.3 | async-start | bytes 8773632 | tf_op jit(solution)/shard_map/all_gather | solution.py:165
  11.3 429.8 %copy-start.4 = (bf16[896,512]{1,0:T(8,128)(2,1)}, bf16[896,512]{1,0:T(8,128)(2,1)S(1)}, u32[]{:S(2)}) copy-start(bf16[896,512]{1,0:T(8,128)(2,1)S(1)} %get-tuple-element.22) | copy-start | bytes 2752516
  20.2 7.2 %copy-start.5 = (bf16[896,512]{1,0:T(8,128)(2,1)S(1)}, bf16[896,512]{1,0:T(8,128)(2,1)}, u32[]{:S(2)}) copy-start(bf16[896,512]{1,0:T(8,128)(2,1)} %get-tuple-element.26) | copy-start | bytes 2752516
  20.2 110.9 %all-to-all-start = ((bf16[16,56,3584]{2,1,0:T(8,128)(2,1)}), bf16[16,56,3584]{2,1,0:T(8,128)(2,1)}, u32[]{:S(2)}, u32[]{:S(2)}) async-start(bf16[16,56,3584]{2,1,0:T(8,128)(2,1)} %bitcast.75), calls=%async_computation | async-start | bytes 12845056 | tf_op jit(solution)/shard_map/all_to_all | solution.py:181
  27.4 65.1 %collective-permute-start = (bf16[896,512]{1,0:T(8,128)(2,1)S(1)}, bf16[896,512]{1,0:T(8,128)(2,1)S(1)}, u32[]{:S(2)}, u32[]{:S(2)}) collective-permute-start(bf16[896,512]{1,0:T(8,128)(2,1)S(1)} %copy-done.5), channel_id=1, source_target_pairs={{0,192},{1,193},{2,194},{3,195},{4,196},{5,197},{6,198},{7,199},{8... | collective-permute-start | bytes 2752520 | tf_op jit(solution)/shard_map/ppermute | solution.py:161
  92.5 47.2 %copy-start.6 = (bf16[896,512]{1,0:T(8,128)(2,1)}, bf16[896,512]{1,0:T(8,128)(2,1)S(1)}, u32[]{:S(2)}) copy-start(bf16[896,512]{1,0:T(8,128)(2,1)S(1)} %collective-permute-done) | copy-start | bytes 2752516
  139.7 110.4 %all-to-all-start.1 = ((bf16[16,56,3584]{2,1,0:T(8,128)(2,1)}), bf16[16,56,3584]{2,1,0:T(8,128)(2,1)}, u32[]{:S(2)}, u32[]{:S(2)}) async-start(bf16[16,56,3584]{2,1,0:T(8,128)(2,1)} %bitcast.74), calls=%async_computation.1 | async-start | bytes 12845056 | tf_op jit(solution)/shard_map/all_to_all | solution.py:181
  152.3 357.9 %reduce-scatter.2.cloned.1.call-start = ((), (), s32[]{:S(2)}) async-start(), calls=%async_computation.4 | async-start | bytes 8257536 | tf_op jit(solution)/shard_map/reduce_scatter | solution.py:233
  274.6 0.8 slice-start.2
  277.0 7.6 %slice-start = ((s8[7798784]{0:T(1024)(128)(4,1)}), s8[4194304]{0:T(1024)(128)(4,1)S(1)}, s32[]{:S(2)}) async-start(s8[7798784]{0:T(1024)(128)(4,1)} %bitcast.72), calls=%async_computation.5 | async-start | bytes 8388608
  280.7 70.5 %collective-permute-start.1 = (bf16[224,3584]{1,0:T(8,128)(2,1)S(1)}, bf16[224,3584]{1,0:T(8,128)(2,1)S(1)}, u32[]{:S(2)}, u32[]{:S(2)}) collective-permute-start(bf16[224,3584]{1,0:T(8,128)(2,1)S(1)} %convolution_convert_fusion.10), channel_id=1, source_target_pairs={{0,16},{16,32},{32,48},{48,0},{1,17},{17,33},{33,49},{49,1},{2,18}... | collective-permute-start | bytes 4816904 | tf_op jit(solution)/shard_map/ppermute | solution.py:36
  280.8 3.8 slice-start.1
  284.5 69.4 %collective-permute-start.2 = (bf16[224,3584]{1,0:T(8,128)(2,1)S(1)}, bf16[224,3584]{1,0:T(8,128)(2,1)S(1)}, u32[]{:S(2)}, u32[]{:S(2)}) collective-permute-start(bf16[224,3584]{1,0:T(8,128)(2,1)S(1)} %convolution_convert_fusion.9), channel_id=1, source_target_pairs={{0,32},{16,48},{32,0},{48,16},{1,33},{17,49},{33,1},{49,17},{2,34}... | collective-permute-start | bytes 4816904 | tf_op jit(solution)/shard_map/ppermute | solution.py:36
  286.1 69.7 %collective-permute-start.3 = (bf16[224,3584]{1,0:T(8,128)(2,1)S(1)}, bf16[224,3584]{1,0:T(8,128)(2,1)}, u32[]{:S(2)}, u32[]{:S(2)}) collective-permute-start(bf16[224,3584]{1,0:T(8,128)(2,1)S(1)} %convolution_convert_fusion.8), channel_id=1, source_target_pairs={{0,48},{16,0},{32,16},{48,32},{1,49},{17,1},{33,17},{49,33},{2,50}... | collective-permute-start | bytes 4816904 | tf_op jit(solution)/shard_map/ppermute | solution.py:36
  292.2 84.0 %collective-permute-start.7 = (bf16[224,3584]{1,0:T(8,128)(2,1)}, bf16[224,3584]{1,0:T(8,128)(2,1)}, u32[]{:S(2)}, u32[]{:S(2)}) collective-permute-start(bf16[224,3584]{1,0:T(8,128)(2,1)} %convolution_convert_fusion.6), channel_id=1, source_target_pairs={{0,1},{1,2},{2,3},{3,0},{4,5},{5,6},{6,7},{7,4},{8,9},{9,10},{10,1... | collective-permute-start | bytes 4816904 | tf_op jit(solution)/shard_map/ppermute | solution.py:36
  296.1 80.4 %collective-permute-start.8 = (bf16[224,3584]{1,0:T(8,128)(2,1)}, bf16[224,3584]{1,0:T(8,128)(2,1)}, u32[]{:S(2)}, u32[]{:S(2)}) collective-permute-start(bf16[224,3584]{1,0:T(8,128)(2,1)} %convolution_convert_fusion.5), channel_id=1, source_target_pairs={{0,2},{1,3},{2,0},{3,1},{4,6},{5,7},{6,4},{7,5},{8,10},{9,11},{10,... | collective-permute-start | bytes 4816904 | tf_op jit(solution)/shard_map/ppermute | solution.py:36
  351.2 2.6 copy-start
  351.2 68.2 %collective-permute-start.9 = (bf16[224,3584]{1,0:T(8,128)(2,1)}, bf16[224,3584]{1,0:T(8,128)(2,1)}, u32[]{:S(2)}, u32[]{:S(2)}) collective-permute-start(bf16[224,3584]{1,0:T(8,128)(2,1)} %convolution_convert_fusion.4), channel_id=1, source_target_pairs={{0,3},{1,0},{2,1},{3,2},{4,7},{5,4},{6,5},{7,6},{8,11},{9,8},{10,9... | collective-permute-start | bytes 4816904 | tf_op jit(solution)/shard_map/ppermute | solution.py:36
  353.9 1.9 copy-start.1
  359.6 78.6 %collective-permute-start.4 = (bf16[224,3584]{1,0:T(8,128)(2,1)}, bf16[224,3584]{1,0:T(8,128)(2,1)S(1)}, u32[]{:S(2)}, u32[]{:S(2)}) collective-permute-start(bf16[224,3584]{1,0:T(8,128)(2,1)} %merged.9), channel_id=1, source_target_pairs={{0,1},{1,2},{2,3},{3,0},{4,5},{5,6},{6,7},{7,4},{8,9},{9,10},{10,1... | collective-permute-start | bytes 4816904 | tf_op jit(solution)/shard_map/ppermute | solution.py:36
  369.6 86.6 %collective-permute-start.5 = (bf16[224,3584]{1,0:T(8,128)(2,1)}, bf16[224,3584]{1,0:T(8,128)(2,1)}, u32[]{:S(2)}, u32[]{:S(2)}) collective-permute-start(bf16[224,3584]{1,0:T(8,128)(2,1)} %merged.10), channel_id=1, source_target_pairs={{0,2},{1,3},{2,0},{3,1},{4,6},{5,7},{6,4},{7,5},{8,10},{9,11},{10,... | collective-permute-start | bytes 4816904 | tf_op jit(solution)/shard_map/ppermute | solution.py:36
  376.2 80.0 %collective-permute-start.6 = (bf16[224,3584]{1,0:T(8,128)(2,1)}, bf16[224,3584]{1,0:T(8,128)(2,1)}, u32[]{:S(2)}, u32[]{:S(2)}) collective-permute-start(bf16[224,3584]{1,0:T(8,128)(2,1)} %merged.11), channel_id=1, source_target_pairs={{0,3},{1,0},{2,1},{3,2},{4,7},{5,4},{6,5},{7,6},{8,11},{9,8},{10,9... | collective-permute-start | bytes 4816904 | tf_op jit(solution)/shard_map/ppermute | solution.py:36
  423.2 40.7 %collective-permute-start.10 = (bf16[224,3584]{1,0:T(8,128)(2,1)}, bf16[224,3584]{1,0:T(8,128)(2,1)}, u32[]{:S(2)}, u32[]{:S(2)}) collective-permute-start(bf16[224,3584]{1,0:T(8,128)(2,1)} %merged.13), channel_id=1, source_target_pairs={{0,16},{16,32},{32,48},{48,0},{1,17},{17,33},{33,49},{49,1},{2,18}... | collective-permute-start | bytes 4816904 | tf_op jit(solution)/shard_map/ppermute | solution.py:36
  431.9 60.9 %collective-permute-start.11 = (bf16[224,3584]{1,0:T(8,128)(2,1)}, bf16[224,3584]{1,0:T(8,128)(2,1)}, u32[]{:S(2)}, u32[]{:S(2)}) collective-permute-start(bf16[224,3584]{1,0:T(8,128)(2,1)} %merged.14), channel_id=1, source_target_pairs={{0,32},{16,48},{32,0},{48,16},{1,33},{17,49},{33,1},{49,17},{2,34}... | collective-permute-start | bytes 4816904 | tf_op jit(solution)/shard_map/ppermute | solution.py:36
  438.1 3.0 copy-start.3
  438.2 58.1 %collective-permute-start.12 = (bf16[224,3584]{1,0:T(8,128)(2,1)}, bf16[224,3584]{1,0:T(8,128)(2,1)}, u32[]{:S(2)}, u32[]{:S(2)}) collective-permute-start(bf16[224,3584]{1,0:T(8,128)(2,1)} %merged.15), channel_id=1, source_target_pairs={{0,48},{16,0},{32,16},{48,32},{1,49},{17,1},{33,17},{49,33},{2,50}... | collective-permute-start | bytes 4816904 | tf_op jit(solution)/shard_map/ppermute | solution.py:36
Sparse Core Ops, SparseCore 0:
  10.4 128.6 all-gather.1
  274.8 87.7 reduce-scatter.1

commit v3 on v2

--- a/solution.py
+++ b/solution.py
@@ -40,46 +40,84 @@
     return lax.dot_general(a, b, (dims, ((), ())), preferred_element_type=jnp.float32)
 
 
-def hidden_sum_kernel(*refs):
-    grads, out = refs[0], refs[-1]
-    total = None
-    for i, piece in enumerate(refs[1:-1]):
-        part = jnp.dot(grads[i], piece[...], preferred_element_type=jnp.float32)
-        total = part if total is None else total + part
+def hidden_sum_kernel(tile, *refs):
+    grads, pieces, out, block, arrived = refs[0], refs[1:-3], refs[-3], refs[-2], refs[-1]
+    step, steps = pl.program_id(0), pl.num_programs(0)
+    depth = pieces[0].shape[0]
+
+    def copies(at, slot):
+        columns = pl.ds(pl.multiple_of(at * tile, tile), tile)
+        return [
+            pltpu.make_async_copy(
+                piece.at[:, columns],
+                block.at[slot, i * depth : (i + 1) * depth],
+                arrived.at[slot, i],
+            )
+            for i, piece in enumerate(pieces)
+        ]
+
+    @pl.when(step == 0)
+    def _():
+        for copy in copies(0, 0):
+            copy.start()
+
+    @pl.when(step + 1 < steps)
+    def _():
+        for copy in copies(step + 1, (step + 1) % 2):
+            copy.start()
+
+    for copy in copies(step, step % 2):
+        copy.wait()
+    total = jnp.dot(grads[...], block[step % 2], preferred_element_type=jnp.float32)
     out[...] = total.T.astype(out.dtype)
 
 
 def hidden_sum(grads, pieces):
-    count, half, depth = grads.shape
-    width = pieces[0].shape[1]
+    half, rows = grads.shape
+    _, width = pieces[0].shape
     tile = 512 if width % 512 == 0 else width
     return pl.pallas_call(
-        hidden_sum_kernel,
+        functools.partial(hidden_sum_kernel, tile),
         out_shape=jax.ShapeDtypeStruct((width, half), jnp.bfloat16),
         grid=(width // tile,),
-        in_specs=[pl.BlockSpec((count, half, depth), lambda i: (0, 0, 0))]
-        + [pl.BlockSpec((depth, tile), lambda i: (0, i))] * count,
+        in_specs=[pl.BlockSpec((half, rows), lambda i: (0, 0))]
+        + [pl.BlockSpec(memory_space=pl.ANY)] * len(pieces),
         out_specs=pl.BlockSpec((tile, half), lambda i: (i, 0)),
+        scratch_shapes=[
+            pltpu.VMEM((2, rows, tile), jnp.bfloat16),
+            pltpu.SemaphoreType.DMA((2, len(pieces))),
+        ],
         name="hidden_sum",
     )(grads, *pieces)
 
 
-def merge_kernel(*refs):
-    out = refs[-1]
-    size = refs[0].shape[0]
-    for i, piece in enumerate(refs[:-1]):
-        out[i * size : (i + 1) * size, :] = piece[...]
-
-
-def merged(parts, step, size):
-    width = parts[0].shape[1]
-    tile = 896 if width % 896 == 0 else width
+def merge_kernel(size, *refs):
+    count = (len(refs) - 1) // 2
+    parts, outs, arrived = refs[:count], refs[count:-1], refs[-1]
+    copies = []
+    for step in range(len(outs)):
+        for i, part in enumerate(parts):
+            copies.append(
+                pltpu.make_async_copy(
+                    part.at[step * size : (step + 1) * size],
+                    outs[step].at[i * size : (i + 1) * size],
+                    arrived.at[step, i],
+                )
+            )
+    for copy in copies:
+        copy.start()
+    for copy in copies:
+        copy.wait()
+
+
+def merged(parts, size):
+    count = len(parts)
     return pl.pallas_call(
-        merge_kernel,
-        out_shape=jax.ShapeDtypeStruct((len(parts) * size, width), parts[0].dtype),
-        grid=(width // tile,),
-        in_specs=[pl.BlockSpec((size, tile), lambda i: (step, i))] * len(parts),
-        out_specs=pl.BlockSpec((len(parts) * size, tile), lambda i: (0, i)),
+        functools.partial(merge_kernel, size),
+        out_shape=[jax.ShapeDtypeStruct(parts[0].shape, parts[0].dtype)] * count,
+        in_specs=[pl.BlockSpec(memory_space=pl.ANY)] * count,
+        out_specs=[pl.BlockSpec(memory_space=pl.ANY)] * count,
+        scratch_shapes=[pltpu.SemaphoreType.DMA((count, count))],
         name="merged",
     )(*parts)
 
@@ -156,6 +194,12 @@
     spare = 8
 
     grad = jnp.transpose(up_grad[0, 0], (1, 0, 2)).reshape(rows, 2 * half)
+    place = jnp.arange(rows, dtype=jnp.int32)
+    at_x, at_y = place // (n_y * slots), (place // slots) % n_y
+    at_lo, at_slot = (place // most) % n_lo, place % most
+    taken = at_slot * sources + (at_x * n_lo + at_lo) * n_y + at_y
+    by_place = (taken[:, None] == place[None, :]).astype(bf16)
+    grad = lax.optimization_barrier(dot(by_place, grad, ((1,), (0,))).astype(bf16))
     grad_own = jnp.where(low, grad[:, :half], grad[:, half:])
     grad_send = jnp.where(low, grad[:, half:], grad[:, :half])
     grad_mirror = lax.ppermute(grad_send, AXES, mirror_pairs(sizes))
@@ -164,28 +208,17 @@
     outgoing = jnp.concatenate([token_rows, id_rows])
     gathered = lax.all_gather(outgoing, ring_axes, axis=0, axis_index_groups=rings, tiled=True)
 
-    def order(place, at_x, at_y):
-        at_lo, at_slot = (place // most) % n_lo, place % most
-        taken = at_slot * sources + (at_x * n_lo + at_lo) * n_y + at_y
-        return (taken[:, None] == place[None, :]).astype(bf16)
-
-    place = jnp.arange(rows, dtype=jnp.int32)
-    by_place = order(place, place // (n_y * slots), (place // slots) % n_y)
-
-    def row_grad(grads):
-        sorted_rows = dot(by_place, grads, ((1,), (0,))).astype(bf16)
-        return dot(sorted_rows, weight, ((1,), (1,))).astype(bf16)
-
     def exchange(value):
         value = value.reshape(plane, slots, width)
         return lax.all_to_all(value, (X, Y), 0, 0, tiled=True).reshape(rows, width)
 
-    own_out = row_grad(grad_own)
+    my_x, my_lo, my_y = lax.axis_index(X), lax.axis_index(LO), lax.axis_index(Y)
+    own_out = dot(grad_own, weight, ((1,), (1,))).astype(bf16)
+    own_out, my_x, my_lo, my_y = lax.optimization_barrier((own_out, my_x, my_lo, my_y))
     own_back = exchange(own_out)
     own_back, grad_mirror = lax.optimization_barrier((own_back, grad_mirror))
-    mirror_out = row_grad(grad_mirror)
+    mirror_out = dot(grad_mirror, weight, ((1,), (1,))).astype(bf16)
     mirror_back = exchange(mirror_out)
-    my_x, my_lo, my_y = lax.axis_index(X), lax.axis_index(LO), lax.axis_index(Y)
     own_back, mirror_back, grad_own, grad_mirror, gathered, my_x, my_lo, my_y, nil = (
         lax.optimization_barrier(
             (own_back, mirror_back, grad_own, grad_mirror, gathered, my_x, my_lo, my_y, jnp.int32(0))
@@ -234,23 +267,24 @@
         sums, ring_axes, scatter_dimension=0, axis_index_groups=rings, tiled=True
     )
 
-    grad_first = jnp.where(low, grad_own, grad_mirror)
-    grad_second = jnp.where(low, grad_mirror, grad_own)
+    far_first, far_second = [None] * n_y, [None] * n_x
+    turned_first = merged(near_first, slots)
+    turned_second = merged(near_second, slots)
+    for step in (1, 3, 2, 0):
+        far_first[step] = shifted(turned_first[step], Y, n_y, step)
+        far_second[step] = shifted(turned_second[step], X, n_x, step)
+
     late = place + nil
-    outer, inner = late // (n_y * slots), (late // slots) % n_y
-    order_first = order(late, (my_x - inner) % n_x, (my_y - outer) % n_y).reshape(n_y, -1, rows)
-    order_second = order(late, (my_x - outer) % n_x, (my_y - inner) % n_y).reshape(n_x, -1, rows)
-    turned_grad = jnp.concatenate(
-        [
-            jnp.einsum("rf,kcr->kfc", some, by, preferred_element_type=jnp.float32)
-            for some, by in ((grad_first, order_first), (grad_second, order_second))
-        ]
-    ).astype(bf16)
-
-    far_first, far_second = [None] * n_y, [None] * n_x
-    for step in (1, 3, 2, 0):
-        far_first[step] = shifted(merged(near_first, step, slots), Y, n_y, step)
-        far_second[step] = shifted(merged(near_second, step, slots), X, n_x, step)
+    outer, inner, rest = late // (n_y * slots), (late // slots) % n_y, late % slots
+    turned_grad = []
+    for some, row_x, row_y in (
+        (jnp.where(low, grad_own, grad_mirror), my_x - inner, my_y - outer),
+        (jnp.where(low, grad_mirror, grad_own), my_x - outer, my_y - inner),
+    ):
+        row = ((row_x % n_x) * n_y + row_y % n_y) * slots + rest
+        order = (place[:, None] == row[None, :]).astype(bf16)
+        turned_grad.append(dot(some, order, ((0,), (0,))).astype(bf16))
+    turned_grad = jnp.concatenate(turned_grad, axis=1)
     weight_grad = hidden_sum(turned_grad, far_first + far_second)
     return (token_grad[None], weight_grad[None, None])
 

time: 521 us -> 827 us (1.59)
  Pallas kernels: 45.6 us -> 407 us
  waiting for transfers between devices: 327 us -> 209 us
  blocking collectives: 0 us -> 85.9 us
  starting transfers between devices: 51.8 us -> 31.3 us
    pallas_call x9 -> x3, Pallas kernels: 44.1 us -> 406 us  [the longest x2 392 us: merged(): pl.pallas_call(functools.partial(merge_kernel, size), out_shape=[jax.Shap...]
    all_to_all x2 -> x1, waiting for transfers between devices: 136 us -> 38.2 us  [exchange(): return lax.all_to_all(value, (X, Y), 0, 0, tiled=True).reshape(rows, width)]
    all_to_all x0 -> x1, blocking collectives: none -> 85.9 us  [exchange(): return lax.all_to_all(value, (X, Y), 0, 0, tiled=True).reshape(rows, width)]
    ppermute x12, waiting for transfers between devices: 131 us -> 111 us  [shifted(): lax.ppermute(value, axis, [(i, (i + by) % size) for i in range(size)])]
    all_to_all x2 -> x1, starting transfers between devices: 19.8 us -> 7.09 us  [exchange(): return lax.all_to_all(value, (X, Y), 0, 0, tiled=True).reshape(rows, width)]
    dot_general x12 -> x15, matrix products: 56.9 us -> 58.4 us  [dot(): lax.dot_general(a, b, (dims, ((), ())), preferred_element_type=jnp.float32)]
  transfers between devices with their start and end apart: 17 -> 16, of which waited for: 9 -> 5; matrix products, arithmetic and copies ran while one was open for 10% -> 6% of each run, Pallas kernels for 9% -> 49%
where the time goes in v3:
time: 827 us; the launch traced here: 825 us
  Pallas kernels  407 us (49%)
  waiting for transfers between devices  209 us (25%)
  blocking collectives  85.9 us (10%)
  matrix products  58.4 us (7%)
  starting transfers between devices  31.3 us (4%)
  other arithmetic  15.4 us (2%)
  between operations  14.3 us (2%)
    pallas_call x2, Pallas kernels, merged(): pl.pallas_call(functools.partial(merge_kernel, size), out_shape=[jax.Shap...  392 us
    ppermute x12, waiting for transfers between devices, shifted(): lax.ppermute(value, axis, [(i, (i + by) % size) for i in range(size)])  111 us
    all_to_all x1, blocking collectives, exchange(): return lax.all_to_all(value, (X, Y), 0, 0, tiled=True).reshape(rows, width)  85.9 us
    ppermute x1, waiting for transfers between devices, on_device(): grad_mirror = lax.ppermute(grad_send, AXES, mirror_pairs(sizes))  59.6 us
    dot_general x15, matrix products, dot(): lax.dot_general(a, b, (dims, ((), ())), preferred_element_type=jnp.float32)  58.4 us
    all_to_all x1, waiting for transfers between devices, exchange(): return lax.all_to_all(value, (X, Y), 0, 0, tiled=True).reshape(rows, width)  38.2 us
    ppermute x12, starting transfers between devices, shifted(): lax.ppermute(value, axis, [(i, (i + by) % size) for i in range(size)])  18.6 us
  transfers between devices with their start and end apart: 16, of which 5 were waited for; matrix products, arithmetic and copies ran while one was open for 6% of the time, Pallas kernels for 49%

profile of v3, /device:TPU:32, one launch (start us, length us, event | category | flops | bytes accessed | tf_op | source)
XLA Modules:
  0.0 825.4 jit_solution(3804761360545113862)
XLA Ops:
  8.0 2.2 fusion.20
  10.3 3.3 fusion.14
  13.7 1.7 broadcast_select_fusion.2
  16.2 5.4 convolution_convert_fusion.1
  21.7 7.1 all-to-all-start
  28.8 5.5 collective-permute-start
  34.4 59.6 %collective-permute-done = bf16[896,512]{1,0:T(8,128)(2,1)S(1)} collective-permute-done((bf16[896,512]{1,0:T(8,128)(2,1)S(1)}, bf16[896,512]{1,0:T(8,128)(2,1)S(1)}, u32[]{:S(2)}, u32[]{:S(2)}) %collective-permute-start) | collective-permute-done | bytes 917536 | tf_op jit(solution)/shard_map/ppermute | solution.py:205
  93.9 38.2 %all-to-all-done = bf16[16,56,3584]{2,1,0:T(8,128)(2,1)} async-done(((bf16[16,56,3584]{2,1,0:T(8,128)(2,1)}), bf16[16,56,3584]{2,1,0:T(8,128)(2,1)}, u32[]{:S(2)}, u32[]{:S(2)}) %all-to-all-start) | async-done | bytes 6422560 | tf_op jit(solution)/shard_map/all_to_all | solution.py:213
  132.1 5.8 convolution_convert_fusion
  137.9 85.9 %all_to_all.10 = bf16[16,56,3584]{2,1,0:T(8,128)(2,1)} all-to-all(bf16[16,56,3584]{2,1,0:T(8,128)(2,1)S(1)} %bitcast.70), channel_id=1, replica_groups=mesh['hi'=2,'core'=2,'x'=4,'lo'=4,'y'=4] {'x','y'}, dimensions={0} | all-to-all | bytes 12845056 | tf_op jit(solution)/shard_map/all_to_all | solution.py:213
  227.4 7.1 convolution_convert_fusion.2
  234.5 9.0 %broadcast_select_fusion.1 = (bf16[512,3584]{1,0:T(8,128)(2,1)}, bf16[512,3584]{1,0:T(8,128)(2,1)}) fusion(bf16[512,3584]{1,0:T(8,128)(2,1)S(1)} %convolution_convert_fusion.2, pred[]{:T(512)S(6)} %eq.220, pred[896,512]{1,0:T(32,128)(4,1)S(1)} %get-tuple-element.62, bf16[896,3584]{1,0:T(8,128)(2,1)} %bitcast.5), kind=kOutput, calls=%fused_computation.16 | convolution fusion | flops 3293839360 | bytes 17891328 | tf_op jit(solution)/shard_map/dot_general | solution.py:40
  243.5 6.6 pad_maximum_fusion
  252.5 3.7 convolution_convert_fusion.10
  257.0 3.7 convolution_convert_fusion.9
  260.6 2.0 collective-permute-start.2
  264.1 1.7 collective-permute-start.3
  265.9 2.7 convolution_convert_fusion.6
  269.0 2.7 convolution_convert_fusion.5
  271.7 2.1 collective-permute-start.8
  273.8 2.6 convolution_convert_fusion.4
  276.4 49.8 %collective-permute-done.1.refs_1_ = bf16[224,3584]{1,0:T(8,128)(2,1)S(1)} collective-permute-done((bf16[224,3584]{1,0:T(8,128)(2,1)S(1)}, bf16[224,3584]{1,0:T(8,128)(2,1)S(1)}, u32[]{:S(2)}, u32[]{:S(2)}) %collective-permute-start.1) | collective-permute-done | bytes 1605664 | tf_op jit(solution)/shard_map/ppermute | solution.py:36
  327.5 2.6 convolution_convert_fusion.11.refs_0_
  331.2 195.8 %merged.2 = (bf16[224,3584]{1,0:T(8,128)(2,1)}, bf16[224,3584]{1,0:T(8,128)(2,1)}, bf16[224,3584]{1,0:T(8,128)(2,1)}, bf16[224,3584]{1,0:T(8,128)(2,1)}) custom-call(bf16[224,3584]{1,0:T(8,128)(2,1)} %convolution_convert_fusion.11.refs_0_, bf16[224,3584]{1,0:T(8,128)(2,1)} %copy-done.4, bf16[224,3584]{1,0:T(8,128)(2,1)} %copy-done.5, ...), custom_call_target="tpu_custom_call" | custom-call | tf_op jit(solution)/shard_map/merged/pallas_call | solution.py:115
  527.9 4.7 convolution_convert_fusion.7.refs_0_
  535.6 195.8 %merged.3 = (bf16[224,3584]{1,0:T(8,128)(2,1)}, bf16[224,3584]{1,0:T(8,128)(2,1)}, bf16[224,3584]{1,0:T(8,128)(2,1)}, bf16[224,3584]{1,0:T(8,128)(2,1)}) custom-call(bf16[224,3584]{1,0:T(8,128)(2,1)} %convolution_convert_fusion.7.refs_0_, bf16[224,3584]{1,0:T(8,128)(2,1)} %copy-done.3, bf16[224,3584]{1,0:T(8,128)(2,1)} %collective-permute-done.8.refs_2_, ...), custom_call_target="tpu_custom_call" | custom-call | tf_op jit(solution)/shard_map/merged/pallas_call | solution.py:115
  731.4 3.1 collective-permute-start.10
  735.6 2.2 collective-permute-start.12
  737.8 2.5 fusion.18
  743.1 27.3 %collective-permute-done.10.refs_6_ = bf16[224,3584]{1,0:T(8,128)(2,1)} collective-permute-done((bf16[224,3584]{1,0:T(8,128)(2,1)}, bf16[224,3584]{1,0:T(8,128)(2,1)}, u32[]{:S(2)}, u32[]{:S(2)}) %collective-permute-start.10) | collective-permute-done | bytes 1605664 | tf_op jit(solution)/shard_map/ppermute | solution.py:36
  770.3 34.1 %collective-permute-done.11.refs_7_ = bf16[224,3584]{1,0:T(8,128)(2,1)} collective-permute-done((bf16[224,3584]{1,0:T(8,128)(2,1)}, bf16[224,3584]{1,0:T(8,128)(2,1)}, u32[]{:S(2)}, u32[]{:S(2)}) %collective-permute-start.11) | collective-permute-done | bytes 1605664 | tf_op jit(solution)/shard_map/ppermute | solution.py:36
  804.4 14.1 %hidden_sum.1 = bf16[3584,512]{1,0:T(8,128)(2,1)} custom-call(bf16[512,1792]{1,0:T(8,128)(2,1)} %pad_maximum_fusion.1.refs_0_, bf16[224,3584]{1,0:T(8,128)(2,1)} %get-tuple-element.40.refs_1_, bf16[224,3584]{1,0:T(8,128)(2,1)} %copy-done.2, bf16[224,3584]{1,0:T(8,128)(2,1)} %collective-permute-done.5.refs_3_, ...), custom_call_target="tpu_custom_call" | custom-call | tf_op jit(solution)/shard_map/hidden_sum/pallas_call | solution.py:79
  (77 shorter events, 20.5 us)
Async XLA Ops:
  7.2 3.1 copy-start
  7.2 216.6 %all-gather.2.cloned.1.call-start = ((), (), s32[]{:S(2)}) async-start(), calls=%async_computation.3 | async-start | bytes 8773632 | tf_op jit(solution)/shard_map/all_gather | solution.py:209
  13.6 2.6 copy-start.8
  15.4 6.3 copy-start.6
  21.7 110.4 %all-to-all-start = ((bf16[16,56,3584]{2,1,0:T(8,128)(2,1)}), bf16[16,56,3584]{2,1,0:T(8,128)(2,1)}, u32[]{:S(2)}, u32[]{:S(2)}) async-start(bf16[16,56,3584]{2,1,0:T(8,128)(2,1)} %bitcast.69), calls=%async_computation | async-start | bytes 12845056 | tf_op jit(solution)/shard_map/all_to_all | solution.py:213
  28.8 789.8 %reduce-scatter.2.cloned.1.call-start = ((), (), s32[]{:S(2)}) async-start(), calls=%async_computation.4 | async-start | bytes 8257536 | tf_op jit(solution)/shard_map/reduce_scatter | solution.py:266
  28.8 65.1 %collective-permute-start = (bf16[896,512]{1,0:T(8,128)(2,1)S(1)}, bf16[896,512]{1,0:T(8,128)(2,1)S(1)}, u32[]{:S(2)}, u32[]{:S(2)}) collective-permute-start(bf16[896,512]{1,0:T(8,128)(2,1)S(1)} %get-tuple-element.50), channel_id=1, source_target_pairs={{0,192},{1,193},{2,194},{3,195},{4,196},{5,197},{6,198},{7,199},{8... | collective-permute-start | bytes 2752520 | tf_op jit(solution)/shard_map/ppermute | solution.py:205
  93.9 44.0 %copy-start.9 = (bf16[896,512]{1,0:T(8,128)(2,1)}, bf16[896,512]{1,0:T(8,128)(2,1)S(1)}, u32[]{:S(2)}) copy-start(bf16[896,512]{1,0:T(8,128)(2,1)S(1)} %collective-permute-done) | copy-start | bytes 2752516
  250.1 0.8 slice-start.2
  252.5 10.2 %slice-start = ((s8[7798784]{0:T(1024)(128)(4,1)}), s8[4194304]{0:T(1024)(128)(4,1)S(1)}, s32[]{:S(2)}) async-start(s8[7798784]{0:T(1024)(128)(4,1)} %bitcast.66), calls=%async_computation.5 | async-start | bytes 8388608
  256.2 70.0 %collective-permute-start.1 = (bf16[224,3584]{1,0:T(8,128)(2,1)S(1)}, bf16[224,3584]{1,0:T(8,128)(2,1)S(1)}, u32[]{:S(2)}, u32[]{:S(2)}) collective-permute-start(bf16[224,3584]{1,0:T(8,128)(2,1)S(1)} %convolution_convert_fusion.10), channel_id=1, source_target_pairs={{0,16},{16,32},{32,48},{48,0},{1,17},{17,33},{33,49},{49,1},{2,18}... | collective-permute-start | bytes 4816904 | tf_op jit(solution)/shard_map/ppermute | solution.py:36
  257.0 5.7 slice-start.1
  260.6 69.4 %collective-permute-start.2 = (bf16[224,3584]{1,0:T(8,128)(2,1)S(1)}, bf16[224,3584]{1,0:T(8,128)(2,1)S(1)}, u32[]{:S(2)}, u32[]{:S(2)}) collective-permute-start(bf16[224,3584]{1,0:T(8,128)(2,1)S(1)} %convolution_convert_fusion.9), channel_id=1, source_target_pairs={{0,32},{16,48},{32,0},{48,16},{1,33},{17,49},{33,1},{49,17},{2,34}... | collective-permute-start | bytes 4816904 | tf_op jit(solution)/shard_map/ppermute | solution.py:36
  264.1 67.1 %collective-permute-start.3 = (bf16[224,3584]{1,0:T(8,128)(2,1)S(1)}, bf16[224,3584]{1,0:T(8,128)(2,1)}, u32[]{:S(2)}, u32[]{:S(2)}) collective-permute-start(bf16[224,3584]{1,0:T(8,128)(2,1)S(1)} %convolution_convert_fusion.8), channel_id=1, source_target_pairs={{0,48},{16,0},{32,16},{48,32},{1,49},{17,1},{33,17},{49,33},{2,50}... | collective-permute-start | bytes 4816904 | tf_op jit(solution)/shard_map/ppermute | solution.py:36
  268.5 265.4 %collective-permute-start.7 = (bf16[224,3584]{1,0:T(8,128)(2,1)}, bf16[224,3584]{1,0:T(8,128)(2,1)S(1)}, u32[]{:S(2)}, u32[]{:S(2)}) collective-permute-start(bf16[224,3584]{1,0:T(8,128)(2,1)} %convolution_convert_fusion.6), channel_id=1, source_target_pairs={{0,1},{1,2},{2,3},{3,0},{4,5},{5,6},{6,7},{7,4},{8,9},{9,10},{10,1... | collective-permute-start | bytes 4816904 | tf_op jit(solution)/shard_map/ppermute | solution.py:36
  271.7 263.9 %collective-permute-start.8 = (bf16[224,3584]{1,0:T(8,128)(2,1)}, bf16[224,3584]{1,0:T(8,128)(2,1)}, u32[]{:S(2)}, u32[]{:S(2)}) collective-permute-start(bf16[224,3584]{1,0:T(8,128)(2,1)} %convolution_convert_fusion.5), channel_id=1, source_target_pairs={{0,2},{1,3},{2,0},{3,1},{4,6},{5,7},{6,4},{7,5},{8,10},{9,11},{10,... | collective-permute-start | bytes 4816904 | tf_op jit(solution)/shard_map/ppermute | solution.py:36
  326.2 3.8 copy-start.4
  326.2 209.3 %collective-permute-start.9 = (bf16[224,3584]{1,0:T(8,128)(2,1)}, bf16[224,3584]{1,0:T(8,128)(2,1)}, u32[]{:S(2)}, u32[]{:S(2)}) collective-permute-start(bf16[224,3584]{1,0:T(8,128)(2,1)} %convolution_convert_fusion.4), channel_id=1, source_target_pairs={{0,3},{1,0},{2,1},{3,2},{4,7},{5,4},{6,5},{7,6},{8,11},{9,8},{10,9... | collective-permute-start | bytes 4816904 | tf_op jit(solution)/shard_map/ppermute | solution.py:36
  330.1 1.2 copy-start.5
  527.0 208.5 %collective-permute-start.4 = (bf16[224,3584]{1,0:T(8,128)(2,1)}, bf16[224,3584]{1,0:T(8,128)(2,1)S(1)}, u32[]{:S(2)}, u32[]{:S(2)}) collective-permute-start(bf16[224,3584]{1,0:T(8,128)(2,1)} %get-tuple-element.41), channel_id=1, source_target_pairs={{0,1},{1,2},{2,3},{3,0},{4,5},{5,6},{6,7},{7,4},{8,9},{9,10},{10,1... | collective-permute-start | bytes 4816904 | tf_op jit(solution)/shard_map/ppermute | solution.py:36
  532.6 210.5 %collective-permute-start.5 = (bf16[224,3584]{1,0:T(8,128)(2,1)}, bf16[224,3584]{1,0:T(8,128)(2,1)}, u32[]{:S(2)}, u32[]{:S(2)}) collective-permute-start(bf16[224,3584]{1,0:T(8,128)(2,1)} %get-tuple-element.42), channel_id=1, source_target_pairs={{0,2},{1,3},{2,0},{3,1},{4,6},{5,7},{6,4},{7,5},{8,10},{9,11},{10,... | collective-permute-start | bytes 4816904 | tf_op jit(solution)/shard_map/ppermute | solution.py:36
  534.0 1.6 copy-start.3
  534.0 209.1 %collective-permute-start.6 = (bf16[224,3584]{1,0:T(8,128)(2,1)}, bf16[224,3584]{1,0:T(8,128)(2,1)}, u32[]{:S(2)}, u32[]{:S(2)}) collective-permute-start(bf16[224,3584]{1,0:T(8,128)(2,1)} %get-tuple-element.43), channel_id=1, source_target_pairs={{0,3},{1,0},{2,1},{3,2},{4,7},{5,4},{6,5},{7,6},{8,11},{9,8},{10,9... | collective-permute-start | bytes 4816904 | tf_op jit(solution)/shard_map/ppermute | solution.py:36
  731.4 9.0 %copy-start.7 = (bf16[896,512]{1,0:T(8,128)(2,1)S(1)}, bf16[896,512]{1,0:T(8,128)(2,1)}, u32[]{:S(2)}) copy-start(bf16[896,512]{1,0:T(8,128)(2,1)} %copy-done.6) | copy-start | bytes 2752516
  731.4 9.0 %copy-start.10 = (bf16[896,512]{1,0:T(8,128)(2,1)S(1)}, bf16[896,512]{1,0:T(8,128)(2,1)}, u32[]{:S(2)}) copy-start(bf16[896,512]{1,0:T(8,128)(2,1)} %copy-done.9) | copy-start | bytes 2752516
  731.4 38.9 %collective-permute-start.10 = (bf16[224,3584]{1,0:T(8,128)(2,1)}, bf16[224,3584]{1,0:T(8,128)(2,1)}, u32[]{:S(2)}, u32[]{:S(2)}) collective-permute-start(bf16[224,3584]{1,0:T(8,128)(2,1)} %get-tuple-element.45), channel_id=1, source_target_pairs={{0,16},{16,32},{32,48},{48,0},{1,17},{17,33},{33,49},{49,1},{2,18}... | collective-permute-start | bytes 4816904 | tf_op jit(solution)/shard_map/ppermute | solution.py:36
  734.5 69.9 %collective-permute-start.11 = (bf16[224,3584]{1,0:T(8,128)(2,1)}, bf16[224,3584]{1,0:T(8,128)(2,1)}, u32[]{:S(2)}, u32[]{:S(2)}) collective-permute-start(bf16[224,3584]{1,0:T(8,128)(2,1)} %get-tuple-element.46), channel_id=1, source_target_pairs={{0,32},{16,48},{32,0},{48,16},{1,33},{17,49},{33,1},{49,17},{2,34}... | collective-permute-start | bytes 4816904 | tf_op jit(solution)/shard_map/ppermute | solution.py:36
  735.6 6.1 copy-start.2
  735.6 68.9 %collective-permute-start.12 = (bf16[224,3584]{1,0:T(8,128)(2,1)}, bf16[224,3584]{1,0:T(8,128)(2,1)}, u32[]{:S(2)}, u32[]{:S(2)}) collective-permute-start(bf16[224,3584]{1,0:T(8,128)(2,1)} %get-tuple-element.47), channel_id=1, source_target_pairs={{0,48},{16,0},{32,16},{48,32},{1,49},{17,1},{33,17},{49,33},{2,50}... | collective-permute-start | bytes 4816904 | tf_op jit(solution)/shard_map/ppermute | solution.py:36
  804.4 14.1 %copy-start.1 = (bf16[1,1,64,14,1024]{4,2,3,1,0:T(8,128)(2,1)S(1)}, bf16[1,1,64,14,1024]{4,2,3,1,0:T(8,128)(2,1)}, u32[]{:S(2)}) copy-start(bf16[1,1,64,14,1024]{4,2,3,1,0:T(8,128)(2,1)} %param.7) | copy-start | bytes 5505028
Sparse Core Ops, SparseCore 0:
  10.4 128.6 all-gather.1
  250.3 83.1 reduce-scatter.1

commit v4 on v2

--- a/solution.py
+++ b/solution.py
@@ -41,47 +41,98 @@
 
 
 def hidden_sum_kernel(*refs):
-    grads, out = refs[0], refs[-1]
+    grads, pieces, out = refs[0], refs[1:9], refs[-1]
     total = None
-    for i, piece in enumerate(refs[1:-1]):
-        part = jnp.dot(grads[i], piece[...], preferred_element_type=jnp.float32)
+    for i, piece in enumerate(pieces):
+        part = lax.dot_general(
+            piece[...], grads[i], (((0,), (0,)), ((), ())), preferred_element_type=jnp.float32
+        )
         total = part if total is None else total + part
-    out[...] = total.T.astype(out.dtype)
-
-
-def hidden_sum(grads, pieces):
-    count, half, depth = grads.shape
+    out[...] = total.astype(out.dtype)
+
+
+def hidden_sum(grads, pieces, part, parts, before):
+    count, depth, half = grads.shape
     width = pieces[0].shape[1]
-    tile = 512 if width % 512 == 0 else width
+    tile = width // 2 if width % 256 == 0 else width
+    steps = width // tile
+    given = [] if before is None else [before]
     return pl.pallas_call(
         hidden_sum_kernel,
-        out_shape=jax.ShapeDtypeStruct((width, half), jnp.bfloat16),
+        out_shape=jax.ShapeDtypeStruct((parts * width, half), jnp.bfloat16),
+        grid=(steps,),
+        in_specs=[pl.BlockSpec((count, depth, half), lambda i: (0, 0, 0))]
+        + [pl.BlockSpec((depth, tile), lambda i: (0, i))] * count
+        + [pl.BlockSpec(memory_space=pl.ANY)] * len(given),
+        out_specs=pl.BlockSpec((tile, half), lambda i: (part * steps + i, 0)),
+        input_output_aliases={1 + count: 0} if given else {},
+        name="hidden_sum",
+    )(grads, *pieces, *given)
+
+
+def merge_kernel(size, *refs):
+    count = len(refs) // 2
+    for step in range(count):
+        for i in range(count):
+            refs[count + step][i * size : (i + 1) * size, :] = refs[i][
+                step * size : (step + 1) * size, :
+            ]
+
+
+def merged(parts, size):
+    count = len(parts)
+    rows, width = parts[0].shape
+    tile = width // 2 if width % 256 == 0 else width
+    block = pl.BlockSpec((rows, tile), lambda i: (0, i))
+    return pl.pallas_call(
+        functools.partial(merge_kernel, size),
+        out_shape=[jax.ShapeDtypeStruct(parts[0].shape, parts[0].dtype)] * count,
         grid=(width // tile,),
-        in_specs=[pl.BlockSpec((count, half, depth), lambda i: (0, 0, 0))]
-        + [pl.BlockSpec((depth, tile), lambda i: (0, i))] * count,
-        out_specs=pl.BlockSpec((tile, half), lambda i: (i, 0)),
-        name="hidden_sum",
-    )(grads, *pieces)
-
-
-def merge_kernel(*refs):
-    out = refs[-1]
-    size = refs[0].shape[0]
-    for i, piece in enumerate(refs[:-1]):
-        out[i * size : (i + 1) * size, :] = piece[...]
-
-
-def merged(parts, step, size):
-    width = parts[0].shape[1]
-    tile = 896 if width % 896 == 0 else width
-    return pl.pallas_call(
-        merge_kernel,
-        out_shape=jax.ShapeDtypeStruct((len(parts) * size, width), parts[0].dtype),
-        grid=(width // tile,),
-        in_specs=[pl.BlockSpec((size, tile), lambda i: (step, i))] * len(parts),
-        out_specs=pl.BlockSpec((len(parts) * size, tile), lambda i: (0, i)),
+        in_specs=[block] * count,
+        out_specs=[block] * count,
         name="merged",
     )(*parts)
+
+
+def pick_kernel(slots, keys, rows, *refs):
+    outs, chosen = refs[:-1], refs[-1]
+    total = keys.shape[2]
+
+    @pl.when(pl.program_id(0) == 0)
+    def _():
+        slot = lax.broadcasted_iota(jnp.int32, (slots, total), 0)
+        per_out = keys.shape[1] // len(outs)
+        for k in range(len(outs)):
+            some = [
+                jnp.where(keys[0, k * per_out + m : k * per_out + m + 1, :] == slot, 1.0, 0.0)
+                for m in range(per_out)
+            ]
+            chosen[k] = jnp.concatenate(some).astype(chosen.dtype)
+
+    tokens = rows[...].reshape(total, rows.shape[2])
+    for k, out in enumerate(outs):
+        found = jnp.dot(chosen[k], tokens, preferred_element_type=jnp.float32)
+        out[...] = found.astype(out.dtype)
+
+
+def picked(keys, gathered, section, lo, count, slots, outs, part, parts):
+    width = gathered.shape[2] // parts
+    tile = width // 2 if width % 256 == 0 else width
+    steps = width // tile
+    total = lo * count
+    per_out = keys.shape[1] // outs * slots
+    return pl.pallas_call(
+        functools.partial(pick_kernel, slots),
+        out_shape=[jax.ShapeDtypeStruct((per_out, width), gathered.dtype)] * outs,
+        grid=(steps,),
+        in_specs=[
+            pl.BlockSpec((1, keys.shape[1], total), lambda i: (section, 0, 0)),
+            pl.BlockSpec((lo, count, tile), lambda i: (section, 0, part * steps + i)),
+        ],
+        out_specs=[pl.BlockSpec((per_out, tile), lambda i: (0, i))] * outs,
+        scratch_shapes=[pltpu.VMEM((outs, per_out, total), gathered.dtype)],
+        name="picked",
+    )(keys, gathered)
 
 
 def key_kernel(sizes, most, top, place, ids, out, named_all):
@@ -156,6 +207,12 @@
     spare = 8
 
     grad = jnp.transpose(up_grad[0, 0], (1, 0, 2)).reshape(rows, 2 * half)
+    place = jnp.arange(rows, dtype=jnp.int32)
+    at_x, at_y = place // (n_y * slots), (place // slots) % n_y
+    at_lo, at_slot = (place // most) % n_lo, place % most
+    taken = at_slot * sources + (at_x * n_lo + at_lo) * n_y + at_y
+    by_place = (taken[:, None] == place[None, :]).astype(bf16)
+    grad = lax.optimization_barrier(dot(by_place, grad, ((1,), (0,))).astype(bf16))
     grad_own = jnp.where(low, grad[:, :half], grad[:, half:])
     grad_send = jnp.where(low, grad[:, half:], grad[:, :half])
     grad_mirror = lax.ppermute(grad_send, AXES, mirror_pairs(sizes))
@@ -164,64 +221,38 @@
     outgoing = jnp.concatenate([token_rows, id_rows])
     gathered = lax.all_gather(outgoing, ring_axes, axis=0, axis_index_groups=rings, tiled=True)
 
-    def order(place, at_x, at_y):
-        at_lo, at_slot = (place // most) % n_lo, place % most
-        taken = at_slot * sources + (at_x * n_lo + at_lo) * n_y + at_y
-        return (taken[:, None] == place[None, :]).astype(bf16)
-
-    place = jnp.arange(rows, dtype=jnp.int32)
-    by_place = order(place, place // (n_y * slots), (place // slots) % n_y)
-
-    def row_grad(grads):
-        sorted_rows = dot(by_place, grads, ((1,), (0,))).astype(bf16)
-        return dot(sorted_rows, weight, ((1,), (1,))).astype(bf16)
-
     def exchange(value):
         value = value.reshape(plane, slots, width)
         return lax.all_to_all(value, (X, Y), 0, 0, tiled=True).reshape(rows, width)
 
-    own_out = row_grad(grad_own)
+    my_x, my_lo, my_y = lax.axis_index(X), lax.axis_index(LO), lax.axis_index(Y)
+    own_out = dot(grad_own, weight, ((1,), (1,))).astype(bf16)
+    own_out, my_x, my_lo, my_y = lax.optimization_barrier((own_out, my_x, my_lo, my_y))
     own_back = exchange(own_out)
     own_back, grad_mirror = lax.optimization_barrier((own_back, grad_mirror))
-    mirror_out = row_grad(grad_mirror)
+    mirror_out = dot(grad_mirror, weight, ((1,), (1,))).astype(bf16)
     mirror_back = exchange(mirror_out)
-    my_x, my_lo, my_y = lax.axis_index(X), lax.axis_index(LO), lax.axis_index(Y)
     own_back, mirror_back, grad_own, grad_mirror, gathered, my_x, my_lo, my_y, nil = (
         lax.optimization_barrier(
             (own_back, mirror_back, grad_own, grad_mirror, gathered, my_x, my_lo, my_y, jnp.int32(0))
         )
     )
 
-    per_source = count + spare
-    keys = key_table(
-        sizes,
-        most,
-        top,
-        count,
-        jnp.stack([my_x, my_lo, my_y]).astype(jnp.int32),
-        gathered.reshape(n_hi * n_lo, per_source, width),
-    )
-    spaced = jnp.pad(
-        keys[:2].reshape(2, plane, n_lo, count),
-        ((0, 0), (0, 0), (0, 0), (0, spare)),
-        constant_values=-1,
-    ).reshape(2, plane, n_lo * per_source)
+    gathered = gathered.reshape(n_hi * n_lo, count + spare, width)
+    position = jnp.stack([my_x, my_lo, my_y]).astype(jnp.int32)
+    keys = key_table(sizes, most, top, count, position, gathered)
 
     def selector(some):
         slot = (jnp.arange(slots, dtype=jnp.int32) + nil)[None, :, None]
         return (some[:, None, :] == slot).astype(bf16).reshape(-1, some.shape[1])
 
-    per_section = n_lo * per_source
-    near_first, near_second = [None] * n_x, [None] * n_y
-    for step in (1, 3, 2, 0):
-        for key, which, near, axis, size in (
-            (spaced[0], 0, near_first, X, n_x),
-            (spaced[1], 1, near_second, Y, n_y),
-        ):
-            some = selector(key[step * (plane // size) : (step + 1) * (plane // size)])
-            section = gathered[which * per_section : (which + 1) * per_section]
-            sent = dot(some, section, ((1,), (0,))).astype(bf16)
-            near[step] = shifted(sent, axis, size, step)
+    parts = 2
+    routes = ((X, n_x, Y, n_y), (Y, n_y, X, n_x))
+    near = {}
+    for part in range(parts):
+        for section, (axis, size, _, _) in enumerate(routes):
+            sent = picked(keys, gathered, section, n_lo, count, slots, size, part, parts)
+            near[part, section] = [shifted(sent[i], axis, size, i) for i in range(size)]
 
     key_own = jnp.where(low, keys[2], keys[3])
     key_mirror = jnp.where(low, keys[3], keys[2])
@@ -234,24 +265,27 @@
         sums, ring_axes, scatter_dimension=0, axis_index_groups=rings, tiled=True
     )
 
-    grad_first = jnp.where(low, grad_own, grad_mirror)
-    grad_second = jnp.where(low, grad_mirror, grad_own)
+    far = {}
+    for part in range(parts):
+        for section, (_, _, axis, size) in enumerate(routes):
+            turned = merged(near[part, section], slots)
+            far[part, section] = [shifted(turned[i], axis, size, i) for i in range(size)]
+
     late = place + nil
-    outer, inner = late // (n_y * slots), (late // slots) % n_y
-    order_first = order(late, (my_x - inner) % n_x, (my_y - outer) % n_y).reshape(n_y, -1, rows)
-    order_second = order(late, (my_x - outer) % n_x, (my_y - inner) % n_y).reshape(n_x, -1, rows)
-    turned_grad = jnp.concatenate(
-        [
-            jnp.einsum("rf,kcr->kfc", some, by, preferred_element_type=jnp.float32)
-            for some, by in ((grad_first, order_first), (grad_second, order_second))
-        ]
-    ).astype(bf16)
-
-    far_first, far_second = [None] * n_y, [None] * n_x
-    for step in (1, 3, 2, 0):
-        far_first[step] = shifted(merged(near_first, step, slots), Y, n_y, step)
-        far_second[step] = shifted(merged(near_second, step, slots), X, n_x, step)
-    weight_grad = hidden_sum(turned_grad, far_first + far_second)
+    outer, inner, rest = late // (n_y * slots), (late // slots) % n_y, late % slots
+    turned_grad = []
+    for some, row_x, row_y in (
+        (jnp.where(low, grad_own, grad_mirror), my_x - inner, my_y - outer),
+        (jnp.where(low, grad_mirror, grad_own), my_x - outer, my_y - inner),
+    ):
+        row = ((row_x % n_x) * n_y + row_y % n_y) * slots + rest
+        order = (row[:, None] == place[None, :]).astype(bf16)
+        turned_grad.append(dot(order, some, ((1,), (0,))).astype(bf16))
+    turned_grad = jnp.concatenate(turned_grad).reshape(n_y + n_x, -1, half)
+    weight_grad = None
+    for part in range(parts):
+        pieces = far[part, 0] + far[part, 1]
+        weight_grad = hidden_sum(turned_grad, pieces, part, parts, weight_grad)
     return (token_grad[None], weight_grad[None, None])
 
 

time: 521 us -> 488 us (0.937)
  the two profiles are of different devices: /device:TPU:32 before, /device:TPU:88 now
where the time goes in v4:
time: 488 us; the launch traced here: 483 us
  waiting for transfers between devices  194 us (40%)
  blocking collectives  97.9 us (20%)
  starting transfers between devices  75.1 us (15%)
  Pallas kernels  49 us (10%)
  matrix products  34.3 us (7%)
  other arithmetic  15.4 us (3%)
  between operations  14.5 us (3%)
    ppermute x24, waiting for transfers between devices, shifted(): lax.ppermute(value, axis, [(i, (i + by) % size) for i in range(size)])  108 us
    all_to_all x1, blocking collectives, exchange(): return lax.all_to_all(value, (X, Y), 0, 0, tiled=True).reshape(rows, width)  97.9 us
    ppermute x24, starting transfers between devices, shifted(): lax.ppermute(value, axis, [(i, (i + by) % size) for i in range(size)])  63.5 us
    ppermute x1, waiting for transfers between devices, on_device(): grad_mirror = lax.ppermute(grad_send, AXES, mirror_pairs(sizes))  61.6 us
    dot_general x7, matrix products, dot(): lax.dot_general(a, b, (dims, ((), ())), preferred_element_type=jnp.float32)  34.3 us
    all_to_all x1, waiting for transfers between devices, exchange(): return lax.all_to_all(value, (X, Y), 0, 0, tiled=True).reshape(rows, width)  24.1 us
    pallas_call x4, Pallas kernels, picked(): pl.pallas_call(functools.partial(pick_kernel, slots), out_shape=[jax.Shap...  17.8 us
    pallas_call x2, Pallas kernels, hidden_sum(): pl.pallas_call(hidden_sum_kernel, out_shape=jax.ShapeDtypeStruct((parts *...  16.7 us
  transfers between devices with their start and end apart: 28, of which 10 were waited for; matrix products, arithmetic and copies ran while one was open for 5% of the time, Pallas kernels for 10%

profile of v4, /device:TPU:88, one launch (start us, length us, event | category | flops | bytes accessed | tf_op | source)
XLA Modules:
  0.0 483.0 jit_solution(15238928353824918822)
XLA Ops:
  10.4 3.3 fusion.6
  16.3 5.5 %convolution_convert_fusion.1 = bf16[896,3584]{1,0:T(8,128)(2,1)} fusion(bf16[896,512]{1,0:T(8,128)(2,1)S(1)} %get-tuple-element.62, bf16[1,1,3584,512]{3,2,1,0:T(8,128)(2,1)S(1)} %copy-done.12), kind=kOutput, calls=%fused_computation.2 | convolution fusion | flops 3291545600 | bytes 11010048 | tf_op jit(solution)/shard_map/dot_general | solution.py:40
  21.8 7.2 %all-to-all-start = ((bf16[16,56,3584]{2,1,0:T(8,128)(2,1)}), bf16[16,56,3584]{2,1,0:T(8,128)(2,1)}, u32[]{:S(2)}, u32[]{:S(2)}) async-start(bf16[16,56,3584]{2,1,0:T(8,128)(2,1)} %bitcast.51), calls=%async_computation | async-start | bytes 12845056 | tf_op jit(solution)/shard_map/all_to_all | solution.py:226
  29.0 4.4 collective-permute-start
  33.3 61.6 %collective-permute-done = bf16[896,512]{1,0:T(8,128)(2,1)S(1)} collective-permute-done((bf16[896,512]{1,0:T(8,128)(2,1)S(1)}, bf16[896,512]{1,0:T(8,128)(2,1)S(1)}, u32[]{:S(2)}, u32[]{:S(2)}) %collective-permute-start) | collective-permute-done | bytes 917536 | tf_op jit(solution)/shard_map/ppermute | solution.py:218
  95.0 24.1 %all-to-all-done = bf16[16,56,3584]{2,1,0:T(8,128)(2,1)} async-done(((bf16[16,56,3584]{2,1,0:T(8,128)(2,1)}), bf16[16,56,3584]{2,1,0:T(8,128)(2,1)}, u32[]{:S(2)}, u32[]{:S(2)}) %all-to-all-start) | async-done | bytes 6422560 | tf_op jit(solution)/shard_map/all_to_all | solution.py:226
  119.1 5.8 %convolution_convert_fusion = bf16[896,3584]{1,0:T(8,128)(2,1)S(1)} fusion(bf16[896,512]{1,0:T(8,128)(2,1)S(1)} %collective-permute-done, bf16[1,1,3584,512]{3,2,1,0:T(8,128)(2,1)} %param.6), kind=kOutput, calls=%fused_computation.1 | convolution fusion | flops 3291545600 | bytes 11010048 | tf_op jit(solution)/shard_map/dot_general | solution.py:40
  124.9 97.9 %all_to_all.10 = bf16[16,56,3584]{2,1,0:T(8,128)(2,1)} all-to-all(bf16[16,56,3584]{2,1,0:T(8,128)(2,1)S(1)} %bitcast.52), channel_id=1, replica_groups=mesh['hi'=2,'core'=2,'x'=4,'lo'=4,'y'=4] {'x','y'}, dimensions={0} | all-to-all | bytes 12845056 | tf_op jit(solution)/shard_map/all_to_all | solution.py:226
  226.5 7.1 %convolution_convert_fusion.2 = bf16[512,3584]{1,0:T(8,128)(2,1)S(1)} fusion(pred[896,512]{1,0:T(32,128)(4,1)S(1)} %get-tuple-element.103, bf16[896,3584]{1,0:T(8,128)(2,1)} %bitcast.50), kind=kOutput, calls=%fused_computation.3 | convolution fusion | flops 3290169344 | bytes 10551296 | tf_op jit(solution)/shard_map/dot_general | solution.py:40
  233.6 9.0 %broadcast_select_fusion.1 = (bf16[512,3584]{1,0:T(8,128)(2,1)}, bf16[512,3584]{1,0:T(8,128)(2,1)}) fusion(bf16[512,3584]{1,0:T(8,128)(2,1)S(1)} %convolution_convert_fusion.2, pred[]{:T(512)S(6)} %eq.86, pred[896,512]{1,0:T(32,128)(4,1)S(1)} %get-tuple-element.102, bf16[896,3584]{1,0:T(8,128)(2,1)} %bitcast.5), kind=kOutput, calls=%fused_computation.8 | convolution fusion | flops 3293839360 | bytes 17891328 | tf_op jit(solution)/shard_map/dot_general | solution.py:40
  242.5 6.6 %pad_maximum_fusion = bf16[1024,3584]{1,0:T(8,128)(2,1)} fusion(bf16[512,3584]{1,0:T(8,128)(2,1)} %get-tuple-element.97, bf16[512,3584]{1,0:T(8,128)(2,1)} %get-tuple-element.96), kind=kLoop, calls=%fused_computation | loop fusion | flops 14680064 | bytes 14680064 | tf_op jit(solution)/shard_map/concatenate | solution.py:261
  249.2 4.4 picked.4
  257.4 4.4 picked.6
  264.2 28.8 %collective-permute-done.1.refs_1_ = bf16[224,1792]{1,0:T(8,128)(2,1)S(1)} collective-permute-done((bf16[224,1792]{1,0:T(8,128)(2,1)}, bf16[224,1792]{1,0:T(8,128)(2,1)S(1)}, u32[]{:S(2)}, u32[]{:S(2)}) %collective-permute-start.1) | collective-permute-done | bytes 802848 | tf_op jit(solution)/shard_map/ppermute | solution.py:36
  293.1 4.5 picked.7
  300.7 6.9 %collective-permute-done.13.refs_1_ = bf16[224,1792]{1,0:T(8,128)(2,1)S(1)} collective-permute-done((bf16[224,1792]{1,0:T(8,128)(2,1)}, bf16[224,1792]{1,0:T(8,128)(2,1)S(1)}, u32[]{:S(2)}, u32[]{:S(2)}) %collective-permute-start.13) | collective-permute-done | bytes 802848 | tf_op jit(solution)/shard_map/ppermute | solution.py:36
  309.9 4.4 picked.5
  314.4 3.3 merged.4
  317.6 7.1 %collective-permute-done.14.refs_2_ = bf16[224,1792]{1,0:T(8,128)(2,1)S(1)} collective-permute-done((bf16[224,1792]{1,0:T(8,128)(2,1)}, bf16[224,1792]{1,0:T(8,128)(2,1)S(1)}, u32[]{:S(2)}, u32[]{:S(2)}) %collective-permute-start.14) | collective-permute-done | bytes 802848 | tf_op jit(solution)/shard_map/ppermute | solution.py:36
  324.7 9.2 %collective-permute-start.7 = (bf16[224,1792]{1,0:T(8,128)(2,1)}, bf16[224,1792]{1,0:T(8,128)(2,1)S(1)}, u32[]{:S(2)}, u32[]{:S(2)}) collective-permute-start(bf16[224,1792]{1,0:T(8,128)(2,1)} %get-tuple-element.73), channel_id=1, source_target_pairs={{0,1},{1,2},{2,3},{3,0},{4,5},{5,6},{6,7},{7,4},{8,9},{9,10},{10,1... | collective-permute-start | bytes 2408456 | tf_op jit(solution)/shard_map/ppermute | solution.py:36
  342.4 13.6 %collective-permute-done.21.refs_3_ = bf16[224,1792]{1,0:T(8,128)(2,1)} collective-permute-done((bf16[224,1792]{1,0:T(8,128)(2,1)}, bf16[224,1792]{1,0:T(8,128)(2,1)}, u32[]{:S(2)}, u32[]{:S(2)}) %collective-permute-start.21) | collective-permute-done | bytes 802848 | tf_op jit(solution)/shard_map/ppermute | solution.py:36
  356.1 3.3 merged.7
  359.4 10.4 %collective-permute-done.7.refs_1_ = bf16[224,1792]{1,0:T(8,128)(2,1)S(1)} collective-permute-done((bf16[224,1792]{1,0:T(8,128)(2,1)}, bf16[224,1792]{1,0:T(8,128)(2,1)S(1)}, u32[]{:S(2)}, u32[]{:S(2)}) %collective-permute-start.7) | collective-permute-done | bytes 802848 | tf_op jit(solution)/shard_map/ppermute | solution.py:36
  371.5 4.4 collective-permute-start.18
  376.0 14.5 %collective-permute-done.9.refs_3_ = bf16[224,1792]{1,0:T(8,128)(2,1)} collective-permute-done((bf16[224,1792]{1,0:T(8,128)(2,1)}, bf16[224,1792]{1,0:T(8,128)(2,1)}, u32[]{:S(2)}, u32[]{:S(2)}) %collective-permute-start.9) | collective-permute-done | bytes 802848 | tf_op jit(solution)/shard_map/ppermute | solution.py:36
  390.5 6.9 %collective-permute-done.16.refs_2_ = bf16[224,1792]{1,0:T(8,128)(2,1)S(1)} collective-permute-done((bf16[224,1792]{1,0:T(8,128)(2,1)}, bf16[224,1792]{1,0:T(8,128)(2,1)S(1)}, u32[]{:S(2)}, u32[]{:S(2)}) %collective-permute-start.16) | collective-permute-done | bytes 802848 | tf_op jit(solution)/shard_map/ppermute | solution.py:36
  397.4 22.9 %collective-permute-start.24 = (bf16[224,1792]{1,0:T(8,128)(2,1)}, bf16[224,1792]{1,0:T(8,128)(2,1)}, u32[]{:S(2)}, u32[]{:S(2)}) collective-permute-start(bf16[224,1792]{1,0:T(8,128)(2,1)} %get-tuple-element.95), channel_id=1, source_target_pairs={{0,48},{16,0},{32,16},{48,32},{1,49},{17,1},{33,17},{49,33},{2,50}... | collective-permute-start | bytes 2408456 | tf_op jit(solution)/shard_map/ppermute | solution.py:36
  424.5 4.4 collective-permute-start.6
  430.4 20.0 %collective-permute-done.24.refs_8_ = bf16[224,1792]{1,0:T(8,128)(2,1)} collective-permute-done((bf16[224,1792]{1,0:T(8,128)(2,1)}, bf16[224,1792]{1,0:T(8,128)(2,1)}, u32[]{:S(2)}, u32[]{:S(2)}) %collective-permute-start.24) | collective-permute-done | bytes 802848 | tf_op jit(solution)/shard_map/ppermute | solution.py:36
  450.4 3.7 collective-permute-start.12
  459.2 8.3 %hidden_sum.2.refs_9_ = bf16[3584,512]{1,0:T(8,128)(2,1)} custom-call(bf16[8,224,512]{2,1,0:T(8,128)(2,1)} %bitcast.47, bf16[224,1792]{1,0:T(8,128)(2,1)} %get-tuple-element.84.refs_1_, bf16[224,1792]{1,0:T(8,128)(2,1)} %copy-done.2, bf16[224,1792]{1,0:T(8,128)(2,1)} %copy-done.3, bf16[224,1792]{1,0:T(8,128)(2,1)} %copy-done.4, ...), custom_call_target="tpu_custom_call" | custom-call | tf_op jit(solution)/shard_map/hidden_sum/pallas_call | solution.py:60
  467.5 8.4 %hidden_sum.3 = bf16[3584,512]{1,0:T(8,128)(2,1)} custom-call(bf16[8,224,512]{2,1,0:T(8,128)(2,1)} %bitcast.48, bf16[224,1792]{1,0:T(8,128)(2,1)} %get-tuple-element.68.refs_1_, bf16[224,1792]{1,0:T(8,128)(2,1)} %collective-permute-done.4.refs_2_, bf16[224,1792]{1,0:T(8,128)(2,1)} %collective-permute-done.5.refs_3_, ...), custom_call_target="tpu_custom_call", output_to_operand_aliasing={{}: (9, {})} | custom-call | tf_op jit(solution)/shard_map/hidden_sum/pallas_call | solution.py:60
  (88 shorter events, 42.1 us)
Async XLA Ops:
  7.2 215.6 %all-gather.2.cloned.1.call-start = ((), (), s32[]{:S(2)}) async-start(), calls=%async_computation.3 | async-start | bytes 8773632 | tf_op jit(solution)/shard_map/all_gather | solution.py:222
  21.8 97.3 %all-to-all-start = ((bf16[16,56,3584]{2,1,0:T(8,128)(2,1)}), bf16[16,56,3584]{2,1,0:T(8,128)(2,1)}, u32[]{:S(2)}, u32[]{:S(2)}) async-start(bf16[16,56,3584]{2,1,0:T(8,128)(2,1)} %bitcast.51), calls=%async_computation | async-start | bytes 12845056 | tf_op jit(solution)/shard_map/all_to_all | solution.py:226
  28.9 447.0 %reduce-scatter.2.cloned.1.call-start = ((), (), s32[]{:S(2)}) async-start(), calls=%async_computation.4 | async-start | bytes 8257536 | tf_op jit(solution)/shard_map/reduce_scatter | solution.py:264
  29.0 66.0 %collective-permute-start = (bf16[896,512]{1,0:T(8,128)(2,1)S(1)}, bf16[896,512]{1,0:T(8,128)(2,1)S(1)}, u32[]{:S(2)}, u32[]{:S(2)}) collective-permute-start(bf16[896,512]{1,0:T(8,128)(2,1)S(1)} %get-tuple-element.98), channel_id=1, source_target_pairs={{0,192},{1,193},{2,194},{3,195},{4,196},{5,197},{6,198},{7,199},{8... | collective-permute-start | bytes 2752520 | tf_op jit(solution)/shard_map/ppermute | solution.py:218
  94.9 30.0 %copy-start.13 = (bf16[896,512]{1,0:T(8,128)(2,1)}, bf16[896,512]{1,0:T(8,128)(2,1)S(1)}, u32[]{:S(2)}) copy-start(bf16[896,512]{1,0:T(8,128)(2,1)S(1)} %collective-permute-done) | copy-start | bytes 2752516
  253.6 39.4 %collective-permute-start.1 = (bf16[224,1792]{1,0:T(8,128)(2,1)}, bf16[224,1792]{1,0:T(8,128)(2,1)S(1)}, u32[]{:S(2)}, u32[]{:S(2)}) collective-permute-start(bf16[224,1792]{1,0:T(8,128)(2,1)} %get-tuple-element.65), channel_id=1, source_target_pairs={{0,16},{16,32},{32,48},{48,0},{1,17},{17,33},{33,49},{49,1},{2,18}... | collective-permute-start | bytes 2408456 | tf_op jit(solution)/shard_map/ppermute | solution.py:36
  254.0 43.7 %collective-permute-start.2 = (bf16[224,1792]{1,0:T(8,128)(2,1)}, bf16[224,1792]{1,0:T(8,128)(2,1)}, u32[]{:S(2)}, u32[]{:S(2)}) collective-permute-start(bf16[224,1792]{1,0:T(8,128)(2,1)} %get-tuple-element.66), channel_id=1, source_target_pairs={{0,32},{16,48},{32,0},{48,16},{1,33},{17,49},{33,1},{49,17},{2,34}... | collective-permute-start | bytes 2408456 | tf_op jit(solution)/shard_map/ppermute | solution.py:36
  256.1 43.7 %collective-permute-start.3 = (bf16[224,1792]{1,0:T(8,128)(2,1)}, bf16[224,1792]{1,0:T(8,128)(2,1)}, u32[]{:S(2)}, u32[]{:S(2)}) collective-permute-start(bf16[224,1792]{1,0:T(8,128)(2,1)} %get-tuple-element.67), channel_id=1, source_target_pairs={{0,48},{16,0},{32,16},{48,32},{1,49},{17,1},{33,17},{49,33},{2,50}... | collective-permute-start | bytes 2408456 | tf_op jit(solution)/shard_map/ppermute | solution.py:36
  261.8 45.7 %collective-permute-start.13 = (bf16[224,1792]{1,0:T(8,128)(2,1)}, bf16[224,1792]{1,0:T(8,128)(2,1)S(1)}, u32[]{:S(2)}, u32[]{:S(2)}) collective-permute-start(bf16[224,1792]{1,0:T(8,128)(2,1)} %get-tuple-element.81), channel_id=1, source_target_pairs={{0,16},{16,32},{32,48},{48,0},{1,17},{17,33},{33,49},{49,1},{2,18}... | collective-permute-start | bytes 2408456 | tf_op jit(solution)/shard_map/ppermute | solution.py:36
  262.5 62.2 %collective-permute-start.14 = (bf16[224,1792]{1,0:T(8,128)(2,1)}, bf16[224,1792]{1,0:T(8,128)(2,1)S(1)}, u32[]{:S(2)}, u32[]{:S(2)}) collective-permute-start(bf16[224,1792]{1,0:T(8,128)(2,1)} %get-tuple-element.82), channel_id=1, source_target_pairs={{0,32},{16,48},{32,0},{48,16},{1,33},{17,49},{33,1},{49,17},{2,34}... | collective-permute-start | bytes 2408456 | tf_op jit(solution)/shard_map/ppermute | solution.py:36
  293.0 41.0 %collective-permute-start.15 = (bf16[224,1792]{1,0:T(8,128)(2,1)}, bf16[224,1792]{1,0:T(8,128)(2,1)}, u32[]{:S(2)}, u32[]{:S(2)}) collective-permute-start(bf16[224,1792]{1,0:T(8,128)(2,1)} %get-tuple-element.83), channel_id=1, source_target_pairs={{0,48},{16,0},{32,16},{48,32},{1,49},{17,1},{33,17},{49,33},{2,50}... | collective-permute-start | bytes 2408456 | tf_op jit(solution)/shard_map/ppermute | solution.py:36
  297.7 41.4 %collective-permute-start.19 = (bf16[224,1792]{1,0:T(8,128)(2,1)}, bf16[224,1792]{1,0:T(8,128)(2,1)S(1)}, u32[]{:S(2)}, u32[]{:S(2)}) collective-permute-start(bf16[224,1792]{1,0:T(8,128)(2,1)} %get-tuple-element.89), channel_id=1, source_target_pairs={{0,1},{1,2},{2,3},{3,0},{4,5},{5,6},{6,7},{7,4},{8,9},{9,10},{10,1... | collective-permute-start | bytes 2408456 | tf_op jit(solution)/shard_map/ppermute | solution.py:36
  299.7 40.1 %collective-permute-start.20 = (bf16[224,1792]{1,0:T(8,128)(2,1)}, bf16[224,1792]{1,0:T(8,128)(2,1)}, u32[]{:S(2)}, u32[]{:S(2)}) collective-permute-start(bf16[224,1792]{1,0:T(8,128)(2,1)} %get-tuple-element.90), channel_id=1, source_target_pairs={{0,2},{1,3},{2,0},{3,1},{4,6},{5,7},{6,4},{7,5},{8,10},{9,11},{10,... | collective-permute-start | bytes 2408456 | tf_op jit(solution)/shard_map/ppermute | solution.py:36
  307.6 48.5 %collective-permute-start.21 = (bf16[224,1792]{1,0:T(8,128)(2,1)}, bf16[224,1792]{1,0:T(8,128)(2,1)}, u32[]{:S(2)}, u32[]{:S(2)}) collective-permute-start(bf16[224,1792]{1,0:T(8,128)(2,1)} %get-tuple-element.91), channel_id=1, source_target_pairs={{0,3},{1,0},{2,1},{3,2},{4,7},{5,4},{6,5},{7,6},{8,11},{9,8},{10,9... | collective-permute-start | bytes 2408456 | tf_op jit(solution)/shard_map/ppermute | solution.py:36
  324.7 45.0 %collective-permute-start.7 = (bf16[224,1792]{1,0:T(8,128)(2,1)}, bf16[224,1792]{1,0:T(8,128)(2,1)S(1)}, u32[]{:S(2)}, u32[]{:S(2)}) collective-permute-start(bf16[224,1792]{1,0:T(8,128)(2,1)} %get-tuple-element.73), channel_id=1, source_target_pairs={{0,1},{1,2},{2,3},{3,0},{4,5},{5,6},{6,7},{7,4},{8,9},{9,10},{10,1... | collective-permute-start | bytes 2408456 | tf_op jit(solution)/shard_map/ppermute | solution.py:36
  334.0 36.7 %collective-permute-start.8 = (bf16[224,1792]{1,0:T(8,128)(2,1)}, bf16[224,1792]{1,0:T(8,128)(2,1)S(1)}, u32[]{:S(2)}, u32[]{:S(2)}) collective-permute-start(bf16[224,1792]{1,0:T(8,128)(2,1)} %get-tuple-element.74), channel_id=1, source_target_pairs={{0,2},{1,3},{2,0},{3,1},{4,6},{5,7},{6,4},{7,5},{8,10},{9,11},{10,... | collective-permute-start | bytes 2408456 | tf_op jit(solution)/shard_map/ppermute | solution.py:36
  339.1 51.3 %collective-permute-start.9 = (bf16[224,1792]{1,0:T(8,128)(2,1)}, bf16[224,1792]{1,0:T(8,128)(2,1)}, u32[]{:S(2)}, u32[]{:S(2)}) collective-permute-start(bf16[224,1792]{1,0:T(8,128)(2,1)} %get-tuple-element.75), channel_id=1, source_target_pairs={{0,3},{1,0},{2,1},{3,2},{4,7},{5,4},{6,5},{7,6},{8,11},{9,8},{10,9... | collective-permute-start | bytes 2408456 | tf_op jit(solution)/shard_map/ppermute | solution.py:36
  339.8 50.6 %collective-permute-start.4 = (bf16[224,1792]{1,0:T(8,128)(2,1)}, bf16[224,1792]{1,0:T(8,128)(2,1)}, u32[]{:S(2)}, u32[]{:S(2)}) collective-permute-start(bf16[224,1792]{1,0:T(8,128)(2,1)} %get-tuple-element.69), channel_id=1, source_target_pairs={{0,1},{1,2},{2,3},{3,0},{4,5},{5,6},{6,7},{7,4},{8,9},{9,10},{10,1... | collective-permute-start | bytes 2408456 | tf_op jit(solution)/shard_map/ppermute | solution.py:36
  356.1 41.3 %collective-permute-start.16 = (bf16[224,1792]{1,0:T(8,128)(2,1)}, bf16[224,1792]{1,0:T(8,128)(2,1)S(1)}, u32[]{:S(2)}, u32[]{:S(2)}) collective-permute-start(bf16[224,1792]{1,0:T(8,128)(2,1)} %get-tuple-element.85), channel_id=1, source_target_pairs={{0,1},{1,2},{2,3},{3,0},{4,5},{5,6},{6,7},{7,4},{8,9},{9,10},{10,1... | collective-permute-start | bytes 2408456 | tf_op jit(solution)/shard_map/ppermute | solution.py:36
  370.6 53.5 %collective-permute-start.17 = (bf16[224,1792]{1,0:T(8,128)(2,1)}, bf16[224,1792]{1,0:T(8,128)(2,1)S(1)}, u32[]{:S(2)}, u32[]{:S(2)}) collective-permute-start(bf16[224,1792]{1,0:T(8,128)(2,1)} %get-tuple-element.86), channel_id=1, source_target_pairs={{0,2},{1,3},{2,0},{3,1},{4,6},{5,7},{6,4},{7,5},{8,10},{9,11},{10,... | collective-permute-start | bytes 2408456 | tf_op jit(solution)/shard_map/ppermute | solution.py:36
  371.5 52.9 %collective-permute-start.18 = (bf16[224,1792]{1,0:T(8,128)(2,1)}, bf16[224,1792]{1,0:T(8,128)(2,1)S(1)}, u32[]{:S(2)}, u32[]{:S(2)}) collective-permute-start(bf16[224,1792]{1,0:T(8,128)(2,1)} %get-tuple-element.87), channel_id=1, source_target_pairs={{0,3},{1,0},{2,1},{3,2},{4,7},{5,4},{6,5},{7,6},{8,11},{9,8},{10,9... | collective-permute-start | bytes 2408456 | tf_op jit(solution)/shard_map/ppermute | solution.py:36
  390.5 38.4 %collective-permute-start.22 = (bf16[224,1792]{1,0:T(8,128)(2,1)}, bf16[224,1792]{1,0:T(8,128)(2,1)}, u32[]{:S(2)}, u32[]{:S(2)}) collective-permute-start(bf16[224,1792]{1,0:T(8,128)(2,1)} %get-tuple-element.93), channel_id=1, source_target_pairs={{0,16},{16,32},{32,48},{48,0},{1,17},{17,33},{33,49},{49,1},{2,18}... | collective-permute-start | bytes 2408456 | tf_op jit(solution)/shard_map/ppermute | solution.py:36
  390.5 38.4 %collective-permute-start.23 = (bf16[224,1792]{1,0:T(8,128)(2,1)}, bf16[224,1792]{1,0:T(8,128)(2,1)}, u32[]{:S(2)}, u32[]{:S(2)}) collective-permute-start(bf16[224,1792]{1,0:T(8,128)(2,1)} %get-tuple-element.94), channel_id=1, source_target_pairs={{0,32},{16,48},{32,0},{48,16},{1,33},{17,49},{33,1},{49,17},{2,34}... | collective-permute-start | bytes 2408456 | tf_op jit(solution)/shard_map/ppermute | solution.py:36
  397.4 59.2 %copy-start.2 = (bf16[224,1792]{1,0:T(8,128)(2,1)}, bf16[224,1792]{1,0:T(8,128)(2,1)S(1)}, u32[]{:S(2)}) copy-start(bf16[224,1792]{1,0:T(8,128)(2,1)S(1)} %collective-permute-done.16.refs_2_) | copy-start | bytes 2408452
  397.4 53.1 %collective-permute-start.24 = (bf16[224,1792]{1,0:T(8,128)(2,1)}, bf16[224,1792]{1,0:T(8,128)(2,1)}, u32[]{:S(2)}, u32[]{:S(2)}) collective-permute-start(bf16[224,1792]{1,0:T(8,128)(2,1)} %get-tuple-element.95), channel_id=1, source_target_pairs={{0,48},{16,0},{32,16},{48,32},{1,49},{17,1},{33,17},{49,33},{2,50}... | collective-permute-start | bytes 2408456 | tf_op jit(solution)/shard_map/ppermute | solution.py:36
  424.2 29.9 %copy-start.3 = (bf16[224,1792]{1,0:T(8,128)(2,1)}, bf16[224,1792]{1,0:T(8,128)(2,1)S(1)}, u32[]{:S(2)}) copy-start(bf16[224,1792]{1,0:T(8,128)(2,1)S(1)} %collective-permute-done.17.refs_3_) | copy-start | bytes 2408452
  424.2 43.3 %collective-permute-start.5 = (bf16[224,1792]{1,0:T(8,128)(2,1)}, bf16[224,1792]{1,0:T(8,128)(2,1)}, u32[]{:S(2)}, u32[]{:S(2)}) collective-permute-start(bf16[224,1792]{1,0:T(8,128)(2,1)} %get-tuple-element.70), channel_id=1, source_target_pairs={{0,2},{1,3},{2,0},{3,1},{4,6},{5,7},{6,4},{7,5},{8,10},{9,11},{10,... | collective-permute-start | bytes 2408456 | tf_op jit(solution)/shard_map/ppermute | solution.py:36
  424.5 29.6 %copy-start.4 = (bf16[224,1792]{1,0:T(8,128)(2,1)}, bf16[224,1792]{1,0:T(8,128)(2,1)S(1)}, u32[]{:S(2)}) copy-start(bf16[224,1792]{1,0:T(8,128)(2,1)S(1)} %collective-permute-done.18.refs_4_) | copy-start | bytes 2408452
  424.5 42.9 %collective-permute-start.6 = (bf16[224,1792]{1,0:T(8,128)(2,1)}, bf16[224,1792]{1,0:T(8,128)(2,1)}, u32[]{:S(2)}, u32[]{:S(2)}) collective-permute-start(bf16[224,1792]{1,0:T(8,128)(2,1)} %get-tuple-element.71), channel_id=1, source_target_pairs={{0,3},{1,0},{2,1},{3,2},{4,7},{5,4},{6,5},{7,6},{8,11},{9,8},{10,9... | collective-permute-start | bytes 2408456 | tf_op jit(solution)/shard_map/ppermute | solution.py:36
  428.9 38.6 %collective-permute-start.10 = (bf16[224,1792]{1,0:T(8,128)(2,1)}, bf16[224,1792]{1,0:T(8,128)(2,1)}, u32[]{:S(2)}, u32[]{:S(2)}) collective-permute-start(bf16[224,1792]{1,0:T(8,128)(2,1)} %get-tuple-element.77), channel_id=1, source_target_pairs={{0,16},{16,32},{32,48},{48,0},{1,17},{17,33},{33,49},{49,1},{2,18}... | collective-permute-start | bytes 2408456 | tf_op jit(solution)/shard_map/ppermute | solution.py:36
  428.9 38.6 %collective-permute-start.11 = (bf16[224,1792]{1,0:T(8,128)(2,1)}, bf16[224,1792]{1,0:T(8,128)(2,1)}, u32[]{:S(2)}, u32[]{:S(2)}) collective-permute-start(bf16[224,1792]{1,0:T(8,128)(2,1)} %get-tuple-element.78), channel_id=1, source_target_pairs={{0,32},{16,48},{32,0},{48,16},{1,33},{17,49},{33,1},{49,17},{2,34}... | collective-permute-start | bytes 2408456 | tf_op jit(solution)/shard_map/ppermute | solution.py:36
  450.4 17.0 %collective-permute-start.12 = (bf16[224,1792]{1,0:T(8,128)(2,1)}, bf16[224,1792]{1,0:T(8,128)(2,1)}, u32[]{:S(2)}, u32[]{:S(2)}) collective-permute-start(bf16[224,1792]{1,0:T(8,128)(2,1)} %get-tuple-element.79), channel_id=1, source_target_pairs={{0,48},{16,0},{32,16},{48,32},{1,49},{17,1},{33,17},{49,33},{2,50}... | collective-permute-start | bytes 2408456 | tf_op jit(solution)/shard_map/ppermute | solution.py:36
  (11 other events, 58.6 us)
Sparse Core Ops, SparseCore 0:
  10.4 128.0 all-gather.1
  249.3 83.9 reduce-scatter.1

commit v5 on v4

--- a/solution.py
+++ b/solution.py
@@ -13,13 +13,8 @@
 
 
 def mirror_pairs(sizes):
-    n_hi, n_core, n_x, n_lo, n_y = sizes
-    block = n_x * n_lo * n_y
-    pairs = []
-    for section in range(n_hi * n_core):
-        for place in range(block):
-            pairs.append((section * block + place, (n_hi * n_core - 1 - section) * block + place))
-    return pairs
+    count = sizes[0] * sizes[1]
+    return [[section, count - 1 - section] for section in range(count // 2)]
 
 
 def mirror_rings(sizes):
@@ -94,18 +89,18 @@
     )(*parts)
 
 
-def pick_kernel(slots, keys, rows, *refs):
+def pick_kernel(slots, per_out, blocks, keys, rows, *refs):
     outs, chosen = refs[:-1], refs[-1]
     total = keys.shape[2]
 
     @pl.when(pl.program_id(0) == 0)
     def _():
         slot = lax.broadcasted_iota(jnp.int32, (slots, total), 0)
-        per_out = keys.shape[1] // len(outs)
-        for k in range(len(outs)):
+        for k, block in enumerate(blocks):
+            first = block * per_out
             some = [
-                jnp.where(keys[0, k * per_out + m : k * per_out + m + 1, :] == slot, 1.0, 0.0)
-                for m in range(per_out)
+                jnp.where(keys[0, m : m + 1, :] == slot, 1.0, 0.0)
+                for m in range(first, first + per_out)
             ]
             chosen[k] = jnp.concatenate(some).astype(chosen.dtype)
 
@@ -115,22 +110,23 @@
         out[...] = found.astype(out.dtype)
 
 
-def picked(keys, gathered, section, lo, count, slots, outs, part, parts):
+def picked(keys, gathered, section, lo, count, slots, size, blocks, part, parts):
     width = gathered.shape[2] // parts
     tile = width // 2 if width % 256 == 0 else width
     steps = width // tile
     total = lo * count
-    per_out = keys.shape[1] // outs * slots
+    per_out = keys.shape[1] // size
+    shape = (per_out * slots, width)
     return pl.pallas_call(
-        functools.partial(pick_kernel, slots),
-        out_shape=[jax.ShapeDtypeStruct((per_out, width), gathered.dtype)] * outs,
+        functools.partial(pick_kernel, slots, per_out, blocks),
+        out_shape=[jax.ShapeDtypeStruct(shape, gathered.dtype)] * len(blocks),
         grid=(steps,),
         in_specs=[
             pl.BlockSpec((1, keys.shape[1], total), lambda i: (section, 0, 0)),
             pl.BlockSpec((lo, count, tile), lambda i: (section, 0, part * steps + i)),
         ],
-        out_specs=[pl.BlockSpec((per_out, tile), lambda i: (0, i))] * outs,
-        scratch_shapes=[pltpu.VMEM((outs, per_out, total), gathered.dtype)],
+        out_specs=[pl.BlockSpec((shape[0], tile), lambda i: (0, i))] * len(blocks),
+        scratch_shapes=[pltpu.VMEM((len(blocks), shape[0], total), gathered.dtype)],
         name="picked",
     )(keys, gathered)
 
@@ -215,7 +211,8 @@
     grad = lax.optimization_barrier(dot(by_place, grad, ((1,), (0,))).astype(bf16))
     grad_own = jnp.where(low, grad[:, :half], grad[:, half:])
     grad_send = jnp.where(low, grad[:, half:], grad[:, :half])
-    grad_mirror = lax.ppermute(grad_send, AXES, mirror_pairs(sizes))
+    pair = (HI, CORE)
+    swapped = lax.all_gather(grad_send, pair, axis=0, axis_index_groups=mirror_pairs(sizes))
 
     id_rows = jnp.pad(expert_ids[0].T.astype(bf16), ((0, spare - top), (0, width - count)))
     outgoing = jnp.concatenate([token_rows, id_rows])
@@ -229,7 +226,8 @@
     own_out = dot(grad_own, weight, ((1,), (1,))).astype(bf16)
     own_out, my_x, my_lo, my_y = lax.optimization_barrier((own_out, my_x, my_lo, my_y))
     own_back = exchange(own_out)
-    own_back, grad_mirror = lax.optimization_barrier((own_back, grad_mirror))
+    own_back, swapped = lax.optimization_barrier((own_back, swapped))
+    grad_mirror = jnp.where(low, swapped[1], swapped[0])
     mirror_out = dot(grad_mirror, weight, ((1,), (1,))).astype(bf16)
     mirror_back = exchange(mirror_out)
     own_back, mirror_back, grad_own, grad_mirror, gathered, my_x, my_lo, my_y, nil = (
@@ -248,11 +246,14 @@
 
     parts = 2
     routes = ((X, n_x, Y, n_y), (Y, n_y, X, n_x))
-    near = {}
-    for part in range(parts):
+    near = {(part, section): [None] * n_x for part in range(parts) for section in range(n_hi)}
+    turn = 0
+    for part, blocks in ((0, (1,)), (0, (n_x - 1,)), (0, (2, 0)), (1, (1, n_x - 1, 2, 0))):
         for section, (axis, size, _, _) in enumerate(routes):
-            sent = picked(keys, gathered, section, n_lo, count, slots, size, part, parts)
-            near[part, section] = [shifted(sent[i], axis, size, i) for i in range(size)]
+            sent = picked(keys, gathered, section, n_lo, count, slots, size, blocks, part, parts)
+            for block, value in zip(blocks, sent):
+                near[part, section][block] = shifted(value, axis, size, block)
+            turn += 1
 
     key_own = jnp.where(low, keys[2], keys[3])
     key_mirror = jnp.where(low, keys[3], keys[2])
@@ -268,6 +269,7 @@
     far = {}
     for part in range(parts):
         for section, (_, _, axis, size) in enumerate(routes):
+            turn = str(2 * part + section)
             turned = merged(near[part, section], slots)
             far[part, section] = [shifted(turned[i], axis, size, i) for i in range(size)]
 

time: 488 us -> 501 us (1.027)
  the two profiles are of different devices: /device:TPU:88 before, /device:TPU:104 now
where the time goes in v5:
time: 501 us; the launch traced here: 496 us
  waiting for transfers between devices  183 us (37%)
  blocking collectives  98.1 us (20%)
  starting transfers between devices  86.8 us (17%)
  Pallas kernels  58.7 us (12%)
  matrix products  36.9 us (7%)
  other arithmetic  15.9 us (3%)
  between operations  14.2 us (3%)
    all_to_all x1, blocking collectives, exchange(): return lax.all_to_all(value, (X, Y), 0, 0, tiled=True).reshape(rows, width)  98.1 us
    ppermute x24, waiting for transfers between devices, shifted(): lax.ppermute(value, axis, [(i, (i + by) % size) for i in range(size)])  92.6 us
    ppermute x24, starting transfers between devices, shifted(): lax.ppermute(value, axis, [(i, (i + by) % size) for i in range(size)])  79.3 us
    all_to_all x1, waiting for transfers between devices, exchange(): return lax.all_to_all(value, (X, Y), 0, 0, tiled=True).reshape(rows, width)  50 us
    all_gather x1, waiting for transfers between devices, on_device(): lax.all_gather(grad_send, pair, axis=0, axis_index_groups=mirror_pairs(si...  40.1 us
    dot_general x7, matrix products, dot(): lax.dot_general(a, b, (dims, ((), ())), preferred_element_type=jnp.float32)  36.9 us
    pallas_call x8, Pallas kernels, picked(): pl.pallas_call(functools.partial(pick_kernel, slots, per_out, blocks), ou...  27.5 us
    pallas_call x2, Pallas kernels, hidden_sum(): pl.pallas_call(hidden_sum_kernel, out_shape=jax.ShapeDtypeStruct((parts *...  16.7 us
  transfers between devices with their start and end apart: 28, of which 8 were waited for; matrix products, arithmetic and copies ran while one was open for 4% of the time, Pallas kernels for 12%

profile of v5, /device:TPU:104, one launch (start us, length us, event | category | flops | bytes accessed | tf_op | source)
XLA Modules:
  0.0 495.8 jit_solution(1979934383625954004)
XLA Ops:
  8.7 3.3 fusion.6
  15.9 7.5 %convolution_convert_fusion.1 = bf16[896,3584]{1,0:T(8,128)(2,1)} fusion(bf16[896,512]{1,0:T(8,128)(2,1)S(1)} %get-tuple-element.58, bf16[1,1,3584,512]{3,2,1,0:T(8,128)(2,1)} %param.6), kind=kOutput, calls=%fused_computation.2 | convolution fusion | flops 3291545600 | bytes 11010048 | tf_op jit(solution)/shard_map/dot_general | solution.py:35
  23.3 7.4 %all-to-all-start = ((bf16[16,56,3584]{2,1,0:T(8,128)(2,1)}), bf16[16,56,3584]{2,1,0:T(8,128)(2,1)}, u32[]{:S(2)}, u32[]{:S(2)}) async-start(bf16[16,56,3584]{2,1,0:T(8,128)(2,1)} %bitcast.58), calls=%async_computation | async-start | bytes 12845056 | tf_op jit(solution)/shard_map/all_to_all | solution.py:223
  30.8 40.1 %all-gather.6.cloned.1.call-done = bf16[1792,512]{1,0:T(8,128)(2,1)} async-done(((bf16[896,512]{1,0:T(8,128)(2,1)}), bf16[1792,512]{1,0:T(8,128)(2,1)}) %all-gather.6.cloned.1.call-update) | async-done | bytes 1835024 | tf_op jit(solution)/shard_map/all_gather | solution.py:215
  70.9 50.0 %all-to-all-done = bf16[16,56,3584]{2,1,0:T(8,128)(2,1)} async-done(((bf16[16,56,3584]{2,1,0:T(8,128)(2,1)}), bf16[16,56,3584]{2,1,0:T(8,128)(2,1)}, u32[]{:S(2)}, u32[]{:S(2)}) %all-to-all-start) | async-done | bytes 6422560 | tf_op jit(solution)/shard_map/all_to_all | solution.py:223
  122.5 5.9 %convolution_convert_fusion = bf16[896,3584]{1,0:T(8,128)(2,1)S(1)} fusion(bf16[896,512]{1,0:T(8,128)(2,1)S(1)} %select_bitcast_fusion, bf16[1,1,3584,512]{3,2,1,0:T(8,128)(2,1)} %param.6), kind=kOutput, calls=%fused_computation.1 | convolution fusion | flops 3291545600 | bytes 11010048 | tf_op jit(solution)/shard_map/dot_general | solution.py:35
  128.4 98.1 %all_to_all.10 = bf16[16,56,3584]{2,1,0:T(8,128)(2,1)} all-to-all(bf16[16,56,3584]{2,1,0:T(8,128)(2,1)S(1)} %bitcast.59), channel_id=1, replica_groups=mesh['hi'=2,'core'=2,'x'=4,'lo'=4,'y'=4] {'x','y'}, dimensions={0} | all-to-all | bytes 12845056 | tf_op jit(solution)/shard_map/all_to_all | solution.py:223
  230.1 7.1 %convolution_convert_fusion.2 = bf16[512,3584]{1,0:T(8,128)(2,1)S(1)} fusion(pred[896,512]{1,0:T(32,128)(4,1)S(1)} %get-tuple-element.95, bf16[896,3584]{1,0:T(8,128)(2,1)} %bitcast.57), kind=kOutput, calls=%fused_computation.3 | convolution fusion | flops 3290169344 | bytes 10551296 | tf_op jit(solution)/shard_map/dot_general | solution.py:35
  237.2 8.9 %broadcast_select_fusion.1 = (bf16[512,3584]{1,0:T(8,128)(2,1)}, bf16[512,3584]{1,0:T(8,128)(2,1)}) fusion(bf16[512,3584]{1,0:T(8,128)(2,1)S(1)} %convolution_convert_fusion.2, pred[]{:T(512)S(6)} %eq.86, pred[896,512]{1,0:T(32,128)(4,1)S(1)} %get-tuple-element.94, bf16[896,3584]{1,0:T(8,128)(2,1)} %bitcast.5), kind=kOutput, calls=%fused_computation.8 | convolution fusion | flops 3293839360 | bytes 17891328 | tf_op jit(solution)/shard_map/dot_general | solution.py:35
  246.1 6.6 %pad_maximum_fusion = bf16[1024,3584]{1,0:T(8,128)(2,1)} fusion(bf16[512,3584]{1,0:T(8,128)(2,1)} %get-tuple-element.89, bf16[512,3584]{1,0:T(8,128)(2,1)} %get-tuple-element.88), kind=kLoop, calls=%fused_computation | loop fusion | flops 14680064 | bytes 14680064 | tf_op jit(solution)/shard_map/concatenate | solution.py:262
  252.8 4.4 picked.8
  266.5 3.6 picked.10
  274.3 21.6 %collective-permute-done.refs_1_ = bf16[224,1792]{1,0:T(8,128)(2,1)S(1)} collective-permute-done((bf16[224,1792]{1,0:T(8,128)(2,1)}, bf16[224,1792]{1,0:T(8,128)(2,1)S(1)}, u32[]{:S(2)}, u32[]{:S(2)}) %collective-permute-start) | collective-permute-done | bytes 802848 | tf_op jit(solution)/shard_map/ppermute | solution.py:31
  296.0 3.5 picked.13
  299.5 2.9 picked.14
  302.9 3.9 collective-permute-start.19
  312.9 4.4 picked.9
  317.3 3.3 merged.4
  320.6 9.4 %collective-permute-done.13.refs_2_ = bf16[224,1792]{1,0:T(8,128)(2,1)} collective-permute-done((bf16[224,1792]{1,0:T(8,128)(2,1)}, bf16[224,1792]{1,0:T(8,128)(2,1)}, u32[]{:S(2)}, u32[]{:S(2)}) %collective-permute-start.13) | collective-permute-done | bytes 802848 | tf_op jit(solution)/shard_map/ppermute | solution.py:31
  332.0 3.2 merged.6
  339.4 3.3 merged.7
  342.7 24.9 %collective-permute-done.6.refs_1_ = bf16[224,1792]{1,0:T(8,128)(2,1)S(1)} collective-permute-done((bf16[224,1792]{1,0:T(8,128)(2,1)}, bf16[224,1792]{1,0:T(8,128)(2,1)S(1)}, u32[]{:S(2)}, u32[]{:S(2)}) %collective-permute-start.6) | collective-permute-done | bytes 802848 | tf_op jit(solution)/shard_map/ppermute | solution.py:31
  368.4 4.6 collective-permute-start.17
  373.0 27.5 %collective-permute-start.21 = (bf16[224,1792]{1,0:T(8,128)(2,1)}, bf16[224,1792]{1,0:T(8,128)(2,1)}, u32[]{:S(2)}, u32[]{:S(2)}) collective-permute-start(bf16[224,1792]{1,0:T(8,128)(2,1)} %get-tuple-element.85), channel_id=1, source_target_pairs={{0,16},{16,32},{32,48},{48,0},{1,17},{17,33},{33,49},{49,1},{2,18}... | collective-permute-start | bytes 2408456 | tf_op jit(solution)/shard_map/ppermute | solution.py:31
  402.9 14.1 %collective-permute-done.15.refs_2_ = bf16[224,1792]{1,0:T(8,128)(2,1)S(1)} collective-permute-done((bf16[224,1792]{1,0:T(8,128)(2,1)}, bf16[224,1792]{1,0:T(8,128)(2,1)S(1)}, u32[]{:S(2)}, u32[]{:S(2)}) %collective-permute-start.15) | collective-permute-done | bytes 802848 | tf_op jit(solution)/shard_map/ppermute | solution.py:31
  417.0 15.1 %collective-permute-start.23 = (bf16[224,1792]{1,0:T(8,128)(2,1)}, bf16[224,1792]{1,0:T(8,128)(2,1)}, u32[]{:S(2)}, u32[]{:S(2)}) collective-permute-start(bf16[224,1792]{1,0:T(8,128)(2,1)} %get-tuple-element.87), channel_id=1, source_target_pairs={{0,48},{16,0},{32,16},{48,32},{1,49},{17,1},{33,17},{49,33},{2,50}... | collective-permute-start | bytes 2408456 | tf_op jit(solution)/shard_map/ppermute | solution.py:31
  432.7 3.3 merged.5
  436.2 4.4 collective-permute-start.5
  442.1 20.9 %collective-permute-done.23.refs_8_ = bf16[224,1792]{1,0:T(8,128)(2,1)} collective-permute-done((bf16[224,1792]{1,0:T(8,128)(2,1)}, bf16[224,1792]{1,0:T(8,128)(2,1)}, u32[]{:S(2)}, u32[]{:S(2)}) %collective-permute-start.23) | collective-permute-done | bytes 802848 | tf_op jit(solution)/shard_map/ppermute | solution.py:31
  463.0 3.7 collective-permute-start.11
  472.3 8.3 %hidden_sum.2.refs_9_ = bf16[3584,512]{1,0:T(8,128)(2,1)} custom-call(bf16[8,224,512]{2,1,0:T(8,128)(2,1)} %bitcast.54, bf16[224,1792]{1,0:T(8,128)(2,1)} %get-tuple-element.78.refs_1_, bf16[224,1792]{1,0:T(8,128)(2,1)} %copy-done.4, bf16[224,1792]{1,0:T(8,128)(2,1)} %copy-done.5, bf16[224,1792]{1,0:T(8,128)(2,1)} %collective-permute-done.17.refs_4_, ...), custom_call_target="tpu_custom_call" | custom-call | tf_op jit(solution)/shard_map/hidden_sum/pallas_call | solution.py:55
  480.7 8.4 %hidden_sum.3 = bf16[3584,512]{1,0:T(8,128)(2,1)} custom-call(bf16[8,224,512]{2,1,0:T(8,128)(2,1)} %bitcast.55, bf16[224,1792]{1,0:T(8,128)(2,1)} %get-tuple-element.64.refs_1_, bf16[224,1792]{1,0:T(8,128)(2,1)} %collective-permute-done.3.refs_2_, bf16[224,1792]{1,0:T(8,128)(2,1)} %collective-permute-done.4.refs_3_, ...), custom_call_target="tpu_custom_call", output_to_operand_aliasing={{}: (9, {})} | custom-call | tf_op jit(solution)/shard_map/hidden_sum/pallas_call | solution.py:55
  (88 shorter events, 48.1 us)
Async XLA Ops:
  7.2 63.7 %all-gather.6.cloned.1.call-start = ((), (), s32[]{:S(2)}) async-start(), calls=%async_computation.5 | async-start | bytes 2752512 | tf_op jit(solution)/shard_map/all_gather | solution.py:215
  14.6 452.2 %copy-start.3 = (bf16[896,512]{1,0:T(8,128)(2,1)}, bf16[896,512]{1,0:T(8,128)(2,1)S(1)}, u32[]{:S(2)}) copy-start(bf16[896,512]{1,0:T(8,128)(2,1)S(1)} %get-tuple-element.58) | copy-start | bytes 2752516
  14.6 211.8 %all-gather.4.cloned.1.call-start = ((), (), s32[]{:S(2)}) async-start(), calls=%async_computation.3 | async-start | bytes 8773632 | tf_op jit(solution)/shard_map/all_gather | solution.py:219
  23.3 97.6 %all-to-all-start = ((bf16[16,56,3584]{2,1,0:T(8,128)(2,1)}), bf16[16,56,3584]{2,1,0:T(8,128)(2,1)}, u32[]{:S(2)}, u32[]{:S(2)}) async-start(bf16[16,56,3584]{2,1,0:T(8,128)(2,1)} %bitcast.58), calls=%async_computation | async-start | bytes 12845056 | tf_op jit(solution)/shard_map/all_to_all | solution.py:223
  30.7 458.3 %reduce-scatter.2.cloned.1.call-start = ((), (), s32[]{:S(2)}) async-start(), calls=%async_computation.4 | async-start | bytes 8257536 | tf_op jit(solution)/shard_map/reduce_scatter | solution.py:265
  257.2 38.7 %collective-permute-start = (bf16[224,1792]{1,0:T(8,128)(2,1)}, bf16[224,1792]{1,0:T(8,128)(2,1)S(1)}, u32[]{:S(2)}, u32[]{:S(2)}) collective-permute-start(bf16[224,1792]{1,0:T(8,128)(2,1)} %get-tuple-element.61), channel_id=1, source_target_pairs={{0,16},{16,32},{32,48},{48,0},{1,17},{17,33},{33,49},{49,1},{2,18}... | collective-permute-start | bytes 2408456 | tf_op jit(solution)/shard_map/ppermute | solution.py:31
  258.3 44.1 %collective-permute-start.1 = (bf16[224,1792]{1,0:T(8,128)(2,1)}, bf16[224,1792]{1,0:T(8,128)(2,1)}, u32[]{:S(2)}, u32[]{:S(2)}) collective-permute-start(bf16[224,1792]{1,0:T(8,128)(2,1)} %get-tuple-element.62), channel_id=1, source_target_pairs={{0,32},{16,48},{32,0},{48,16},{1,33},{17,49},{33,1},{49,17},{2,34}... | collective-permute-start | bytes 2408456 | tf_op jit(solution)/shard_map/ppermute | solution.py:31
  261.1 41.8 %collective-permute-start.2 = (bf16[224,1792]{1,0:T(8,128)(2,1)}, bf16[224,1792]{1,0:T(8,128)(2,1)}, u32[]{:S(2)}, u32[]{:S(2)}) collective-permute-start(bf16[224,1792]{1,0:T(8,128)(2,1)} %get-tuple-element.63), channel_id=1, source_target_pairs={{0,48},{16,0},{32,16},{48,32},{1,49},{17,1},{33,17},{49,33},{2,50}... | collective-permute-start | bytes 2408456 | tf_op jit(solution)/shard_map/ppermute | solution.py:31
  266.5 44.8 %collective-permute-start.12 = (bf16[224,1792]{1,0:T(8,128)(2,1)}, bf16[224,1792]{1,0:T(8,128)(2,1)S(1)}, u32[]{:S(2)}, u32[]{:S(2)}) collective-permute-start(bf16[224,1792]{1,0:T(8,128)(2,1)} %picked.11), channel_id=1, source_target_pairs={{0,16},{16,32},{32,48},{48,0},{1,17},{17,33},{33,49},{49,1},{2,18}... | collective-permute-start | bytes 2408456 | tf_op jit(solution)/shard_map/ppermute | solution.py:31
  270.2 59.8 %collective-permute-start.13 = (bf16[224,1792]{1,0:T(8,128)(2,1)}, bf16[224,1792]{1,0:T(8,128)(2,1)}, u32[]{:S(2)}, u32[]{:S(2)}) collective-permute-start(bf16[224,1792]{1,0:T(8,128)(2,1)} %get-tuple-element.77), channel_id=1, source_target_pairs={{0,32},{16,48},{32,0},{48,16},{1,33},{17,49},{33,1},{49,17},{2,34}... | collective-permute-start | bytes 2408456 | tf_op jit(solution)/shard_map/ppermute | solution.py:31
  295.9 36.0 %collective-permute-start.14 = (bf16[224,1792]{1,0:T(8,128)(2,1)}, bf16[224,1792]{1,0:T(8,128)(2,1)}, u32[]{:S(2)}, u32[]{:S(2)}) collective-permute-start(bf16[224,1792]{1,0:T(8,128)(2,1)} %picked.12), channel_id=1, source_target_pairs={{0,48},{16,0},{32,16},{48,32},{1,49},{17,1},{33,17},{49,33},{2,50}... | collective-permute-start | bytes 2408456 | tf_op jit(solution)/shard_map/ppermute | solution.py:31
  302.5 32.7 %collective-permute-start.18 = (bf16[224,1792]{1,0:T(8,128)(2,1)}, bf16[224,1792]{1,0:T(8,128)(2,1)S(1)}, u32[]{:S(2)}, u32[]{:S(2)}) collective-permute-start(bf16[224,1792]{1,0:T(8,128)(2,1)} %picked.14), channel_id=1, source_target_pairs={{0,1},{1,2},{2,3},{3,0},{4,5},{5,6},{6,7},{7,4},{8,9},{9,10},{10,1... | collective-permute-start | bytes 2408456 | tf_op jit(solution)/shard_map/ppermute | solution.py:31
  302.9 34.4 %collective-permute-start.19 = (bf16[224,1792]{1,0:T(8,128)(2,1)}, bf16[224,1792]{1,0:T(8,128)(2,1)}, u32[]{:S(2)}, u32[]{:S(2)}) collective-permute-start(bf16[224,1792]{1,0:T(8,128)(2,1)} %get-tuple-element.83), channel_id=1, source_target_pairs={{0,2},{1,3},{2,0},{3,1},{4,6},{5,7},{6,4},{7,5},{8,10},{9,11},{10,... | collective-permute-start | bytes 2408456 | tf_op jit(solution)/shard_map/ppermute | solution.py:31
  311.4 25.9 %collective-permute-start.20 = (bf16[224,1792]{1,0:T(8,128)(2,1)}, bf16[224,1792]{1,0:T(8,128)(2,1)}, u32[]{:S(2)}, u32[]{:S(2)}) collective-permute-start(bf16[224,1792]{1,0:T(8,128)(2,1)} %picked.15), channel_id=1, source_target_pairs={{0,3},{1,0},{2,1},{3,2},{4,7},{5,4},{6,5},{7,6},{8,11},{9,8},{10,9... | collective-permute-start | bytes 2408456 | tf_op jit(solution)/shard_map/ppermute | solution.py:31
  330.0 37.5 %collective-permute-start.6 = (bf16[224,1792]{1,0:T(8,128)(2,1)}, bf16[224,1792]{1,0:T(8,128)(2,1)S(1)}, u32[]{:S(2)}, u32[]{:S(2)}) collective-permute-start(bf16[224,1792]{1,0:T(8,128)(2,1)} %get-tuple-element.69), channel_id=1, source_target_pairs={{0,1},{1,2},{2,3},{3,0},{4,5},{5,6},{6,7},{7,4},{8,9},{9,10},{10,1... | collective-permute-start | bytes 2408456 | tf_op jit(solution)/shard_map/ppermute | solution.py:31
  331.9 36.5 %collective-permute-start.7 = (bf16[224,1792]{1,0:T(8,128)(2,1)}, bf16[224,1792]{1,0:T(8,128)(2,1)}, u32[]{:S(2)}, u32[]{:S(2)}) collective-permute-start(bf16[224,1792]{1,0:T(8,128)(2,1)} %get-tuple-element.70), channel_id=1, source_target_pairs={{0,2},{1,3},{2,0},{3,1},{4,6},{5,7},{6,4},{7,5},{8,10},{9,11},{10,... | collective-permute-start | bytes 2408456 | tf_op jit(solution)/shard_map/ppermute | solution.py:31
  335.2 37.8 %collective-permute-start.8 = (bf16[224,1792]{1,0:T(8,128)(2,1)}, bf16[224,1792]{1,0:T(8,128)(2,1)}, u32[]{:S(2)}, u32[]{:S(2)}) collective-permute-start(bf16[224,1792]{1,0:T(8,128)(2,1)} %get-tuple-element.71), channel_id=1, source_target_pairs={{0,3},{1,0},{2,1},{3,2},{4,7},{5,4},{6,5},{7,6},{8,11},{9,8},{10,9... | collective-permute-start | bytes 2408456 | tf_op jit(solution)/shard_map/ppermute | solution.py:31
  337.3 63.2 %collective-permute-start.3 = (bf16[224,1792]{1,0:T(8,128)(2,1)}, bf16[224,1792]{1,0:T(8,128)(2,1)}, u32[]{:S(2)}, u32[]{:S(2)}) collective-permute-start(bf16[224,1792]{1,0:T(8,128)(2,1)} %get-tuple-element.65), channel_id=1, source_target_pairs={{0,1},{1,2},{2,3},{3,0},{4,5},{5,6},{6,7},{7,4},{8,9},{9,10},{10,1... | collective-permute-start | bytes 2408456 | tf_op jit(solution)/shard_map/ppermute | solution.py:31
  337.3 79.7 %collective-permute-start.15 = (bf16[224,1792]{1,0:T(8,128)(2,1)}, bf16[224,1792]{1,0:T(8,128)(2,1)S(1)}, u32[]{:S(2)}, u32[]{:S(2)}) collective-permute-start(bf16[224,1792]{1,0:T(8,128)(2,1)} %get-tuple-element.79), channel_id=1, source_target_pairs={{0,1},{1,2},{2,3},{3,0},{4,5},{5,6},{6,7},{7,4},{8,9},{9,10},{10,1... | collective-permute-start | bytes 2408456 | tf_op jit(solution)/shard_map/ppermute | solution.py:31
  368.4 67.6 %collective-permute-start.16 = (bf16[224,1792]{1,0:T(8,128)(2,1)}, bf16[224,1792]{1,0:T(8,128)(2,1)S(1)}, u32[]{:S(2)}, u32[]{:S(2)}) collective-permute-start(bf16[224,1792]{1,0:T(8,128)(2,1)} %get-tuple-element.80), channel_id=1, source_target_pairs={{0,2},{1,3},{2,0},{3,1},{4,6},{5,7},{6,4},{7,5},{8,10},{9,11},{10,... | collective-permute-start | bytes 2408456 | tf_op jit(solution)/shard_map/ppermute | solution.py:31
  368.4 67.7 %collective-permute-start.17 = (bf16[224,1792]{1,0:T(8,128)(2,1)}, bf16[224,1792]{1,0:T(8,128)(2,1)}, u32[]{:S(2)}, u32[]{:S(2)}) collective-permute-start(bf16[224,1792]{1,0:T(8,128)(2,1)} %get-tuple-element.81), channel_id=1, source_target_pairs={{0,3},{1,0},{2,1},{3,2},{4,7},{5,4},{6,5},{7,6},{8,11},{9,8},{10,9... | collective-permute-start | bytes 2408456 | tf_op jit(solution)/shard_map/ppermute | solution.py:31
  373.0 67.6 %collective-permute-start.21 = (bf16[224,1792]{1,0:T(8,128)(2,1)}, bf16[224,1792]{1,0:T(8,128)(2,1)}, u32[]{:S(2)}, u32[]{:S(2)}) collective-permute-start(bf16[224,1792]{1,0:T(8,128)(2,1)} %get-tuple-element.85), channel_id=1, source_target_pairs={{0,16},{16,32},{32,48},{48,0},{1,17},{17,33},{33,49},{49,1},{2,18}... | collective-permute-start | bytes 2408456 | tf_op jit(solution)/shard_map/ppermute | solution.py:31
  400.5 40.1 %collective-permute-start.22 = (bf16[224,1792]{1,0:T(8,128)(2,1)}, bf16[224,1792]{1,0:T(8,128)(2,1)}, u32[]{:S(2)}, u32[]{:S(2)}) collective-permute-start(bf16[224,1792]{1,0:T(8,128)(2,1)} %get-tuple-element.86), channel_id=1, source_target_pairs={{0,32},{16,48},{32,0},{48,16},{1,33},{17,49},{33,1},{49,17},{2,34}... | collective-permute-start | bytes 2408456 | tf_op jit(solution)/shard_map/ppermute | solution.py:31
  417.0 51.6 %copy-start.4 = (bf16[224,1792]{1,0:T(8,128)(2,1)}, bf16[224,1792]{1,0:T(8,128)(2,1)S(1)}, u32[]{:S(2)}) copy-start(bf16[224,1792]{1,0:T(8,128)(2,1)S(1)} %collective-permute-done.15.refs_2_) | copy-start | bytes 2408452
  417.0 46.1 %collective-permute-start.23 = (bf16[224,1792]{1,0:T(8,128)(2,1)}, bf16[224,1792]{1,0:T(8,128)(2,1)}, u32[]{:S(2)}, u32[]{:S(2)}) collective-permute-start(bf16[224,1792]{1,0:T(8,128)(2,1)} %get-tuple-element.87), channel_id=1, source_target_pairs={{0,48},{16,0},{32,16},{48,32},{1,49},{17,1},{33,17},{49,33},{2,50}... | collective-permute-start | bytes 2408456 | tf_op jit(solution)/shard_map/ppermute | solution.py:31
  436.0 30.7 %copy-start.5 = (bf16[224,1792]{1,0:T(8,128)(2,1)}, bf16[224,1792]{1,0:T(8,128)(2,1)S(1)}, u32[]{:S(2)}) copy-start(bf16[224,1792]{1,0:T(8,128)(2,1)S(1)} %collective-permute-done.16.refs_3_) | copy-start | bytes 2408452
  436.1 44.6 %collective-permute-start.4 = (bf16[224,1792]{1,0:T(8,128)(2,1)}, bf16[224,1792]{1,0:T(8,128)(2,1)}, u32[]{:S(2)}, u32[]{:S(2)}) collective-permute-start(bf16[224,1792]{1,0:T(8,128)(2,1)} %get-tuple-element.66), channel_id=1, source_target_pairs={{0,2},{1,3},{2,0},{3,1},{4,6},{5,7},{6,4},{7,5},{8,10},{9,11},{10,... | collective-permute-start | bytes 2408456 | tf_op jit(solution)/shard_map/ppermute | solution.py:31
  436.2 44.5 %collective-permute-start.5 = (bf16[224,1792]{1,0:T(8,128)(2,1)}, bf16[224,1792]{1,0:T(8,128)(2,1)}, u32[]{:S(2)}, u32[]{:S(2)}) collective-permute-start(bf16[224,1792]{1,0:T(8,128)(2,1)} %get-tuple-element.67), channel_id=1, source_target_pairs={{0,3},{1,0},{2,1},{3,2},{4,7},{5,4},{6,5},{7,6},{8,11},{9,8},{10,9... | collective-permute-start | bytes 2408456 | tf_op jit(solution)/shard_map/ppermute | solution.py:31
  440.6 40.0 %collective-permute-start.9 = (bf16[224,1792]{1,0:T(8,128)(2,1)}, bf16[224,1792]{1,0:T(8,128)(2,1)}, u32[]{:S(2)}, u32[]{:S(2)}) collective-permute-start(bf16[224,1792]{1,0:T(8,128)(2,1)} %get-tuple-element.73), channel_id=1, source_target_pairs={{0,16},{16,32},{32,48},{48,0},{1,17},{17,33},{33,49},{49,1},{2,18}... | collective-permute-start | bytes 2408456 | tf_op jit(solution)/shard_map/ppermute | solution.py:31
  440.6 40.0 %collective-permute-start.10 = (bf16[224,1792]{1,0:T(8,128)(2,1)}, bf16[224,1792]{1,0:T(8,128)(2,1)}, u32[]{:S(2)}, u32[]{:S(2)}) collective-permute-start(bf16[224,1792]{1,0:T(8,128)(2,1)} %get-tuple-element.74), channel_id=1, source_target_pairs={{0,32},{16,48},{32,0},{48,16},{1,33},{17,49},{33,1},{49,17},{2,34}... | collective-permute-start | bytes 2408456 | tf_op jit(solution)/shard_map/ppermute | solution.py:31
  463.0 17.6 %collective-permute-start.11 = (bf16[224,1792]{1,0:T(8,128)(2,1)}, bf16[224,1792]{1,0:T(8,128)(2,1)}, u32[]{:S(2)}, u32[]{:S(2)}) collective-permute-start(bf16[224,1792]{1,0:T(8,128)(2,1)} %get-tuple-element.75), channel_id=1, source_target_pairs={{0,48},{16,0},{32,16},{48,32},{1,49},{17,1},{33,17},{49,33},{2,50}... | collective-permute-start | bytes 2408456 | tf_op jit(solution)/shard_map/ppermute | solution.py:31
  480.7 8.4 %copy-start.1 = (bf16[1,1,64,14,1024]{4,2,3,1,0:T(8,128)(2,1)S(1)}, bf16[1,1,64,14,1024]{4,2,3,1,0:T(8,128)(2,1)}, u32[]{:S(2)}) copy-start(bf16[1,1,64,14,1024]{4,2,3,1,0:T(8,128)(2,1)} %param.7) | copy-start | bytes 5505028
  (8 other events, 21.3 us)
Sparse Core Ops, SparseCore 0:
  14.7 56.1 all-gather.5
  73.3 88.2 all-gather.3
  252.9 86.6 reduce-scatter.1

commit v6 on v5

--- a/solution.py
+++ b/solution.py
@@ -129,6 +129,46 @@
         scratch_shapes=[pltpu.VMEM((len(blocks), shape[0], total), gathered.dtype)],
         name="picked",
     )(keys, gathered)
+
+
+def sum_kernel(slots, at, keys, rows, *refs):
+    out, chosen = refs[-2], refs[-1]
+    total = keys.shape[2]
+
+    @pl.when(pl.program_id(0) == 0)
+    def _():
+        slot = lax.broadcasted_iota(jnp.int32, (slots, total), 0)
+        some = [
+            jnp.where(keys[0, m : m + 1, :] == slot, 1.0, 0.0) for m in range(keys.shape[1])
+        ]
+        chosen[...] = jnp.concatenate(some).T.astype(chosen.dtype)
+
+    found = jnp.dot(chosen[...], rows[...], preferred_element_type=jnp.float32)
+    out[...] = found.astype(out.dtype)
+
+
+def token_sums(section, keys, rows, slots, before):
+    count, width = rows.shape
+    total = keys.shape[2]
+    tile = width // 4 if width % 512 == 0 else width
+    given = [] if before is None else [before]
+    return pl.pallas_call(
+        functools.partial(sum_kernel, slots),
+        out_shape=jax.ShapeDtypeStruct((2 * total, width), rows.dtype),
+        grid_spec=pltpu.PrefetchScalarGridSpec(
+            num_scalar_prefetch=1,
+            grid=(width // tile,),
+            in_specs=[
+                pl.BlockSpec((1, keys.shape[1], total), lambda i, at: (2 + at[0], 0, 0)),
+                pl.BlockSpec((count, tile), lambda i, at: (0, i)),
+            ]
+            + [pl.BlockSpec(memory_space=pl.ANY)] * len(given),
+            out_specs=pl.BlockSpec((total, tile), lambda i, at: (at[0], i)),
+            scratch_shapes=[pltpu.VMEM((total, count), rows.dtype)],
+        ),
+        input_output_aliases={3: 0} if given else {},
+        name="token_sums",
+    )(section, keys, rows, *given)
 
 
 def key_kernel(sizes, most, top, place, ids, out, named_all):
@@ -222,46 +262,42 @@
         value = value.reshape(plane, slots, width)
         return lax.all_to_all(value, (X, Y), 0, 0, tiled=True).reshape(rows, width)
 
-    my_x, my_lo, my_y = lax.axis_index(X), lax.axis_index(LO), lax.axis_index(Y)
+    my_hi, my_x = lax.axis_index(HI), lax.axis_index(X)
+    my_lo, my_y = lax.axis_index(LO), lax.axis_index(Y)
     own_out = dot(grad_own, weight, ((1,), (1,))).astype(bf16)
-    own_out, my_x, my_lo, my_y = lax.optimization_barrier((own_out, my_x, my_lo, my_y))
+    own_out, my_hi, my_x, my_lo, my_y = lax.optimization_barrier(
+        (own_out, my_hi, my_x, my_lo, my_y)
+    )
     own_back = exchange(own_out)
     own_back, swapped = lax.optimization_barrier((own_back, swapped))
     grad_mirror = jnp.where(low, swapped[1], swapped[0])
     mirror_out = dot(grad_mirror, weight, ((1,), (1,))).astype(bf16)
     mirror_back = exchange(mirror_out)
-    own_back, mirror_back, grad_own, grad_mirror, gathered, my_x, my_lo, my_y, nil = (
-        lax.optimization_barrier(
-            (own_back, mirror_back, grad_own, grad_mirror, gathered, my_x, my_lo, my_y, jnp.int32(0))
-        )
+    own_back, mirror_back, grad_own, grad_mirror, gathered = lax.optimization_barrier(
+        (own_back, mirror_back, grad_own, grad_mirror, gathered)
+    )
+    _, my_hi, my_x, my_lo, my_y, nil = lax.optimization_barrier(
+        (mirror_back, my_hi, my_x, my_lo, my_y, jnp.int32(0))
     )
 
     gathered = gathered.reshape(n_hi * n_lo, count + spare, width)
     position = jnp.stack([my_x, my_lo, my_y]).astype(jnp.int32)
     keys = key_table(sizes, most, top, count, position, gathered)
-
-    def selector(some):
-        slot = (jnp.arange(slots, dtype=jnp.int32) + nil)[None, :, None]
-        return (some[:, None, :] == slot).astype(bf16).reshape(-1, some.shape[1])
 
     parts = 2
     routes = ((X, n_x, Y, n_y), (Y, n_y, X, n_x))
     near = {(part, section): [None] * n_x for part in range(parts) for section in range(n_hi)}
     turn = 0
-    for part, blocks in ((0, (1,)), (0, (n_x - 1,)), (0, (2, 0)), (1, (1, n_x - 1, 2, 0))):
+    for part, blocks in ((0, (1, n_x - 1, 2, 0)), (1, (1, n_x - 1, 2, 0))):
         for section, (axis, size, _, _) in enumerate(routes):
             sent = picked(keys, gathered, section, n_lo, count, slots, size, blocks, part, parts)
             for block, value in zip(blocks, sent):
                 near[part, section][block] = shifted(value, axis, size, block)
             turn += 1
 
-    key_own = jnp.where(low, keys[2], keys[3])
-    key_mirror = jnp.where(low, keys[3], keys[2])
-    sums_own = dot(selector(key_own), own_back, ((0,), (0,))).astype(bf16)
-    sums_mirror = dot(selector(key_mirror), mirror_back, ((0,), (0,))).astype(bf16)
-    sums = jnp.concatenate(
-        [jnp.where(low, sums_own, sums_mirror), jnp.where(low, sums_mirror, sums_own)]
-    )
+    section = jnp.reshape(my_hi, (1,)).astype(jnp.int32)
+    sums = token_sums(section, keys, own_back, slots, None)
+    sums = token_sums(1 - section, keys, mirror_back, slots, sums)
     token_grad = lax.psum_scatter(
         sums, ring_axes, scatter_dimension=0, axis_index_groups=rings, tiled=True
     )

time: 501 us -> 444 us (0.89)
  the two profiles are of different devices: /device:TPU:104 before, /device:TPU:114 now
where the time goes in v6:
time: 444 us
  waiting for transfers between devices  162 us (36%)
  blocking collectives  105 us (24%)
  starting transfers between devices  68.1 us (15%)
  Pallas kernels  65.7 us (15%)
  matrix products  19.1 us (4%)
  between operations  13.9 us (3%)
  other arithmetic  7.79 us (2%)
    all_to_all x1, blocking collectives, exchange(): return lax.all_to_all(value, (X, Y), 0, 0, tiled=True).reshape(rows, width)  105 us
    ppermute x24, waiting for transfers between devices, shifted(): lax.ppermute(value, axis, [(i, (i + by) % size) for i in range(size)])  80.5 us
    ppermute x24, starting transfers between devices, shifted(): lax.ppermute(value, axis, [(i, (i + by) % size) for i in range(size)])  60.7 us
    all_to_all x1, waiting for transfers between devices, exchange(): return lax.all_to_all(value, (X, Y), 0, 0, tiled=True).reshape(rows, width)  41.5 us
    all_gather x1, waiting for transfers between devices, on_device(): lax.all_gather(grad_send, pair, axis=0, axis_index_groups=mirror_pairs(si...  40.2 us
    dot_general x5, matrix products, dot(): lax.dot_general(a, b, (dims, ((), ())), preferred_element_type=jnp.float32)  19.1 us
    pallas_call x4, Pallas kernels, picked(): pl.pallas_call(functools.partial(pick_kernel, slots, per_out, blocks), ou...  18 us
    pallas_call x2, Pallas kernels, hidden_sum(): pl.pallas_call(hidden_sum_kernel, out_shape=jax.ShapeDtypeStruct((parts *...  16.6 us
  transfers between devices with their start and end apart: 28, of which 14 were waited for; matrix products, arithmetic and copies ran while one was open for 5% of the time, Pallas kernels for 11%

profile of v6, /device:TPU:114, one launch (start us, length us, event | category | flops | bytes accessed | tf_op | source)
XLA Modules:
  0.0 443.8 jit_solution(13012473314867081837)
XLA Ops:
  8.7 3.3 fusion.6
  15.7 7.6 %convolution_convert_fusion.1 = bf16[896,3584]{1,0:T(8,128)(2,1)} fusion(bf16[896,512]{1,0:T(8,128)(2,1)S(1)} %get-tuple-element.66, bf16[1,1,3584,512]{3,2,1,0:T(8,128)(2,1)} %param.6), kind=kOutput, calls=%fused_computation.1 | convolution fusion | flops 3291545600 | bytes 11010048 | tf_op jit(solution)/shard_map/dot_general | solution.py:35
  23.3 7.2 %all-to-all-start = ((bf16[16,56,3584]{2,1,0:T(8,128)(2,1)}), bf16[16,56,3584]{2,1,0:T(8,128)(2,1)}, u32[]{:S(2)}, u32[]{:S(2)}) async-start(bf16[16,56,3584]{2,1,0:T(8,128)(2,1)} %bitcast.43), calls=%async_computation | async-start | bytes 12845056 | tf_op jit(solution)/shard_map/all_to_all | solution.py:263
  30.6 40.2 %all-gather.6.cloned.1.call-done = bf16[1792,512]{1,0:T(8,128)(2,1)} async-done(((bf16[896,512]{1,0:T(8,128)(2,1)}), bf16[1792,512]{1,0:T(8,128)(2,1)}) %all-gather.6.cloned.1.call-update) | async-done | bytes 1835024 | tf_op jit(solution)/shard_map/all_gather | solution.py:255
  70.8 41.5 %all-to-all-done = bf16[16,56,3584]{2,1,0:T(8,128)(2,1)} async-done(((bf16[16,56,3584]{2,1,0:T(8,128)(2,1)}), bf16[16,56,3584]{2,1,0:T(8,128)(2,1)}, u32[]{:S(2)}, u32[]{:S(2)}) %all-to-all-start) | async-done | bytes 6422560 | tf_op jit(solution)/shard_map/all_to_all | solution.py:263
  113.9 5.8 %convolution_convert_fusion = bf16[896,3584]{1,0:T(8,128)(2,1)S(1)} fusion(bf16[896,512]{1,0:T(8,128)(2,1)S(1)} %select_bitcast_fusion, bf16[1,1,3584,512]{3,2,1,0:T(8,128)(2,1)} %param.6), kind=kOutput, calls=%fused_computation | convolution fusion | flops 3291545600 | bytes 11010048 | tf_op jit(solution)/shard_map/dot_general | solution.py:35
  119.7 105.4 %all_to_all.10 = bf16[16,56,3584]{2,1,0:T(8,128)(2,1)} all-to-all(bf16[16,56,3584]{2,1,0:T(8,128)(2,1)S(1)} %bitcast.44), channel_id=1, replica_groups=mesh['hi'=2,'core'=2,'x'=4,'lo'=4,'y'=4] {'x','y'}, dimensions={0} | all-to-all | bytes 12845056 | tf_op jit(solution)/shard_map/all_to_all | solution.py:263
  227.3 8.3 %token_sums.2.refs_0_ = bf16[1024,3584]{1,0:T(8,128)(2,1)} custom-call(s32[1]{0:T(128)} %bitcast.13.at, s32[4,16,512]{2,1,0:T(8,128)} %key_table.1.keys, bf16[896,3584]{1,0:T(8,128)(2,1)} %bitcast.5.rows), custom_call_target="tpu_custom_call" | custom-call | tf_op jit(solution)/shard_map/token_sums/pallas_call | solution.py:155
  235.5 8.3 %token_sums.3 = bf16[1024,3584]{1,0:T(8,128)(2,1)} custom-call(s32[1]{0:T(128)S(6)} %sub.64.at, s32[4,16,512]{2,1,0:T(8,128)} %key_table.1.keys, bf16[896,3584]{1,0:T(8,128)(2,1)} %bitcast.39, bf16[1024,3584]{1,0:T(8,128)(2,1)} %token_sums.2.refs_0_), custom_call_target="tpu_custom_call", output_to_operand_aliasing={{}: (3, {})} | custom-call | tf_op jit(solution)/shard_map/token_sums/pallas_call | solution.py:155
  243.9 4.4 %picked.7 = (bf16[224,1792]{1,0:T(8,128)(2,1)}, bf16[224,1792]{1,0:T(8,128)(2,1)}, bf16[224,1792]{1,0:T(8,128)(2,1)}, bf16[224,1792]{1,0:T(8,128)(2,1)}) custom-call(s32[4,16,512]{2,1,0:T(8,128)} %key_table.1.keys, bf16[8,136,3584]{2,1,0:T(8,128)(2,1)} %bitcast.35), custom_call_target="tpu_custom_call" | custom-call | tf_op jit(solution)/shard_map/picked/pallas_call | solution.py:120
  253.0 4.4 picked.6
  258.1 4.7 %picked.5 = (bf16[224,1792]{1,0:T(8,128)(2,1)}, bf16[224,1792]{1,0:T(8,128)(2,1)}, bf16[224,1792]{1,0:T(8,128)(2,1)}, bf16[224,1792]{1,0:T(8,128)(2,1)}) custom-call(s32[4,16,512]{2,1,0:T(8,128)} %key_table.1.keys, bf16[8,136,3584]{2,1,0:T(8,128)(2,1)} %bitcast.37), custom_call_target="tpu_custom_call" | custom-call | tf_op jit(solution)/shard_map/picked/pallas_call | solution.py:120
  265.1 4.0 collective-permute-done.18.refs_1_
  270.4 13.4 %collective-permute-done.19.refs_2_ = bf16[224,1792]{1,0:T(8,128)(2,1)} collective-permute-done((bf16[224,1792]{1,0:T(8,128)(2,1)}, bf16[224,1792]{1,0:T(8,128)(2,1)}, u32[]{:S(2)}, u32[]{:S(2)}) %collective-permute-start.19) | collective-permute-done | bytes 802848 | tf_op jit(solution)/shard_map/ppermute | solution.py:31
  287.0 4.0 collective-permute-done.12.refs_1_
  293.0 4.4 picked.4
  297.4 3.2 merged.7
  307.5 10.4 %collective-permute-done.7.refs_2_ = bf16[224,1792]{1,0:T(8,128)(2,1)} collective-permute-done((bf16[224,1792]{1,0:T(8,128)(2,1)}, bf16[224,1792]{1,0:T(8,128)(2,1)}, u32[]{:S(2)}, u32[]{:S(2)}) %collective-permute-start.7) | collective-permute-done | bytes 802848 | tf_op jit(solution)/shard_map/ppermute | solution.py:31
  317.9 5.5 %collective-permute-start.21 = (bf16[224,1792]{1,0:T(8,128)(2,1)}, bf16[224,1792]{1,0:T(8,128)(2,1)S(1)}, u32[]{:S(2)}, u32[]{:S(2)}) collective-permute-start(bf16[224,1792]{1,0:T(8,128)(2,1)} %get-tuple-element.97), channel_id=1, source_target_pairs={{0,16},{16,32},{32,48},{48,0},{1,17},{17,33},{33,49},{49,1},{2,18}... | collective-permute-start | bytes 2408456 | tf_op jit(solution)/shard_map/ppermute | solution.py:31
  325.5 3.3 merged.6
  328.8 3.3 merged.5
  335.1 4.2 collective-permute-start.15
  339.2 3.8 collective-permute-done.2.refs_3_
  343.1 18.1 %collective-permute-start.16 = (bf16[224,1792]{1,0:T(8,128)(2,1)}, bf16[224,1792]{1,0:T(8,128)(2,1)}, u32[]{:S(2)}, u32[]{:S(2)}) collective-permute-start(bf16[224,1792]{1,0:T(8,128)(2,1)} %get-tuple-element.90), channel_id=1, source_target_pairs={{0,2},{1,3},{2,0},{3,1},{4,6},{5,7},{6,4},{7,5},{8,10},{9,11},{10,... | collective-permute-start | bytes 2408456 | tf_op jit(solution)/shard_map/ppermute | solution.py:31
  361.2 6.4 %collective-permute-done.21.refs_6_ = bf16[224,1792]{1,0:T(8,128)(2,1)S(1)} collective-permute-done((bf16[224,1792]{1,0:T(8,128)(2,1)}, bf16[224,1792]{1,0:T(8,128)(2,1)S(1)}, u32[]{:S(2)}, u32[]{:S(2)}) %collective-permute-start.21) | collective-permute-done | bytes 802848 | tf_op jit(solution)/shard_map/ppermute | solution.py:31
  367.5 5.0 %collective-permute-start.17 = (bf16[224,1792]{1,0:T(8,128)(2,1)}, bf16[224,1792]{1,0:T(8,128)(2,1)}, u32[]{:S(2)}, u32[]{:S(2)}) collective-permute-start(bf16[224,1792]{1,0:T(8,128)(2,1)} %get-tuple-element.91), channel_id=1, source_target_pairs={{0,3},{1,0},{2,1},{3,2},{4,7},{5,4},{6,5},{7,6},{8,11},{9,8},{10,9... | collective-permute-start | bytes 2408456 | tf_op jit(solution)/shard_map/ppermute | solution.py:31
  375.6 3.2 merged.4
  381.0 9.1 %collective-permute-done.17.refs_4_ = bf16[224,1792]{1,0:T(8,128)(2,1)} collective-permute-done((bf16[224,1792]{1,0:T(8,128)(2,1)}, bf16[224,1792]{1,0:T(8,128)(2,1)}, u32[]{:S(2)}, u32[]{:S(2)}) %collective-permute-start.17) | collective-permute-done | bytes 802848 | tf_op jit(solution)/shard_map/ppermute | solution.py:31
  390.1 15.5 %collective-permute-done.9.refs_6_ = bf16[224,1792]{1,0:T(8,128)(2,1)} collective-permute-done((bf16[224,1792]{1,0:T(8,128)(2,1)}, bf16[224,1792]{1,0:T(8,128)(2,1)}, u32[]{:S(2)}, u32[]{:S(2)}) %collective-permute-start.9) | collective-permute-done | bytes 802848 | tf_op jit(solution)/shard_map/ppermute | solution.py:31
  410.2 8.3 %hidden_sum.2.refs_9_ = bf16[3584,512]{1,0:T(8,128)(2,1)} custom-call(bf16[8,224,512]{2,1,0:T(8,128)(2,1)} %bitcast.40, bf16[224,1792]{1,0:T(8,128)(2,1)} %get-tuple-element.88.refs_1_, bf16[224,1792]{1,0:T(8,128)(2,1)} %collective-permute-done.15.refs_2_, bf16[224,1792]{1,0:T(8,128)(2,1)} %collective-permute-done.16.refs_3_, ...), custom_call_target="tpu_custom_call" | custom-call | tf_op jit(solution)/shard_map/hidden_sum/pallas_call | solution.py:55
  418.5 10.3 %collective-permute-done.5.refs_4_ = bf16[224,1792]{1,0:T(8,128)(2,1)} collective-permute-done((bf16[224,1792]{1,0:T(8,128)(2,1)}, bf16[224,1792]{1,0:T(8,128)(2,1)}, u32[]{:S(2)}, u32[]{:S(2)}) %collective-permute-start.5) | collective-permute-done | bytes 802848 | tf_op jit(solution)/shard_map/ppermute | solution.py:31
  428.8 8.4 %hidden_sum.3 = bf16[3584,512]{1,0:T(8,128)(2,1)} custom-call(bf16[8,224,512]{2,1,0:T(8,128)(2,1)} %bitcast.41, bf16[224,1792]{1,0:T(8,128)(2,1)} %get-tuple-element.72.refs_1_, bf16[224,1792]{1,0:T(8,128)(2,1)} %collective-permute-done.3.refs_2_, bf16[224,1792]{1,0:T(8,128)(2,1)} %collective-permute-done.4.refs_3_, ...), custom_call_target="tpu_custom_call", output_to_operand_aliasing={{}: (9, {})} | custom-call | tf_op jit(solution)/shard_map/hidden_sum/pallas_call | solution.py:55
  (72 shorter events, 45.0 us)
Async XLA Ops:
  7.2 63.6 %all-gather.6.cloned.1.call-start = ((), (), s32[]{:S(2)}) async-start(), calls=%async_computation.5 | async-start | bytes 2752512 | tf_op jit(solution)/shard_map/all_gather | solution.py:255
  14.6 210.5 %all-gather.4.cloned.1.call-start = ((), (), s32[]{:S(2)}) async-start(), calls=%async_computation.3 | async-start | bytes 8773632 | tf_op jit(solution)/shard_map/all_gather | solution.py:259
  23.3 89.0 %all-to-all-start = ((bf16[16,56,3584]{2,1,0:T(8,128)(2,1)}), bf16[16,56,3584]{2,1,0:T(8,128)(2,1)}, u32[]{:S(2)}, u32[]{:S(2)}) async-start(bf16[16,56,3584]{2,1,0:T(8,128)(2,1)} %bitcast.43), calls=%async_computation | async-start | bytes 12845056 | tf_op jit(solution)/shard_map/all_to_all | solution.py:263
  30.6 406.6 %reduce-scatter.2.cloned.1.call-start = ((), (), s32[]{:S(2)}) async-start(), calls=%async_computation.4 | async-start | bytes 8257536 | tf_op jit(solution)/shard_map/reduce_scatter | solution.py:301
  248.3 20.8 %collective-permute-start.18 = (bf16[224,1792]{1,0:T(8,128)(2,1)}, bf16[224,1792]{1,0:T(8,128)(2,1)}, u32[]{:S(2)}, u32[]{:S(2)}) collective-permute-start(bf16[224,1792]{1,0:T(8,128)(2,1)} %get-tuple-element.93), channel_id=1, source_target_pairs={{0,1},{1,2},{2,3},{3,0},{4,5},{5,6},{6,7},{7,4},{8,9},{9,10},{10,1... | collective-permute-start | bytes 2408456 | tf_op jit(solution)/shard_map/ppermute | solution.py:31
  249.3 34.5 %collective-permute-start.19 = (bf16[224,1792]{1,0:T(8,128)(2,1)}, bf16[224,1792]{1,0:T(8,128)(2,1)}, u32[]{:S(2)}, u32[]{:S(2)}) collective-permute-start(bf16[224,1792]{1,0:T(8,128)(2,1)} %get-tuple-element.94), channel_id=1, source_target_pairs={{0,2},{1,3},{2,0},{3,1},{4,6},{5,7},{6,4},{7,5},{8,10},{9,11},{10,... | collective-permute-start | bytes 2408456 | tf_op jit(solution)/shard_map/ppermute | solution.py:31
  250.8 34.1 %collective-permute-start.20 = (bf16[224,1792]{1,0:T(8,128)(2,1)}, bf16[224,1792]{1,0:T(8,128)(2,1)}, u32[]{:S(2)}, u32[]{:S(2)}) collective-permute-start(bf16[224,1792]{1,0:T(8,128)(2,1)} %get-tuple-element.95), channel_id=1, source_target_pairs={{0,3},{1,0},{2,1},{3,2},{4,7},{5,4},{6,5},{7,6},{8,11},{9,8},{10,9... | collective-permute-start | bytes 2408456 | tf_op jit(solution)/shard_map/ppermute | solution.py:31
  257.4 33.6 %collective-permute-start.12 = (bf16[224,1792]{1,0:T(8,128)(2,1)}, bf16[224,1792]{1,0:T(8,128)(2,1)S(1)}, u32[]{:S(2)}, u32[]{:S(2)}) collective-permute-start(bf16[224,1792]{1,0:T(8,128)(2,1)} %get-tuple-element.85), channel_id=1, source_target_pairs={{0,16},{16,32},{32,48},{48,0},{1,17},{17,33},{33,49},{49,1},{2,18}... | collective-permute-start | bytes 2408456 | tf_op jit(solution)/shard_map/ppermute | solution.py:31
  262.8 37.9 %collective-permute-start.13 = (bf16[224,1792]{1,0:T(8,128)(2,1)}, bf16[224,1792]{1,0:T(8,128)(2,1)S(1)}, u32[]{:S(2)}, u32[]{:S(2)}) collective-permute-start(bf16[224,1792]{1,0:T(8,128)(2,1)} %get-tuple-element.86), channel_id=1, source_target_pairs={{0,32},{16,48},{32,0},{48,16},{1,33},{17,49},{33,1},{49,17},{2,34}... | collective-permute-start | bytes 2408456 | tf_op jit(solution)/shard_map/ppermute | solution.py:31
  269.1 34.1 %collective-permute-start.14 = (bf16[224,1792]{1,0:T(8,128)(2,1)}, bf16[224,1792]{1,0:T(8,128)(2,1)}, u32[]{:S(2)}, u32[]{:S(2)}) collective-permute-start(bf16[224,1792]{1,0:T(8,128)(2,1)} %get-tuple-element.87), channel_id=1, source_target_pairs={{0,48},{16,0},{32,16},{48,32},{1,49},{17,1},{33,17},{49,33},{2,50}... | collective-permute-start | bytes 2408456 | tf_op jit(solution)/shard_map/ppermute | solution.py:31
  283.8 21.7 %collective-permute-start.6 = (bf16[224,1792]{1,0:T(8,128)(2,1)}, bf16[224,1792]{1,0:T(8,128)(2,1)}, u32[]{:S(2)}, u32[]{:S(2)}) collective-permute-start(bf16[224,1792]{1,0:T(8,128)(2,1)} %get-tuple-element.77), channel_id=1, source_target_pairs={{0,1},{1,2},{2,3},{3,0},{4,5},{5,6},{6,7},{7,4},{8,9},{9,10},{10,1... | collective-permute-start | bytes 2408456 | tf_op jit(solution)/shard_map/ppermute | solution.py:31
  285.0 33.0 %collective-permute-start.7 = (bf16[224,1792]{1,0:T(8,128)(2,1)}, bf16[224,1792]{1,0:T(8,128)(2,1)}, u32[]{:S(2)}, u32[]{:S(2)}) collective-permute-start(bf16[224,1792]{1,0:T(8,128)(2,1)} %get-tuple-element.78), channel_id=1, source_target_pairs={{0,2},{1,3},{2,0},{3,1},{4,6},{5,7},{6,4},{7,5},{8,10},{9,11},{10,... | collective-permute-start | bytes 2408456 | tf_op jit(solution)/shard_map/ppermute | solution.py:31
  290.9 32.9 %collective-permute-start.8 = (bf16[224,1792]{1,0:T(8,128)(2,1)}, bf16[224,1792]{1,0:T(8,128)(2,1)}, u32[]{:S(2)}, u32[]{:S(2)}) collective-permute-start(bf16[224,1792]{1,0:T(8,128)(2,1)} %get-tuple-element.79), channel_id=1, source_target_pairs={{0,3},{1,0},{2,1},{3,2},{4,7},{5,4},{6,5},{7,6},{8,11},{9,8},{10,9... | collective-permute-start | bytes 2408456 | tf_op jit(solution)/shard_map/ppermute | solution.py:31
  300.7 17.3 %copy-start.6 = (bf16[224,1792]{1,0:T(8,128)(2,1)}, bf16[224,1792]{1,0:T(8,128)(2,1)S(1)}, u32[]{:S(2)}) copy-start(bf16[224,1792]{1,0:T(8,128)(2,1)S(1)} %collective-permute-done.13.refs_2_) | copy-start | bytes 2408452
  300.7 31.4 %collective-permute-start = (bf16[224,1792]{1,0:T(8,128)(2,1)}, bf16[224,1792]{1,0:T(8,128)(2,1)}, u32[]{:S(2)}, u32[]{:S(2)}) collective-permute-start(bf16[224,1792]{1,0:T(8,128)(2,1)} %get-tuple-element.69), channel_id=1, source_target_pairs={{0,16},{16,32},{32,48},{48,0},{1,17},{17,33},{33,49},{49,1},{2,18}... | collective-permute-start | bytes 2408456 | tf_op jit(solution)/shard_map/ppermute | solution.py:31
  303.2 31.9 %collective-permute-start.1 = (bf16[224,1792]{1,0:T(8,128)(2,1)}, bf16[224,1792]{1,0:T(8,128)(2,1)}, u32[]{:S(2)}, u32[]{:S(2)}) collective-permute-start(bf16[224,1792]{1,0:T(8,128)(2,1)} %get-tuple-element.70), channel_id=1, source_target_pairs={{0,32},{16,48},{32,0},{48,16},{1,33},{17,49},{33,1},{49,17},{2,34}... | collective-permute-start | bytes 2408456 | tf_op jit(solution)/shard_map/ppermute | solution.py:31
  305.5 37.5 %collective-permute-start.2 = (bf16[224,1792]{1,0:T(8,128)(2,1)}, bf16[224,1792]{1,0:T(8,128)(2,1)}, u32[]{:S(2)}, u32[]{:S(2)}) collective-permute-start(bf16[224,1792]{1,0:T(8,128)(2,1)} %get-tuple-element.71), channel_id=1, source_target_pairs={{0,48},{16,0},{32,16},{48,32},{1,49},{17,1},{33,17},{49,33},{2,50}... | collective-permute-start | bytes 2408456 | tf_op jit(solution)/shard_map/ppermute | solution.py:31
  317.9 49.6 %collective-permute-start.21 = (bf16[224,1792]{1,0:T(8,128)(2,1)}, bf16[224,1792]{1,0:T(8,128)(2,1)S(1)}, u32[]{:S(2)}, u32[]{:S(2)}) collective-permute-start(bf16[224,1792]{1,0:T(8,128)(2,1)} %get-tuple-element.97), channel_id=1, source_target_pairs={{0,16},{16,32},{32,48},{48,0},{1,17},{17,33},{33,49},{49,1},{2,18}... | collective-permute-start | bytes 2408456 | tf_op jit(solution)/shard_map/ppermute | solution.py:31
  323.8 48.8 %collective-permute-start.22 = (bf16[224,1792]{1,0:T(8,128)(2,1)}, bf16[224,1792]{1,0:T(8,128)(2,1)S(1)}, u32[]{:S(2)}, u32[]{:S(2)}) collective-permute-start(bf16[224,1792]{1,0:T(8,128)(2,1)} %get-tuple-element.98), channel_id=1, source_target_pairs={{0,32},{16,48},{32,0},{48,16},{1,33},{17,49},{33,1},{49,17},{2,34}... | collective-permute-start | bytes 2408456 | tf_op jit(solution)/shard_map/ppermute | solution.py:31
  332.1 46.7 %collective-permute-start.23 = (bf16[224,1792]{1,0:T(8,128)(2,1)}, bf16[224,1792]{1,0:T(8,128)(2,1)}, u32[]{:S(2)}, u32[]{:S(2)}) collective-permute-start(bf16[224,1792]{1,0:T(8,128)(2,1)} %get-tuple-element.99), channel_id=1, source_target_pairs={{0,48},{16,0},{32,16},{48,32},{1,49},{17,1},{33,17},{49,33},{2,50}... | collective-permute-start | bytes 2408456 | tf_op jit(solution)/shard_map/ppermute | solution.py:31
  335.1 43.8 %collective-permute-start.15 = (bf16[224,1792]{1,0:T(8,128)(2,1)}, bf16[224,1792]{1,0:T(8,128)(2,1)}, u32[]{:S(2)}, u32[]{:S(2)}) collective-permute-start(bf16[224,1792]{1,0:T(8,128)(2,1)} %get-tuple-element.89), channel_id=1, source_target_pairs={{0,1},{1,2},{2,3},{3,0},{4,5},{5,6},{6,7},{7,4},{8,9},{9,10},{10,1... | collective-permute-start | bytes 2408456 | tf_op jit(solution)/shard_map/ppermute | solution.py:31
  343.1 38.0 %collective-permute-start.16 = (bf16[224,1792]{1,0:T(8,128)(2,1)}, bf16[224,1792]{1,0:T(8,128)(2,1)}, u32[]{:S(2)}, u32[]{:S(2)}) collective-permute-start(bf16[224,1792]{1,0:T(8,128)(2,1)} %get-tuple-element.90), channel_id=1, source_target_pairs={{0,2},{1,3},{2,0},{3,1},{4,6},{5,7},{6,4},{7,5},{8,10},{9,11},{10,... | collective-permute-start | bytes 2408456 | tf_op jit(solution)/shard_map/ppermute | solution.py:31
  367.5 40.1 %copy-start.3 = (bf16[224,1792]{1,0:T(8,128)(2,1)}, bf16[224,1792]{1,0:T(8,128)(2,1)S(1)}, u32[]{:S(2)}) copy-start(bf16[224,1792]{1,0:T(8,128)(2,1)S(1)} %collective-permute-done.21.refs_6_) | copy-start | bytes 2408452
  367.5 22.6 %collective-permute-start.17 = (bf16[224,1792]{1,0:T(8,128)(2,1)}, bf16[224,1792]{1,0:T(8,128)(2,1)}, u32[]{:S(2)}, u32[]{:S(2)}) collective-permute-start(bf16[224,1792]{1,0:T(8,128)(2,1)} %get-tuple-element.91), channel_id=1, source_target_pairs={{0,3},{1,0},{2,1},{3,2},{4,7},{5,4},{6,5},{7,6},{8,11},{9,8},{10,9... | collective-permute-start | bytes 2408456 | tf_op jit(solution)/shard_map/ppermute | solution.py:31
  372.6 33.9 %copy-start.4 = (bf16[224,1792]{1,0:T(8,128)(2,1)}, bf16[224,1792]{1,0:T(8,128)(2,1)S(1)}, u32[]{:S(2)}) copy-start(bf16[224,1792]{1,0:T(8,128)(2,1)S(1)} %collective-permute-done.22.refs_7_) | copy-start | bytes 2408452
  372.6 33.0 %collective-permute-start.9 = (bf16[224,1792]{1,0:T(8,128)(2,1)}, bf16[224,1792]{1,0:T(8,128)(2,1)}, u32[]{:S(2)}, u32[]{:S(2)}) collective-permute-start(bf16[224,1792]{1,0:T(8,128)(2,1)} %get-tuple-element.81), channel_id=1, source_target_pairs={{0,16},{16,32},{32,48},{48,0},{1,17},{17,33},{33,49},{49,1},{2,18}... | collective-permute-start | bytes 2408456 | tf_op jit(solution)/shard_map/ppermute | solution.py:31
  378.8 39.7 %collective-permute-start.10 = (bf16[224,1792]{1,0:T(8,128)(2,1)}, bf16[224,1792]{1,0:T(8,128)(2,1)}, u32[]{:S(2)}, u32[]{:S(2)}) collective-permute-start(bf16[224,1792]{1,0:T(8,128)(2,1)} %get-tuple-element.82), channel_id=1, source_target_pairs={{0,32},{16,48},{32,0},{48,16},{1,33},{17,49},{33,1},{49,17},{2,34}... | collective-permute-start | bytes 2408456 | tf_op jit(solution)/shard_map/ppermute | solution.py:31
  378.9 39.6 %collective-permute-start.11 = (bf16[224,1792]{1,0:T(8,128)(2,1)}, bf16[224,1792]{1,0:T(8,128)(2,1)}, u32[]{:S(2)}, u32[]{:S(2)}) collective-permute-start(bf16[224,1792]{1,0:T(8,128)(2,1)} %get-tuple-element.83), channel_id=1, source_target_pairs={{0,48},{16,0},{32,16},{48,32},{1,49},{17,1},{33,17},{49,33},{2,50}... | collective-permute-start | bytes 2408456 | tf_op jit(solution)/shard_map/ppermute | solution.py:31
  381.0 37.5 %collective-permute-start.3 = (bf16[224,1792]{1,0:T(8,128)(2,1)}, bf16[224,1792]{1,0:T(8,128)(2,1)}, u32[]{:S(2)}, u32[]{:S(2)}) collective-permute-start(bf16[224,1792]{1,0:T(8,128)(2,1)} %get-tuple-element.73), channel_id=1, source_target_pairs={{0,1},{1,2},{2,3},{3,0},{4,5},{5,6},{6,7},{7,4},{8,9},{9,10},{10,1... | collective-permute-start | bytes 2408456 | tf_op jit(solution)/shard_map/ppermute | solution.py:31
  390.1 28.4 %collective-permute-start.4 = (bf16[224,1792]{1,0:T(8,128)(2,1)}, bf16[224,1792]{1,0:T(8,128)(2,1)}, u32[]{:S(2)}, u32[]{:S(2)}) collective-permute-start(bf16[224,1792]{1,0:T(8,128)(2,1)} %get-tuple-element.74), channel_id=1, source_target_pairs={{0,2},{1,3},{2,0},{3,1},{4,6},{5,7},{6,4},{7,5},{8,10},{9,11},{10,... | collective-permute-start | bytes 2408456 | tf_op jit(solution)/shard_map/ppermute | solution.py:31
  405.6 23.3 %collective-permute-start.5 = (bf16[224,1792]{1,0:T(8,128)(2,1)}, bf16[224,1792]{1,0:T(8,128)(2,1)}, u32[]{:S(2)}, u32[]{:S(2)}) collective-permute-start(bf16[224,1792]{1,0:T(8,128)(2,1)} %get-tuple-element.75), channel_id=1, source_target_pairs={{0,3},{1,0},{2,1},{3,2},{4,7},{5,4},{6,5},{7,6},{8,11},{9,8},{10,9... | collective-permute-start | bytes 2408456 | tf_op jit(solution)/shard_map/ppermute | solution.py:31
  428.8 8.4 %copy-start.1 = (bf16[1,1,64,14,1024]{4,2,3,1,0:T(8,128)(2,1)S(1)}, bf16[1,1,64,14,1024]{4,2,3,1,0:T(8,128)(2,1)}, u32[]{:S(2)}) copy-start(bf16[1,1,64,14,1024]{4,2,3,1,0:T(8,128)(2,1)} %param.7) | copy-start | bytes 5505028
  (5 other events, 14.5 us)
Sparse Core Ops, SparseCore 0:
  14.7 56.0 all-gather.5
  73.2 88.2 all-gather.3
  244.0 87.2 reduce-scatter.1

commit v7 on v6

--- a/solution.py
+++ b/solution.py
@@ -129,6 +129,33 @@
         scratch_shapes=[pltpu.VMEM((len(blocks), shape[0], total), gathered.dtype)],
         name="picked",
     )(keys, gathered)
+
+
+def row_kernel(at, rows, weight, out):
+    found = lax.dot_general(
+        rows[...], weight[...], (((1,), (1,)), ((), ())), preferred_element_type=jnp.float32
+    )
+    out[...] = found.astype(out.dtype)
+
+
+def row_grad(at, rows, weight, block):
+    width, half = weight.shape
+    count = rows.shape[0] * rows.shape[1] // (2 * half)
+    tile = 512 if width % 512 == 0 else width
+    return pl.pallas_call(
+        row_kernel,
+        out_shape=jax.ShapeDtypeStruct((count, width), rows.dtype),
+        grid_spec=pltpu.PrefetchScalarGridSpec(
+            num_scalar_prefetch=1,
+            grid=(width // tile,),
+            in_specs=[
+                pl.BlockSpec((count, half), block),
+                pl.BlockSpec((tile, half), lambda i, at: (i, 0)),
+            ],
+            out_specs=pl.BlockSpec((count, tile), lambda i, at: (0, i)),
+        ),
+        name="row_grad",
+    )(at, rows, weight)
 
 
 def sum_kernel(slots, at, keys, rows, *refs):
@@ -249,7 +276,6 @@
     taken = at_slot * sources + (at_x * n_lo + at_lo) * n_y + at_y
     by_place = (taken[:, None] == place[None, :]).astype(bf16)
     grad = lax.optimization_barrier(dot(by_place, grad, ((1,), (0,))).astype(bf16))
-    grad_own = jnp.where(low, grad[:, :half], grad[:, half:])
     grad_send = jnp.where(low, grad[:, half:], grad[:, :half])
     pair = (HI, CORE)
     swapped = lax.all_gather(grad_send, pair, axis=0, axis_index_groups=mirror_pairs(sizes))
@@ -264,21 +290,24 @@
 
     my_hi, my_x = lax.axis_index(HI), lax.axis_index(X)
     my_lo, my_y = lax.axis_index(LO), lax.axis_index(Y)
-    own_out = dot(grad_own, weight, ((1,), (1,))).astype(bf16)
-    own_out, my_hi, my_x, my_lo, my_y = lax.optimization_barrier(
-        (own_out, my_hi, my_x, my_lo, my_y)
+    my_hi = jnp.reshape(my_hi, (1,)).astype(jnp.int32)
+    own_out = row_grad(my_hi, grad, weight, lambda i, at: (0, at[0]))
+    own_out, my_hi, other, my_x, my_lo, my_y = lax.optimization_barrier(
+        (own_out, my_hi, 1 - my_hi, my_x, my_lo, my_y)
     )
     own_back = exchange(own_out)
     own_back, swapped = lax.optimization_barrier((own_back, swapped))
-    grad_mirror = jnp.where(low, swapped[1], swapped[0])
-    mirror_out = dot(grad_mirror, weight, ((1,), (1,))).astype(bf16)
+    swapped = swapped.reshape(n_hi * rows, half)
+    mirror_out = row_grad(other, swapped, weight, lambda i, at: (at[0], 0))
     mirror_back = exchange(mirror_out)
-    own_back, mirror_back, grad_own, grad_mirror, gathered = lax.optimization_barrier(
-        (own_back, mirror_back, grad_own, grad_mirror, gathered)
-    )
-    _, my_hi, my_x, my_lo, my_y, nil = lax.optimization_barrier(
-        (mirror_back, my_hi, my_x, my_lo, my_y, jnp.int32(0))
-    )
+    own_back, mirror_back, grad, swapped, gathered = lax.optimization_barrier(
+        (own_back, mirror_back, grad, swapped, gathered)
+    )
+    _, my_hi, other, my_x, my_lo, my_y, nil = lax.optimization_barrier(
+        (mirror_back, my_hi, other, my_x, my_lo, my_y, jnp.int32(0))
+    )
+    grad_own = jnp.where(low, grad[:, :half], grad[:, half:])
+    grad_mirror = jnp.where(low, swapped[rows:], swapped[:rows])
 
     gathered = gathered.reshape(n_hi * n_lo, count + spare, width)
     position = jnp.stack([my_x, my_lo, my_y]).astype(jnp.int32)
@@ -295,9 +324,8 @@
                 near[part, section][block] = shifted(value, axis, size, block)
             turn += 1
 
-    section = jnp.reshape(my_hi, (1,)).astype(jnp.int32)
-    sums = token_sums(section, keys, own_back, slots, None)
-    sums = token_sums(1 - section, keys, mirror_back, slots, sums)
+    sums = token_sums(my_hi, keys, own_back, slots, None)
+    sums = token_sums(other, keys, mirror_back, slots, sums)
     token_grad = lax.psum_scatter(
         sums, ring_axes, scatter_dimension=0, axis_index_groups=rings, tiled=True
     )

time: 444 us -> 449 us (1.011)
  the two profiles are of different devices: /device:TPU:114 before, /device:TPU:32 now
where the time goes in v7:
time: 449 us; the launch traced here: 440 us
  waiting for transfers between devices  201 us (45%)
  blocking collectives  86 us (19%)
  Pallas kernels  84.3 us (19%)
  starting transfers between devices  38.5 us (9%)
  between operations  14 us (3%)
  matrix products  7.28 us (2%)
  other arithmetic  5.61 us (1%)
    ppermute x24, waiting for transfers between devices, shifted(): lax.ppermute(value, axis, [(i, (i + by) % size) for i in range(size)])  97.4 us
    all_to_all x1, blocking collectives, exchange(): return lax.all_to_all(value, (X, Y), 0, 0, tiled=True).reshape(rows, width)  86 us
    all_to_all x1, waiting for transfers between devices, exchange(): return lax.all_to_all(value, (X, Y), 0, 0, tiled=True).reshape(rows, width)  60.4 us
    all_gather x1, waiting for transfers between devices, on_device(): lax.all_gather(grad_send, pair, axis=0, axis_index_groups=mirror_pairs(si...  43.2 us
    ppermute x24, starting transfers between devices, shifted(): lax.ppermute(value, axis, [(i, (i + by) % size) for i in range(size)])  31.3 us
    pallas_call x2, Pallas kernels, row_grad(): pl.pallas_call(row_kernel, out_shape=jax.ShapeDtypeStruct((count, width),...  18.5 us
    pallas_call x4, Pallas kernels, picked(): pl.pallas_call(functools.partial(pick_kernel, slots, per_out, blocks), ou...  17.7 us
    pallas_call x2, Pallas kernels, hidden_sum(): pl.pallas_call(hidden_sum_kernel, out_shape=jax.ShapeDtypeStruct((parts *...  16.7 us
  transfers between devices with their start and end apart: 28, of which 11 were waited for; matrix products, arithmetic and copies ran while one was open for 1% of the time, Pallas kernels for 15%

profile of v7, /device:TPU:32, one launch (start us, length us, event | category | flops | bytes accessed | tf_op | source)
XLA Modules:
  0.0 440.0 jit_solution(18434317118791824977)
XLA Ops:
  8.7 3.3 fusion.4.rows
  12.0 2.6 slice_select_fusion
  15.7 9.2 %row_grad.2 = bf16[896,3584]{1,0:T(8,128)(2,1)} custom-call(s32[1]{0:T(128)} %bitcast.at, bf16[896,1024]{1,0:T(8,128)(2,1)} %fusion.4.rows, bf16[3584,512]{1,0:T(8,128)(2,1)} %bitcast.37), custom_call_target="tpu_custom_call" | custom-call | tf_op jit(solution)/shard_map/row_grad/pallas_call | solution.py:145
  24.9 7.1 %all-to-all-start = ((bf16[16,56,3584]{2,1,0:T(8,128)(2,1)}), bf16[16,56,3584]{2,1,0:T(8,128)(2,1)}, u32[]{:S(2)}, u32[]{:S(2)}) async-start(bf16[16,56,3584]{2,1,0:T(8,128)(2,1)} %bitcast.33), calls=%async_computation | async-start | bytes 12845056 | tf_op jit(solution)/shard_map/all_to_all | solution.py:289
  32.1 43.2 %all-gather.6.cloned.1.call-done = bf16[1792,512]{1,0:T(8,128)(2,1)} async-done(((bf16[896,512]{1,0:T(8,128)(2,1)}), bf16[1792,512]{1,0:T(8,128)(2,1)}) %all-gather.6.cloned.1.call-update) | async-done | bytes 1835024 | tf_op jit(solution)/shard_map/all_gather | solution.py:281
  75.3 60.4 %all-to-all-done = bf16[16,56,3584]{2,1,0:T(8,128)(2,1)} async-done(((bf16[16,56,3584]{2,1,0:T(8,128)(2,1)}), bf16[16,56,3584]{2,1,0:T(8,128)(2,1)}, u32[]{:S(2)}, u32[]{:S(2)}) %all-to-all-start) | async-done | bytes 6422560 | tf_op jit(solution)/shard_map/all_to_all | solution.py:289
  135.7 9.3 %row_grad.3 = bf16[896,3584]{1,0:T(8,128)(2,1)} custom-call(s32[1]{0:T(128)S(6)} %sub.64.at, bf16[1792,512]{1,0:T(8,128)(2,1)} %all-gather.6.cloned.1.call-done, bf16[3584,512]{1,0:T(8,128)(2,1)} %bitcast.38), custom_call_target="tpu_custom_call" | custom-call | tf_op jit(solution)/shard_map/row_grad/pallas_call | solution.py:145
  145.0 86.0 %all_to_all.10 = bf16[16,56,3584]{2,1,0:T(8,128)(2,1)} all-to-all(bf16[16,56,3584]{2,1,0:T(8,128)(2,1)} %bitcast.34), channel_id=1, replica_groups=mesh['hi'=2,'core'=2,'x'=4,'lo'=4,'y'=4] {'x','y'}, dimensions={0} | all-to-all | bytes 12845056 | tf_op jit(solution)/shard_map/all_to_all | solution.py:289
  233.1 8.3 %token_sums.2.refs_0_ = bf16[1024,3584]{1,0:T(8,128)(2,1)} custom-call(s32[1]{0:T(128)} %bitcast.at, s32[4,16,512]{2,1,0:T(8,128)} %key_table.1.keys, bf16[896,3584]{1,0:T(8,128)(2,1)} %bitcast.6.rows), custom_call_target="tpu_custom_call" | custom-call | tf_op jit(solution)/shard_map/token_sums/pallas_call | solution.py:182
  241.4 8.3 %token_sums.3 = bf16[1024,3584]{1,0:T(8,128)(2,1)} custom-call(s32[1]{0:T(128)S(6)} %sub.64.at, s32[4,16,512]{2,1,0:T(8,128)} %key_table.1.keys, bf16[896,3584]{1,0:T(8,128)(2,1)} %bitcast.32, bf16[1024,3584]{1,0:T(8,128)(2,1)} %token_sums.2.refs_0_), custom_call_target="tpu_custom_call", output_to_operand_aliasing={{}: (3, {})} | custom-call | tf_op jit(solution)/shard_map/token_sums/pallas_call | solution.py:182
  249.8 4.4 %picked.7 = (bf16[224,1792]{1,0:T(8,128)(2,1)}, bf16[224,1792]{1,0:T(8,128)(2,1)}, bf16[224,1792]{1,0:T(8,128)(2,1)}, bf16[224,1792]{1,0:T(8,128)(2,1)}) custom-call(s32[4,16,512]{2,1,0:T(8,128)} %key_table.1.keys, bf16[8,136,3584]{2,1,0:T(8,128)(2,1)} %bitcast.28), custom_call_target="tpu_custom_call" | custom-call | tf_op jit(solution)/shard_map/picked/pallas_call | solution.py:120
  258.4 4.4 %picked.6 = (bf16[224,1792]{1,0:T(8,128)(2,1)}, bf16[224,1792]{1,0:T(8,128)(2,1)}, bf16[224,1792]{1,0:T(8,128)(2,1)}, bf16[224,1792]{1,0:T(8,128)(2,1)}) custom-call(s32[4,16,512]{2,1,0:T(8,128)} %key_table.1.keys, bf16[8,136,3584]{2,1,0:T(8,128)(2,1)} %bitcast.29), custom_call_target="tpu_custom_call" | custom-call | tf_op jit(solution)/shard_map/picked/pallas_call | solution.py:120
  263.2 4.5 %picked.5 = (bf16[224,1792]{1,0:T(8,128)(2,1)}, bf16[224,1792]{1,0:T(8,128)(2,1)}, bf16[224,1792]{1,0:T(8,128)(2,1)}, bf16[224,1792]{1,0:T(8,128)(2,1)}) custom-call(s32[4,16,512]{2,1,0:T(8,128)} %key_table.1.keys, bf16[8,136,3584]{2,1,0:T(8,128)(2,1)} %bitcast.30), custom_call_target="tpu_custom_call" | custom-call | tf_op jit(solution)/shard_map/picked/pallas_call | solution.py:120
  269.8 20.2 %collective-permute-done.18.refs_1_ = bf16[224,1792]{1,0:T(8,128)(2,1)S(1)} collective-permute-done((bf16[224,1792]{1,0:T(8,128)(2,1)}, bf16[224,1792]{1,0:T(8,128)(2,1)S(1)}, u32[]{:S(2)}, u32[]{:S(2)}) %collective-permute-start.18) | collective-permute-done | bytes 802848 | tf_op jit(solution)/shard_map/ppermute | solution.py:31
  296.3 4.4 picked.4
  300.7 3.2 merged.7
  306.4 18.8 %collective-permute-done.6.refs_1_ = bf16[224,1792]{1,0:T(8,128)(2,1)S(1)} collective-permute-done((bf16[224,1792]{1,0:T(8,128)(2,1)}, bf16[224,1792]{1,0:T(8,128)(2,1)S(1)}, u32[]{:S(2)}, u32[]{:S(2)}) %collective-permute-start.6) | collective-permute-done | bytes 802848 | tf_op jit(solution)/shard_map/ppermute | solution.py:31
  327.3 2.3 collective-permute-done.8.refs_3_
  331.1 3.3 merged.6
  334.4 3.2 merged.5
  337.6 3.5 collective-permute-done.refs_1_
  342.7 3.1 collective-permute-start.15
  345.8 11.8 %collective-permute-done.2.refs_3_ = bf16[224,1792]{1,0:T(8,128)(2,1)} collective-permute-done((bf16[224,1792]{1,0:T(8,128)(2,1)}, bf16[224,1792]{1,0:T(8,128)(2,1)}, u32[]{:S(2)}, u32[]{:S(2)}) %collective-permute-start.2) | collective-permute-done | bytes 802848 | tf_op jit(solution)/shard_map/ppermute | solution.py:31
  357.6 4.1 collective-permute-start.16
  362.3 13.9 %collective-permute-done.22.refs_7_ = bf16[224,1792]{1,0:T(8,128)(2,1)S(1)} collective-permute-done((bf16[224,1792]{1,0:T(8,128)(2,1)}, bf16[224,1792]{1,0:T(8,128)(2,1)S(1)}, u32[]{:S(2)}, u32[]{:S(2)}) %collective-permute-start.22) | collective-permute-done | bytes 802848 | tf_op jit(solution)/shard_map/ppermute | solution.py:31
  376.3 3.5 merged.4
  379.9 3.1 collective-permute-start.11
  383.5 2.8 collective-permute-done.17.refs_4_
  388.1 22.6 %collective-permute-done.9.refs_6_ = bf16[224,1792]{1,0:T(8,128)(2,1)} collective-permute-done((bf16[224,1792]{1,0:T(8,128)(2,1)}, bf16[224,1792]{1,0:T(8,128)(2,1)}, u32[]{:S(2)}, u32[]{:S(2)}) %collective-permute-start.9) | collective-permute-done | bytes 802848 | tf_op jit(solution)/shard_map/ppermute | solution.py:31
  411.3 2.8 fusion.9
  416.7 8.3 %hidden_sum.2.refs_9_ = bf16[3584,512]{1,0:T(8,128)(2,1)} custom-call(bf16[8,224,512]{2,1,0:T(8,128)(2,1)} %bitcast.35, bf16[224,1792]{1,0:T(8,128)(2,1)} %get-tuple-element.92.refs_1_, bf16[224,1792]{1,0:T(8,128)(2,1)} %collective-permute-done.15.refs_2_, bf16[224,1792]{1,0:T(8,128)(2,1)} %collective-permute-done.16.refs_3_, ...), custom_call_target="tpu_custom_call" | custom-call | tf_op jit(solution)/shard_map/hidden_sum/pallas_call | solution.py:55
  425.1 8.4 %hidden_sum.3 = bf16[3584,512]{1,0:T(8,128)(2,1)} custom-call(bf16[8,224,512]{2,1,0:T(8,128)(2,1)} %bitcast.36, bf16[224,1792]{1,0:T(8,128)(2,1)} %get-tuple-element.76.refs_1_, bf16[224,1792]{1,0:T(8,128)(2,1)} %collective-permute-done.3.refs_2_, bf16[224,1792]{1,0:T(8,128)(2,1)} %collective-permute-done.4.refs_3_, ...), custom_call_target="tpu_custom_call", output_to_operand_aliasing={{}: (9, {})} | custom-call | tf_op jit(solution)/shard_map/hidden_sum/pallas_call | solution.py:55
  (81 shorter events, 32.0 us)
Async XLA Ops:
  7.2 68.1 %all-gather.6.cloned.1.call-start = ((), (), s32[]{:S(2)}) async-start(), calls=%async_computation.5 | async-start | bytes 2752512 | tf_op jit(solution)/shard_map/all_gather | solution.py:281
  14.6 216.4 %all-gather.4.cloned.1.call-start = ((), (), s32[]{:S(2)}) async-start(), calls=%async_computation.3 | async-start | bytes 8773632 | tf_op jit(solution)/shard_map/all_gather | solution.py:285
  24.9 110.8 %all-to-all-start = ((bf16[16,56,3584]{2,1,0:T(8,128)(2,1)}), bf16[16,56,3584]{2,1,0:T(8,128)(2,1)}, u32[]{:S(2)}, u32[]{:S(2)}) async-start(bf16[16,56,3584]{2,1,0:T(8,128)(2,1)} %bitcast.33), calls=%async_computation | async-start | bytes 12845056 | tf_op jit(solution)/shard_map/all_to_all | solution.py:289
  32.0 401.4 %reduce-scatter.2.cloned.1.call-start = ((), (), s32[]{:S(2)}) async-start(), calls=%async_computation.4 | async-start | bytes 8257536 | tf_op jit(solution)/shard_map/reduce_scatter | solution.py:329
  254.2 35.8 %collective-permute-start.18 = (bf16[224,1792]{1,0:T(8,128)(2,1)}, bf16[224,1792]{1,0:T(8,128)(2,1)S(1)}, u32[]{:S(2)}, u32[]{:S(2)}) collective-permute-start(bf16[224,1792]{1,0:T(8,128)(2,1)} %get-tuple-element.97), channel_id=1, source_target_pairs={{0,1},{1,2},{2,3},{3,0},{4,5},{5,6},{6,7},{7,4},{8,9},{9,10},{10,1... | collective-permute-start | bytes 2408456 | tf_op jit(solution)/shard_map/ppermute | solution.py:31
  254.7 37.4 %collective-permute-start.19 = (bf16[224,1792]{1,0:T(8,128)(2,1)}, bf16[224,1792]{1,0:T(8,128)(2,1)S(1)}, u32[]{:S(2)}, u32[]{:S(2)}) collective-permute-start(bf16[224,1792]{1,0:T(8,128)(2,1)} %get-tuple-element.98), channel_id=1, source_target_pairs={{0,2},{1,3},{2,0},{3,1},{4,6},{5,7},{6,4},{7,5},{8,10},{9,11},{10,... | collective-permute-start | bytes 2408456 | tf_op jit(solution)/shard_map/ppermute | solution.py:31
  256.9 36.0 %collective-permute-start.20 = (bf16[224,1792]{1,0:T(8,128)(2,1)}, bf16[224,1792]{1,0:T(8,128)(2,1)}, u32[]{:S(2)}, u32[]{:S(2)}) collective-permute-start(bf16[224,1792]{1,0:T(8,128)(2,1)} %get-tuple-element.99), channel_id=1, source_target_pairs={{0,3},{1,0},{2,1},{3,2},{4,7},{5,4},{6,5},{7,6},{8,11},{9,8},{10,9... | collective-permute-start | bytes 2408456 | tf_op jit(solution)/shard_map/ppermute | solution.py:31
  262.8 31.4 %collective-permute-start.12 = (bf16[224,1792]{1,0:T(8,128)(2,1)}, bf16[224,1792]{1,0:T(8,128)(2,1)S(1)}, u32[]{:S(2)}, u32[]{:S(2)}) collective-permute-start(bf16[224,1792]{1,0:T(8,128)(2,1)} %get-tuple-element.89), channel_id=1, source_target_pairs={{0,16},{16,32},{32,48},{48,0},{1,17},{17,33},{33,49},{49,1},{2,18}... | collective-permute-start | bytes 2408456 | tf_op jit(solution)/shard_map/ppermute | solution.py:31
  267.7 36.2 %collective-permute-start.13 = (bf16[224,1792]{1,0:T(8,128)(2,1)}, bf16[224,1792]{1,0:T(8,128)(2,1)S(1)}, u32[]{:S(2)}, u32[]{:S(2)}) collective-permute-start(bf16[224,1792]{1,0:T(8,128)(2,1)} %get-tuple-element.90), channel_id=1, source_target_pairs={{0,32},{16,48},{32,0},{48,16},{1,33},{17,49},{33,1},{49,17},{2,34}... | collective-permute-start | bytes 2408456 | tf_op jit(solution)/shard_map/ppermute | solution.py:31
  290.9 13.9 %collective-permute-start.14 = (bf16[224,1792]{1,0:T(8,128)(2,1)}, bf16[224,1792]{1,0:T(8,128)(2,1)S(1)}, u32[]{:S(2)}, u32[]{:S(2)}) collective-permute-start(bf16[224,1792]{1,0:T(8,128)(2,1)} %get-tuple-element.91), channel_id=1, source_target_pairs={{0,48},{16,0},{32,16},{48,32},{1,49},{17,1},{33,17},{49,33},{2,50}... | collective-permute-start | bytes 2408456 | tf_op jit(solution)/shard_map/ppermute | solution.py:31
  293.0 32.3 %collective-permute-start.6 = (bf16[224,1792]{1,0:T(8,128)(2,1)}, bf16[224,1792]{1,0:T(8,128)(2,1)S(1)}, u32[]{:S(2)}, u32[]{:S(2)}) collective-permute-start(bf16[224,1792]{1,0:T(8,128)(2,1)} %get-tuple-element.81), channel_id=1, source_target_pairs={{0,1},{1,2},{2,3},{3,0},{4,5},{5,6},{6,7},{7,4},{8,9},{9,10},{10,1... | collective-permute-start | bytes 2408456 | tf_op jit(solution)/shard_map/ppermute | solution.py:31
  293.0 33.5 %collective-permute-start.7 = (bf16[224,1792]{1,0:T(8,128)(2,1)}, bf16[224,1792]{1,0:T(8,128)(2,1)}, u32[]{:S(2)}, u32[]{:S(2)}) collective-permute-start(bf16[224,1792]{1,0:T(8,128)(2,1)} %get-tuple-element.82), channel_id=1, source_target_pairs={{0,2},{1,3},{2,0},{3,1},{4,6},{5,7},{6,4},{7,5},{8,10},{9,11},{10,... | collective-permute-start | bytes 2408456 | tf_op jit(solution)/shard_map/ppermute | solution.py:31
  294.1 35.4 %collective-permute-start.8 = (bf16[224,1792]{1,0:T(8,128)(2,1)}, bf16[224,1792]{1,0:T(8,128)(2,1)}, u32[]{:S(2)}, u32[]{:S(2)}) collective-permute-start(bf16[224,1792]{1,0:T(8,128)(2,1)} %get-tuple-element.83), channel_id=1, source_target_pairs={{0,3},{1,0},{2,1},{3,2},{4,7},{5,4},{6,5},{7,6},{8,11},{9,8},{10,9... | collective-permute-start | bytes 2408456 | tf_op jit(solution)/shard_map/ppermute | solution.py:31
  303.9 27.2 %copy-start.8 = (bf16[224,1792]{1,0:T(8,128)(2,1)}, bf16[224,1792]{1,0:T(8,128)(2,1)S(1)}, u32[]{:S(2)}) copy-start(bf16[224,1792]{1,0:T(8,128)(2,1)S(1)} %collective-permute-done.13.refs_2_) | copy-start | bytes 2408452
  303.9 37.2 %collective-permute-start = (bf16[224,1792]{1,0:T(8,128)(2,1)}, bf16[224,1792]{1,0:T(8,128)(2,1)}, u32[]{:S(2)}, u32[]{:S(2)}) collective-permute-start(bf16[224,1792]{1,0:T(8,128)(2,1)} %get-tuple-element.73), channel_id=1, source_target_pairs={{0,16},{16,32},{32,48},{48,0},{1,17},{17,33},{33,49},{49,1},{2,18}... | collective-permute-start | bytes 2408456 | tf_op jit(solution)/shard_map/ppermute | solution.py:31
  304.8 38.0 %collective-permute-start.1 = (bf16[224,1792]{1,0:T(8,128)(2,1)}, bf16[224,1792]{1,0:T(8,128)(2,1)}, u32[]{:S(2)}, u32[]{:S(2)}) collective-permute-start(bf16[224,1792]{1,0:T(8,128)(2,1)} %get-tuple-element.74), channel_id=1, source_target_pairs={{0,32},{16,48},{32,0},{48,16},{1,33},{17,49},{33,1},{49,17},{2,34}... | collective-permute-start | bytes 2408456 | tf_op jit(solution)/shard_map/ppermute | solution.py:31
  325.3 32.3 %collective-permute-start.2 = (bf16[224,1792]{1,0:T(8,128)(2,1)}, bf16[224,1792]{1,0:T(8,128)(2,1)}, u32[]{:S(2)}, u32[]{:S(2)}) collective-permute-start(bf16[224,1792]{1,0:T(8,128)(2,1)} %get-tuple-element.75), channel_id=1, source_target_pairs={{0,48},{16,0},{32,16},{48,32},{1,49},{17,1},{33,17},{49,33},{2,50}... | collective-permute-start | bytes 2408456 | tf_op jit(solution)/shard_map/ppermute | solution.py:31
  326.5 35.2 %collective-permute-start.21 = (bf16[224,1792]{1,0:T(8,128)(2,1)}, bf16[224,1792]{1,0:T(8,128)(2,1)S(1)}, u32[]{:S(2)}, u32[]{:S(2)}) collective-permute-start(bf16[224,1792]{1,0:T(8,128)(2,1)} %get-tuple-element.101), channel_id=1, source_target_pairs={{0,16},{16,32},{32,48},{48,0},{1,17},{17,33},{33,49},{49,1},{2,18}... | collective-permute-start | bytes 2408456 | tf_op jit(solution)/shard_map/ppermute | solution.py:31
  329.5 46.7 %collective-permute-start.22 = (bf16[224,1792]{1,0:T(8,128)(2,1)}, bf16[224,1792]{1,0:T(8,128)(2,1)S(1)}, u32[]{:S(2)}, u32[]{:S(2)}) collective-permute-start(bf16[224,1792]{1,0:T(8,128)(2,1)} %get-tuple-element.102), channel_id=1, source_target_pairs={{0,32},{16,48},{32,0},{48,16},{1,33},{17,49},{33,1},{49,17},{2,34}... | collective-permute-start | bytes 2408456 | tf_op jit(solution)/shard_map/ppermute | solution.py:31
  337.6 73.7 %copy-start.2 = (bf16[896,1024]{1,0:T(8,128)(2,1)S(1)}, bf16[896,1024]{1,0:T(8,128)(2,1)}, u32[]{:S(2)}) copy-start(bf16[896,1024]{1,0:T(8,128)(2,1)} %fusion.4.rows) | copy-start | bytes 5505028
  341.1 38.7 %collective-permute-start.23 = (bf16[224,1792]{1,0:T(8,128)(2,1)}, bf16[224,1792]{1,0:T(8,128)(2,1)}, u32[]{:S(2)}, u32[]{:S(2)}) collective-permute-start(bf16[224,1792]{1,0:T(8,128)(2,1)} %get-tuple-element.103), channel_id=1, source_target_pairs={{0,48},{16,0},{32,16},{48,32},{1,49},{17,1},{33,17},{49,33},{2,50}... | collective-permute-start | bytes 2408456 | tf_op jit(solution)/shard_map/ppermute | solution.py:31
  342.7 37.2 %collective-permute-start.15 = (bf16[224,1792]{1,0:T(8,128)(2,1)}, bf16[224,1792]{1,0:T(8,128)(2,1)}, u32[]{:S(2)}, u32[]{:S(2)}) collective-permute-start(bf16[224,1792]{1,0:T(8,128)(2,1)} %get-tuple-element.93), channel_id=1, source_target_pairs={{0,1},{1,2},{2,3},{3,0},{4,5},{5,6},{6,7},{7,4},{8,9},{9,10},{10,1... | collective-permute-start | bytes 2408456 | tf_op jit(solution)/shard_map/ppermute | solution.py:31
  357.6 25.4 %collective-permute-start.16 = (bf16[224,1792]{1,0:T(8,128)(2,1)}, bf16[224,1792]{1,0:T(8,128)(2,1)}, u32[]{:S(2)}, u32[]{:S(2)}) collective-permute-start(bf16[224,1792]{1,0:T(8,128)(2,1)} %get-tuple-element.94), channel_id=1, source_target_pairs={{0,2},{1,3},{2,0},{3,1},{4,6},{5,7},{6,4},{7,5},{8,10},{9,11},{10,... | collective-permute-start | bytes 2408456 | tf_op jit(solution)/shard_map/ppermute | solution.py:31
  361.7 52.4 %copy-start.5 = (bf16[224,1792]{1,0:T(8,128)(2,1)}, bf16[224,1792]{1,0:T(8,128)(2,1)S(1)}, u32[]{:S(2)}) copy-start(bf16[224,1792]{1,0:T(8,128)(2,1)S(1)} %collective-permute-done.21.refs_6_) | copy-start | bytes 2408452
  361.7 24.5 %collective-permute-start.17 = (bf16[224,1792]{1,0:T(8,128)(2,1)}, bf16[224,1792]{1,0:T(8,128)(2,1)}, u32[]{:S(2)}, u32[]{:S(2)}) collective-permute-start(bf16[224,1792]{1,0:T(8,128)(2,1)} %get-tuple-element.95), channel_id=1, source_target_pairs={{0,3},{1,0},{2,1},{3,2},{4,7},{5,4},{6,5},{7,6},{8,11},{9,8},{10,9... | collective-permute-start | bytes 2408456 | tf_op jit(solution)/shard_map/ppermute | solution.py:31
  376.2 37.9 %copy-start.6 = (bf16[224,1792]{1,0:T(8,128)(2,1)}, bf16[224,1792]{1,0:T(8,128)(2,1)S(1)}, u32[]{:S(2)}) copy-start(bf16[224,1792]{1,0:T(8,128)(2,1)S(1)} %collective-permute-done.22.refs_7_) | copy-start | bytes 2408452
  376.2 34.5 %collective-permute-start.9 = (bf16[224,1792]{1,0:T(8,128)(2,1)}, bf16[224,1792]{1,0:T(8,128)(2,1)}, u32[]{:S(2)}, u32[]{:S(2)}) collective-permute-start(bf16[224,1792]{1,0:T(8,128)(2,1)} %get-tuple-element.85), channel_id=1, source_target_pairs={{0,16},{16,32},{32,48},{48,0},{1,17},{17,33},{33,49},{49,1},{2,18}... | collective-permute-start | bytes 2408456 | tf_op jit(solution)/shard_map/ppermute | solution.py:31
  379.8 45.2 %collective-permute-start.10 = (bf16[224,1792]{1,0:T(8,128)(2,1)}, bf16[224,1792]{1,0:T(8,128)(2,1)}, u32[]{:S(2)}, u32[]{:S(2)}) collective-permute-start(bf16[224,1792]{1,0:T(8,128)(2,1)} %get-tuple-element.86), channel_id=1, source_target_pairs={{0,32},{16,48},{32,0},{48,16},{1,33},{17,49},{33,1},{49,17},{2,34}... | collective-permute-start | bytes 2408456 | tf_op jit(solution)/shard_map/ppermute | solution.py:31
  379.9 45.1 %collective-permute-start.11 = (bf16[224,1792]{1,0:T(8,128)(2,1)}, bf16[224,1792]{1,0:T(8,128)(2,1)}, u32[]{:S(2)}, u32[]{:S(2)}) collective-permute-start(bf16[224,1792]{1,0:T(8,128)(2,1)} %get-tuple-element.87), channel_id=1, source_target_pairs={{0,48},{16,0},{32,16},{48,32},{1,49},{17,1},{33,17},{49,33},{2,50}... | collective-permute-start | bytes 2408456 | tf_op jit(solution)/shard_map/ppermute | solution.py:31
  383.0 42.0 %collective-permute-start.3 = (bf16[224,1792]{1,0:T(8,128)(2,1)}, bf16[224,1792]{1,0:T(8,128)(2,1)}, u32[]{:S(2)}, u32[]{:S(2)}) collective-permute-start(bf16[224,1792]{1,0:T(8,128)(2,1)} %get-tuple-element.77), channel_id=1, source_target_pairs={{0,1},{1,2},{2,3},{3,0},{4,5},{5,6},{6,7},{7,4},{8,9},{9,10},{10,1... | collective-permute-start | bytes 2408456 | tf_op jit(solution)/shard_map/ppermute | solution.py:31
  386.2 38.8 %collective-permute-start.4 = (bf16[224,1792]{1,0:T(8,128)(2,1)}, bf16[224,1792]{1,0:T(8,128)(2,1)}, u32[]{:S(2)}, u32[]{:S(2)}) collective-permute-start(bf16[224,1792]{1,0:T(8,128)(2,1)} %get-tuple-element.78), channel_id=1, source_target_pairs={{0,2},{1,3},{2,0},{3,1},{4,6},{5,7},{6,4},{7,5},{8,10},{9,11},{10,... | collective-permute-start | bytes 2408456 | tf_op jit(solution)/shard_map/ppermute | solution.py:31
  410.7 14.3 %collective-permute-start.5 = (bf16[224,1792]{1,0:T(8,128)(2,1)}, bf16[224,1792]{1,0:T(8,128)(2,1)}, u32[]{:S(2)}, u32[]{:S(2)}) collective-permute-start(bf16[224,1792]{1,0:T(8,128)(2,1)} %get-tuple-element.79), channel_id=1, source_target_pairs={{0,3},{1,0},{2,1},{3,2},{4,7},{5,4},{6,5},{7,6},{8,11},{9,8},{10,9... | collective-permute-start | bytes 2408456 | tf_op jit(solution)/shard_map/ppermute | solution.py:31
  (10 other events, 52.4 us)
Sparse Core Ops, SparseCore 0:
  14.7 60.5 all-gather.5
  77.1 83.8 all-gather.3
  249.9 83.9 reduce-scatter.1
